TPU v7x, 32 devices: a whole 2x2x4 slice. The times are simulated.
32 devices in a mesh: row: 8 (over z, core), col: 4 (over y, x).
Axes of the slice: x: 2, y: 2, z: 4, core: 2. Of those that a mesh axis runs over, the one named last changes fastest.
Arguments:
- rhs: bfloat16 [3, 8, 64, 256], P(None, 'row'), may hold values from -6 to 6
- dinv: bfloat16 [3, 8, 256, 256], P(None, 'row'), as said below
- tiles: bfloat16 [2, 8, 8, 256, 256], P(None, 'row', 'col'), may hold values from -0.09375 to 0.09375
- pattern: int32 [2, 2, 8, 8], P(None, None, 'row', 'col'), may hold values from 0 to 7, as said below
Outputs:
- solution: float32 [3, 8, 64, 256], P(None, 'row')
Inputs may be any that keep to these rules, and one draw needn't show every extreme that they name: pattern[0, l, p, t] = p; pattern[1, l, p, t] = j has (j) modulo the size of col equal to t // 2; positions may repeat, and repeated tiles add. `dinv`: lower triangular with a positive diagonal.
All inputs are finite; a program needn't handle non-finite values.
Results may differ from a plain program's by a relative error of at most 0.0055.
Values may be sent and summed in bfloat16 or wider, within the bound.
No kernel may reach another device: no remote copies, remote signals or barrier semaphores. Data moves between devices by JAX's collectives and lax.ppermute only.
A program may use at most 64 MiB of HBM per device.

v0:
```python
import jax
import jax.numpy as jnp
from jax import lax
from jax.sharding import PartitionSpec as P


def broadcast(block, axis, holder):
    block = jnp.where(lax.axis_index(axis) == holder, block, jnp.zeros_like(block))
    return lax.psum(block, axis)


def collect(rounded, mine_col, col_count, repeat):
    whole_level = lax.all_gather(rounded, "row", axis=0, tiled=True)
    shaped = whole_level.reshape((repeat, col_count) + rounded.shape)
    picked = lax.dynamic_index_in_dim(shaped, mine_col, 1, keepdims=False)
    return picked.reshape((-1,) + rounded.shape[1:])


def per_device(rhs, dinv, tiles, pattern):
    blocks = rhs.shape[1]
    levels_all = rhs.shape[0]
    col_count = lax.axis_size("col")
    row_count = lax.axis_size("row")
    repeat = row_count // col_count
    mine_row = lax.axis_index("row")
    mine_col = lax.axis_index("col")
    targets = pattern[0, :, 0, :] % blocks
    raw_cols = pattern[1, :, 0, :]
    sources = raw_cols // blocks // col_count * blocks + raw_cols % blocks
    row_pick = (targets[:, None, :] == jnp.arange(blocks, dtype=jnp.int32)[None, :, None]).astype(
        jnp.float32
    )
    col_pick = (
        sources[:, None, :] == jnp.arange(repeat * blocks, dtype=jnp.int32)[None, :, None]
    ).astype(jnp.float32)
    fronts = [rhs]
    forward_all = [[] for front in fronts]
    rounded_all = [None for front in fronts]
    for level_now in range(levels_all):
        front_index = 0
        front_level = fronts[front_index][level_now]
        current = front_level.astype(jnp.float32)
        if level_now > 0:
            nearby = collect(rounded_all[front_index], mine_col, col_count, repeat)
            source = jnp.take(nearby, sources[level_now - 1], axis=0)
            product = jnp.einsum(
                "sjb,sab->sja", source, tiles[level_now - 1, 0], preferred_element_type=jnp.float32
            )
            partial_value = jnp.sum(
                row_pick[level_now - 1][:, :, None, None] * product[None], axis=1
            )
            total_sum = lax.psum(partial_value, "col")
            current = current - total_sum
        solved = jnp.einsum(
            "rjb,rab->rja",
            current.astype(jnp.bfloat16),
            dinv[level_now],
            preferred_element_type=jnp.float32,
        )
        forward_all[front_index].append(solved)
        rounded_all[front_index] = solved.astype(jnp.bfloat16)
    backward_all = [[None] * levels_all for front in fronts]
    following_all = [None for front in fronts]
    for level_now in range(levels_all - 1, -1, -1):
        front_index = 0
        remainder = forward_all[front_index][level_now]
        if level_now < levels_all - 1:
            source = jnp.take(following_all[front_index], targets[level_now], axis=0)
            product = jnp.einsum(
                "sja,sab->sjb", source, tiles[level_now, 0], preferred_element_type=jnp.float32
            )
            partial_value = jnp.sum(col_pick[level_now][:, :, None, None] * product[None], axis=1)
            column_total = lax.psum(partial_value, "row")
            shaped = column_total.reshape((repeat, blocks) + column_total.shape[1:])
            picked = lax.dynamic_index_in_dim(shaped, mine_row // col_count, 0, keepdims=False)
            arrived = broadcast(picked, "col", mine_row % col_count)
            remainder = remainder - arrived
        solved = jnp.einsum(
            "rjb,rba->rja",
            remainder.astype(jnp.bfloat16),
            dinv[level_now],
            preferred_element_type=jnp.float32,
        )
        backward_all[front_index][level_now] = solved
        following_all[front_index] = solved.astype(jnp.bfloat16)
    front_index = 0
    levels_stack = jnp.stack(backward_all[front_index])
    return levels_stack


def solution(mesh):
    in_specs = (
        P(None, "row", None, None),
        P(None, "row", None, None),
        P(None, "row", "col", None, None),
        P(None, None, "row", "col"),
    )
    out_specs = P(None, "row", None, None)
    return jax.shard_map(
        per_device, mesh=mesh, in_specs=in_specs, out_specs=out_specs, check_vma=False
    )
```

profile of v0, /device:TPU:0, one launch (start us, length us, event | category | flops | bytes accessed | tf_op | source)
XLA Modules:
  0.0 337.1 jit_solution(15482950410898514648)
XLA Ops:
  6.5 0.0 copy-start.1
  6.5 0.0 all-reduce.7.cloned.1.call-start
  6.5 1.1 fusion.57
  7.7 0.0 slice-start
  7.7 15.9 %all-gather = bf16[512,256]{1,0:T(8,128)(2,1)S(1)} all-gather(bf16[64,256]{1,0:T(8,128)(2,1)S(1)} %get-tuple-element.15), channel_id=2, replica_groups=mesh['row'=8,'col'=4] {'row'}, dimensions={0}, use_global_device_ids=true | all-gather | bytes 294912 | tf_op jit(solution)/shard_map/all_gather | solution.py:13
  23.6 0.0 copy-start
  23.6 0.0 slice-done
  23.7 0.6 gather_fusion
  24.3 0.0 copy-done.1
  24.3 0.0 copy-start.2
  24.3 0.8 convolution_bitcast_fusion.2
  25.1 0.0 all-reduce.7.cloned.1.call-update
  25.1 0.0 all-reduce.9.cloned.1.call-start
  25.2 43.0 %all-reduce.7.cloned.1.call-done = f32[1,64,256]{2,1,0:T(8,128)} async-done(((f32[1,64,256]{2,1,0:T(8,128)}), f32[1,64,256]{2,1,0:T(8,128)}) %all-reduce.7.cloned.1.call-update) | async-done | bytes 65552 | tf_op jit(solution)/shard_map/psum | solution.py:52
  68.2 0.0 copy-done
  68.2 0.0 copy-done.2
  68.2 1.0 fusion.58
  69.2 14.3 %all-gather.1 = bf16[512,256]{1,0:T(8,128)(2,1)S(1)} all-gather(bf16[64,256]{1,0:T(8,128)(2,1)S(1)} %get-tuple-element.17), channel_id=3, replica_groups=mesh['row'=8,'col'=4] {'row'}, dimensions={0}, use_global_device_ids=true | all-gather | bytes 294912 | tf_op jit(solution)/shard_map/all_gather | solution.py:13
  83.5 0.5 gather_fusion.1
  84.0 0.8 convolution_bitcast_fusion.1
  84.9 0.0 all-reduce.9.cloned.1.call-update
  84.9 0.0 all-reduce.11.cloned.1.call-start
  84.9 41.9 %all-reduce.9.cloned.1.call-done = f32[1,64,256]{2,1,0:T(8,128)} async-done(((f32[1,64,256]{2,1,0:T(8,128)}), f32[1,64,256]{2,1,0:T(8,128)}) %all-reduce.9.cloned.1.call-update) | async-done | bytes 65552 | tf_op jit(solution)/shard_map/psum | solution.py:52
  126.9 1.1 fusion.59
  128.0 0.2 fusion.1
  128.2 0.8 multiply_reduce_fusion.1
  128.9 0.0 all-reduce.11.cloned.1.call-update
  128.9 0.0 all-reduce.13.cloned.1.call-start
  129.0 55.1 %all-reduce.11.cloned.1.call-done = f32[2,64,256]{2,1,0:T(8,128)} async-done(((f32[2,64,256]{2,1,0:T(8,128)}), f32[2,64,256]{2,1,0:T(8,128)}) %all-reduce.11.cloned.1.call-update) | async-done | bytes 131088 | tf_op jit(solution)/shard_map/psum | solution.py:73
  184.1 1.5 dynamic-slice_select_fusion.1
  185.6 0.0 all-reduce.13.cloned.1.call-update
  185.6 0.0 all-reduce.15.cloned.1.call-start
  185.7 42.1 %all-reduce.13.cloned.1.call-done = f32[1,64,256]{2,1,0:T(8,128)} async-done(((f32[1,64,256]{2,1,0:T(8,128)}), f32[1,64,256]{2,1,0:T(8,128)}) %all-reduce.13.cloned.1.call-update) | async-done | bytes 65552 | tf_op jit(solution)/shard_map/psum | solution.py:9
  227.8 1.0 fusion.64
  228.8 0.2 fusion.4
  228.9 0.7 multiply_reduce_fusion
  229.7 0.0 all-reduce.15.cloned.1.call-update
  229.7 0.0 all-reduce.17.cloned.1.call-start
  229.8 55.1 %all-reduce.15.cloned.1.call-done = f32[2,64,256]{2,1,0:T(8,128)} async-done(((f32[2,64,256]{2,1,0:T(8,128)}), f32[2,64,256]{2,1,0:T(8,128)}) %all-reduce.15.cloned.1.call-update) | async-done | bytes 131088 | tf_op jit(solution)/shard_map/psum | solution.py:73
  284.9 1.5 dynamic-slice_select_fusion
  286.4 0.0 all-reduce.17.cloned.1.call-update
  286.4 42.2 %all-reduce.17.cloned.1.call-done = f32[1,64,256]{2,1,0:T(8,128)} async-done(((f32[1,64,256]{2,1,0:T(8,128)}), f32[1,64,256]{2,1,0:T(8,128)}) %all-reduce.17.cloned.1.call-update) | async-done | bytes 65552 | tf_op jit(solution)/shard_map/psum | solution.py:9
  328.5 1.0 convolution_bitcast_fusion
  329.5 0.7 pad_maximum_fusion
  (8 shorter events, 0.1 us)
Async XLA Ops:
  6.5 17.7 %copy-start.1 = (bf16[2,1,2,256,256]{4,3,2,1,0:T(8,128)(2,1)S(1)}, bf16[2,1,2,256,256]{4,3,2,1,0:T(8,128)(2,1)}, u32[]{:S(2)}) copy-start(bf16[2,1,2,256,256]{4,3,2,1,0:T(8,128)(2,1)} %param.10) | copy-start | bytes 1572868
  6.5 61.6 %all-reduce.7.cloned.1.call-start = ((), (), s32[]{:S(2)}) async-start(), calls=%async_computation | async-start | bytes 131072 | tf_op jit(solution)/shard_map/psum | solution.py:52
  7.7 16.0 %slice-start = ((s32[2,2,1,2]{3,2,1,0:T(1,128)}), s32[1,2,1,2]{3,2,1,0:T(1,128)S(1)}, s32[]{:S(2)}) async-start(s32[2,2,1,2]{3,2,1,0:T(1,128)} %param.11), calls=%async_computation.6 | async-start | bytes 2048 | tf_op jit(solution)/shard_map/slice | solution.py:28
  23.6 44.5 %copy-start = (bf16[3,1,256,256]{3,2,1,0:T(8,128)(2,1)S(1)}, bf16[3,1,256,256]{3,2,1,0:T(8,128)(2,1)}, u32[]{:S(2)}) copy-start(bf16[3,1,256,256]{3,2,1,0:T(8,128)(2,1)} %param.9) | copy-start | bytes 1179652
  24.3 43.9 %copy-start.2 = (bf16[3,1,64,256]{3,2,1,0:T(8,128)(2,1)S(1)}, bf16[3,1,64,256]{3,2,1,0:T(8,128)(2,1)}, u32[]{:S(2)}) copy-start(bf16[3,1,64,256]{3,2,1,0:T(8,128)(2,1)} %param.8) | copy-start | bytes 294916
  25.1 101.7 %all-reduce.9.cloned.1.call-start = ((), (), s32[]{:S(2)}) async-start(), calls=%async_computation.1 | async-start | bytes 131072 | tf_op jit(solution)/shard_map/psum | solution.py:52
  84.9 99.2 %all-reduce.11.cloned.1.call-start = ((), (), s32[]{:S(2)}) async-start(), calls=%async_computation.2 | async-start | bytes 262144 | tf_op jit(solution)/shard_map/psum | solution.py:73
  128.9 98.8 %all-reduce.13.cloned.1.call-start = ((), (), s32[]{:S(2)}) async-start(), calls=%async_computation.3 | async-start | bytes 131072 | tf_op jit(solution)/shard_map/psum | solution.py:9
  185.6 99.3 %all-reduce.15.cloned.1.call-start = ((), (), s32[]{:S(2)}) async-start(), calls=%async_computation.4 | async-start | bytes 262144 | tf_op jit(solution)/shard_map/psum | solution.py:73
  229.7 98.8 %all-reduce.17.cloned.1.call-start = ((), (), s32[]{:S(2)}) async-start(), calls=%async_computation.5 | async-start | bytes 131072 | tf_op jit(solution)/shard_map/psum | solution.py:9
Sparse Core Ops, SparseCore 0:
  25.3 42.8 all-reduce.6
  85.0 41.7 all-reduce.8
  129.2 54.9 all-reduce.10
  186.8 40.8 all-reduce.12
  229.9 54.9 all-reduce.14
  287.6 40.8 all-reduce.16
where the time goes:
time: 337 us
  waiting for transfers between devices  279 us (83%)
  blocking collectives  30.2 us (9%)
  between operations  13.6 us (4%)
  matrix products  7.25 us (2%)
  other arithmetic  5.19 us (2%)
    psum x2, waiting for transfers between devices, per_device(): column_total = lax.psum(partial_value, 'row')  110 us
    psum x2, waiting for transfers between devices, per_device(): total_sum = lax.psum(partial_value, 'col')  84.9 us
    psum x2, waiting for transfers between devices, broadcast(): return lax.psum(block, axis)  84.3 us
    all_gather x2, blocking collectives, collect(): whole_level = lax.all_gather(rounded, 'row', axis=0, tiled=True)  30.2 us
  transfers between devices with their start and end apart: 6, of which 6 were waited for; matrix products, arithmetic and copies ran while one was open for 0% of the time, Pallas kernels for 0%

commit v1 on v0

v1 whole, which is shorter than its diff:
```python
import functools

import jax
import jax.numpy as jnp
from jax import lax
from jax.experimental import pallas as pl
from jax.experimental.pallas import tpu as pltpu
from jax.sharding import PartitionSpec as P

F32 = jnp.float32
BF16 = jnp.bfloat16


def swap(value, axis, size, mask):
    return lax.ppermute(value, axis, [(i, i ^ mask) for i in range(size)])


def dot_t(a, b):
    return lax.dot_general(a, b, (((1,), (1,)), ((), ())), preferred_element_type=F32)


def dot_n(a, b):
    return lax.dot_general(a, b, (((1,), (0,)), ((), ())), preferred_element_type=F32)


def update(near, far, tile_refs, repeat):
    cols = len(tile_refs)
    row = lax.axis_index("row")
    col = lax.axis_index("col")
    total = None
    for step, tile_ref in enumerate(tile_refs):
        for group in range(repeat):
            place = row ^ ((col ^ step) + cols * group)
            offset = place // 2
            odd = jnp.broadcast_to(place % 2, near.shape[1:]) == 1
            segment = jnp.where(odd, far[offset], near[offset])
            term = dot_t(segment, tile_ref[group])
            total = term if total is None else total + term
    return total


def spread(solved, tile_refs, repeat, parts, keep_ref, send_ref):
    cols = len(tile_refs)
    row = lax.axis_index("row")
    col = lax.axis_index("col")
    for step, tile_ref in enumerate(tile_refs):
        for group in range(repeat):
            place = row ^ ((col ^ step) + cols * group)
            parts[place % 2, place // 2] = dot_n(solved, tile_ref[group])
    keep_ref[...] = parts[0]
    send_ref[...] = parts[1].astype(BF16)


def first_kernel(rhs, dinv, out, out_b):
    solved = dot_t(rhs[...], dinv[...])
    out[...] = solved
    out_b[...] = solved.astype(BF16)


def forward_kernel(repeat, cols, near, far, *refs):
    tile_refs, (rhs, dinv, out, out_b) = refs[:cols], refs[cols:]
    current = rhs[...].astype(F32) - update(near, far, tile_refs, repeat)
    solved = dot_t(current.astype(BF16), dinv[...])
    out[...] = solved
    out_b[...] = solved.astype(BF16)


def turn_kernel(repeat, cols, near, far, *refs):
    tile_refs, (rhs, dinv, out, keep, send, parts) = refs[:cols], refs[cols:]
    current = rhs[...].astype(F32) - update(near, far, tile_refs, repeat)
    forward = dot_t(current.astype(BF16), dinv[...])
    solved = dot_n(forward.astype(BF16), dinv[...])
    out[...] = solved
    spread(solved.astype(BF16), tile_refs, repeat, parts, keep, send)


def remainder(count, refs):
    total = refs[0][...].astype(F32)
    for ref in refs[1:count]:
        total = total + ref[...].astype(F32)
    return total


def backward_kernel(repeat, cols, count, *refs):
    arrived, tile_refs = refs[:count], refs[count : count + cols]
    forward, dinv, out, keep, send, parts = refs[count + cols :]
    rest = forward[...] - remainder(count, arrived)
    solved = dot_n(rest.astype(BF16), dinv[...])
    out[...] = solved
    spread(solved.astype(BF16), tile_refs, repeat, parts, keep, send)


def last_kernel(count, upper_count, *refs):
    arrived = refs[:count]
    forward, dinv = refs[count : count + 2]
    upper = refs[count + 2 : count + 2 + upper_count]
    out = refs[-1]
    rest = forward[...] - remainder(count, arrived)
    out[0, 0] = dot_n(rest.astype(BF16), dinv[...])
    for index, ref in enumerate(upper):
        out[index + 1, 0] = ref[...]


def call(kernel, outs, scratch, *args):
    return pl.pallas_call(
        kernel,
        out_shape=outs,
        in_specs=[pl.BlockSpec(memory_space=pltpu.VMEM)] * len(args),
        out_specs=jax.tree.map(lambda _: pl.BlockSpec(memory_space=pltpu.VMEM), outs),
        scratch_shapes=scratch,
    )(*args)


def per_device(rhs, dinv, tiles, pattern):
    levels, blocks, nrhs, bs = rhs.shape
    assert blocks == 1
    cols = lax.axis_size("col")
    rows = lax.axis_size("row")
    repeat = rows // cols
    chips = rows // 2
    slots = pattern[1, :, 0, :] // cols

    seg = jax.ShapeDtypeStruct((nrhs, bs), F32)
    seg_b = jax.ShapeDtypeStruct((nrhs, bs), BF16)
    chip_segs = jax.ShapeDtypeStruct((chips, nrhs, bs), F32)
    chip_segs_b = jax.ShapeDtypeStruct((chips, nrhs, bs), BF16)
    parts = [pltpu.VMEM((2, chips, nrhs, bs), F32)]

    def gathered_tiles(level):
        picks = (slots[level][None, :] == jnp.arange(repeat, dtype=jnp.int32)[:, None]).astype(F32)
        own = jnp.sum(picks[:, :, None, None] * tiles[level, 0][None].astype(F32), axis=1).astype(BF16)
        return [own] + [swap(own, "col", cols, step) for step in range(1, cols)]

    def gather(mine):
        near = [mine] + [swap(mine, "row", rows, 2 * chip) for chip in range(1, chips)]
        near = jnp.stack(near)
        return near, swap(near, "row", rows, 1)

    def scatter(keep, send):
        total = keep + swap(send, "row", rows, 1).astype(F32)
        return [total[0]] + [
            swap(total[chip].astype(BF16), "row", rows, 2 * chip) for chip in range(1, chips)
        ]

    level_tiles = [gathered_tiles(level) for level in range(levels - 1)]
    forward, mine = call(first_kernel, (seg, seg_b), [], rhs[0, 0], dinv[0, 0])
    forwards = [forward]
    for level in range(1, levels - 1):
        near, far = gather(mine)
        forward, mine = call(
            functools.partial(forward_kernel, repeat, cols),
            (seg, seg_b), [], near, far, *level_tiles[level - 1], rhs[level, 0], dinv[level, 0],
        )
        forwards.append(forward)
    near, far = gather(mine)
    top = levels - 1
    solved, keep, send = call(
        functools.partial(turn_kernel, repeat, cols),
        (seg, chip_segs, chip_segs_b), parts, near, far, *level_tiles[top - 1], rhs[top, 0], dinv[top, 0],
    )
    upper = [solved]
    for level in range(levels - 2, 0, -1):
        arrived = scatter(keep, send)
        solved, keep, send = call(
            functools.partial(backward_kernel, repeat, cols, chips),
            (seg, chip_segs, chip_segs_b), parts, *arrived, *level_tiles[level - 1], forwards[level], dinv[level, 0],
        )
        upper.insert(0, solved)
    arrived = scatter(keep, send)
    return call(
        functools.partial(last_kernel, chips, len(upper)),
        jax.ShapeDtypeStruct(rhs.shape, F32), [], *arrived, forwards[0], dinv[0, 0], *upper,
    )


def solution(mesh):
    in_specs = (
        P(None, "row", None, None),
        P(None, "row", None, None),
        P(None, "row", "col", None, None),
        P(None, None, "row", "col"),
    )
    out_specs = P(None, "row", None, None)
    return jax.shard_map(
        per_device, mesh=mesh, in_specs=in_specs, out_specs=out_specs, check_vma=False
    )
```

time: 337 us -> 78.2 us (0.23)
  waiting for transfers between devices: 279 us -> 29 us
  blocking collectives: 30.2 us -> 0 us
  starting transfers between devices: 0.21 us -> 26.2 us
  between operations: 13.6 us -> 0.21 us
  Pallas kernels: 0 us -> 12.1 us
  matrix products: 7.25 us -> 0 us
  local copies, waits for them, and re-layouts: 1.17 us -> 7.87 us
    psum x6 -> x0, waiting for transfers between devices: 279 us -> none  [the longest x2 110 us: per_device(): column_total = lax.psum(partial_value, 'row')]
    all_gather x2 -> x0, blocking collectives: 30.2 us -> none  [collect(): whole_level = lax.all_gather(rounded, 'row', axis=0, tiled=True)]
    ppermute x0 -> x22, waiting for transfers between devices: none -> 29 us  [swap(): return lax.ppermute(value, axis, [(i, i ^ mask) for i in range(size)])]
    ppermute x0 -> x22, starting transfers between devices: none -> 26.2 us  [swap(): return lax.ppermute(value, axis, [(i, i ^ mask) for i in range(size)])]
    pallas_call x0 -> x5, Pallas kernels: none -> 12.1 us  [call(): pl.pallas_call(kernel, out_shape=outs, in_specs=[pl.BlockSpec(memory_spac...]
    dot_general x9 -> x0, matrix products: 7.25 us -> none  [the longest x3 3.11 us: per_device(): jnp.einsum('rjb,rba->rja', remainder.astype(jnp.bfloat16), dinv[level_now...]
    squeeze x0 -> x4, local copies, waits for them, and re-layouts: none -> 4.49 us  [the longest x1 1.82 us: per_device(): dinv[top, 0]]
  transfers between devices with their start and end apart: 6 -> 22, of which waited for: 6 -> 15; matrix products, arithmetic and copies ran while one was open for 0% -> 2% of each run, Pallas kernels for 0% -> 0%
where the time goes in v1:
time: 78.2 us; the launch traced here: 77.8 us
  waiting for transfers between devices  29 us (37%)
  starting transfers between devices  26.2 us (34%)
  Pallas kernels  12.1 us (15%)
  local copies, waits for them, and re-layouts  7.87 us (10%)
  other arithmetic  2.4 us (3%)
    ppermute x22, waiting for transfers between devices, swap(): return lax.ppermute(value, axis, [(i, i ^ mask) for i in range(size)])  29 us
    ppermute x22, starting transfers between devices, swap(): return lax.ppermute(value, axis, [(i, i ^ mask) for i in range(size)])  26.2 us
    pallas_call x5, Pallas kernels, call(): pl.pallas_call(kernel, out_shape=outs, in_specs=[pl.BlockSpec(memory_spac...  12.1 us
    unnamed x42, local copies, waits for them, and re-layouts  2.67 us
    another operation x2, other arithmetic  1.98 us
    squeeze x1, local copies, waits for them, and re-layouts, per_device(): dinv[top, 0]  1.82 us
  transfers between devices with their start and end apart: 22, of which 15 were waited for; matrix products, arithmetic and copies ran while one was open for 2% of the time, Pallas kernels for 0%

profile of v1, /device:TPU:0, one launch (start us, length us, event | category | flops | bytes accessed | tf_op | source)
XLA Modules:
  0.0 77.8 jit_solution(5175438309671349163)
XLA Ops:
  0.0 1.4 %slice_bitcast_fusion.11 = (bf16[64,256]{1,0:T(8,128)(2,1)}, bf16[64,256]{1,0:T(8,128)(2,1)}, bf16[64,256]{1,0:T(8,128)(2,1)}) fusion(bf16[3,1,64,256]{3,2,1,0:T(8,128)(2,1)} %param.4), kind=kLoop, calls=%fused_computation.19 | loop fusion | bytes 196608 | tf_op jit(solution)/shard_map/squeeze | solution.py:159
  1.4 1.8 %slice_bitcast_fusion = (bf16[256,256]{1,0:T(8,128)(2,1)}, bf16[256,256]{1,0:T(8,128)(2,1)}, bf16[256,256]{1,0:T(8,128)(2,1)}) fusion(bf16[3,1,256,256]{3,2,1,0:T(8,128)(2,1)} %param.5), kind=kLoop, calls=%fused_computation.8 | loop fusion | bytes 786432 | tf_op jit(solution)/shard_map/squeeze | solution.py:159
  3.3 1.7 %shard_map.46 = (f32[64,256]{1,0:T(8,128)}, bf16[64,256]{1,0:T(8,128)(2,1)}) custom-call(bf16[64,256]{1,0:T(8,128)(2,1)} %get-tuple-element.41.rhs, bf16[256,256]{1,0:T(8,128)(2,1)} %get-tuple-element.32.dinv.refs_5_), custom_call_target="tpu_custom_call" | custom-call | tf_op jit(solution)/shard_map/pallas_call | solution.py:105
  5.0 5.1 %collective-permute-start.2 = (bf16[64,256]{1,0:T(8,128)(2,1)}, bf16[64,256]{1,0:T(8,128)(2,1)S(1)}, u32[]{:S(2)}, u32[]{:S(2)}) collective-permute-start(bf16[64,256]{1,0:T(8,128)(2,1)} %get-tuple-element.15), channel_id=1, source_target_pairs={{0,24},{4,28},{8,16},{12,20},{16,8},{20,12},{24,0},{28,4},{1,25},{... | collective-permute-start | bytes 98312 | tf_op jit(solution)/shard_map/ppermute | solution.py:15
  10.1 0.0 collective-permute-start.1
  10.1 0.6 collective-permute-start
  10.7 0.7 slice-done
  11.4 0.1 bitcast_convert_fusion
  11.5 0.1 multiply_reduce_fusion.1.refs_0_.refs_4_
  11.6 2.7 %collective-permute-start.6 = (bf16[2,256,256]{2,1,0:T(8,128)(2,1)S(1)}, bf16[2,256,256]{2,1,0:T(8,128)(2,1)S(1)}, u32[]{:S(2)}, u32[]{:S(2)}) collective-permute-start(bf16[2,256,256]{2,1,0:T(8,128)(2,1)S(1)} %multiply_reduce_fusion.1.refs_0_.refs_4_), channel_id=1, source_target_pairs={{0,3},{1,2},{2,1},{3,0},{4,7},{5,6},{6,5},{7,4},{8,11},{9,10},{10,... | collective-permute-start | bytes 786440 | tf_op jit(solution)/shard_map/ppermute | solution.py:15
  14.4 0.5 collective-permute-start.5
  14.9 0.0 collective-permute-done.2
  14.9 0.3 collective-permute-start.4
  15.2 0.1 collective-permute-start.3
  15.3 1.3 %collective-permute-done.3.far = bf16[4,64,256]{2,1,0:T(8,128)(2,1)S(1)} collective-permute-done((bf16[4,64,256]{2,1,0:T(8,128)(2,1)S(1)}, bf16[4,64,256]{2,1,0:T(8,128)(2,1)S(1)}, u32[]{:S(2)}, u32[]{:S(2)}) %collective-permute-start.3) | collective-permute-done | bytes 131104 | tf_op jit(solution)/shard_map/ppermute | solution.py:15
  16.7 5.2 %collective-permute-done.6.refs_3_.refs_7_ = bf16[2,256,256]{2,1,0:T(8,128)(2,1)S(1)} collective-permute-done((bf16[2,256,256]{2,1,0:T(8,128)(2,1)S(1)}, bf16[2,256,256]{2,1,0:T(8,128)(2,1)S(1)}, u32[]{:S(2)}, u32[]{:S(2)}) %collective-permute-start.6) | collective-permute-done | bytes 262176 | tf_op jit(solution)/shard_map/ppermute | solution.py:15
  21.8 3.9 %collective-permute-done.5.refs_2_.refs_6_ = bf16[2,256,256]{2,1,0:T(8,128)(2,1)S(1)} collective-permute-done((bf16[2,256,256]{2,1,0:T(8,128)(2,1)S(1)}, bf16[2,256,256]{2,1,0:T(8,128)(2,1)S(1)}, u32[]{:S(2)}, u32[]{:S(2)}) %collective-permute-start.5) | collective-permute-done | bytes 262176 | tf_op jit(solution)/shard_map/ppermute | solution.py:15
  25.7 0.1 collective-permute-done.4.refs_1_.refs_5_
  25.8 0.6 copy-done.3
  26.4 0.1 copy-done.4
  26.5 2.6 %shard_map.47 = (f32[64,256]{1,0:T(8,128)}, bf16[64,256]{1,0:T(8,128)(2,1)}) custom-call(bf16[4,64,256]{2,1,0:T(8,128)(2,1)} %copy-done.7, bf16[4,64,256]{2,1,0:T(8,128)(2,1)} %copy-done.12, bf16[2,256,256]{2,1,0:T(8,128)(2,1)} %copy-done, bf16[2,256,256]{2,1,0:T(8,128)(2,1)} %copy-done.4, bf16[2,256,256]{2,1,0:T(8,128)(2,1)} %copy-done.3, ...), custom_call_target="tpu_custom_call" | custom-call | tf_op jit(solution)/shard_map/pallas_call | solution.py:105
  29.1 3.5 %collective-permute-start.9 = (bf16[64,256]{1,0:T(8,128)(2,1)}, bf16[64,256]{1,0:T(8,128)(2,1)S(1)}, u32[]{:S(2)}, u32[]{:S(2)}) collective-permute-start(bf16[64,256]{1,0:T(8,128)(2,1)} %get-tuple-element.16), channel_id=1, source_target_pairs={{0,24},{4,28},{8,16},{12,20},{16,8},{20,12},{24,0},{28,4},{1,25},{... | collective-permute-start | bytes 98312 | tf_op jit(solution)/shard_map/ppermute | solution.py:15
  32.6 0.8 %collective-permute-start.7 = (bf16[64,256]{1,0:T(8,128)(2,1)}, bf16[64,256]{1,0:T(8,128)(2,1)S(1)}, u32[]{:S(2)}, u32[]{:S(2)}) collective-permute-start(bf16[64,256]{1,0:T(8,128)(2,1)} %get-tuple-element.16), channel_id=1, source_target_pairs={{0,8},{4,12},{8,0},{12,4},{16,24},{20,28},{24,16},{28,20},{1,9},{5... | collective-permute-start | bytes 98312 | tf_op jit(solution)/shard_map/ppermute | solution.py:15
  33.5 0.1 multiply_reduce_fusion.refs_0_
  33.6 1.8 %collective-permute-start.13 = (bf16[2,256,256]{2,1,0:T(8,128)(2,1)S(1)}, bf16[2,256,256]{2,1,0:T(8,128)(2,1)S(1)}, u32[]{:S(2)}, u32[]{:S(2)}) collective-permute-start(bf16[2,256,256]{2,1,0:T(8,128)(2,1)S(1)} %multiply_reduce_fusion.refs_0_), channel_id=1, source_target_pairs={{0,3},{1,2},{2,1},{3,0},{4,7},{5,6},{6,5},{7,4},{8,11},{9,10},{10,... | collective-permute-start | bytes 786440 | tf_op jit(solution)/shard_map/ppermute | solution.py:15
  35.4 1.2 %collective-permute-start.12 = (bf16[2,256,256]{2,1,0:T(8,128)(2,1)S(1)}, bf16[2,256,256]{2,1,0:T(8,128)(2,1)S(1)}, u32[]{:S(2)}, u32[]{:S(2)}) collective-permute-start(bf16[2,256,256]{2,1,0:T(8,128)(2,1)S(1)} %multiply_reduce_fusion.refs_0_), channel_id=1, source_target_pairs={{0,2},{1,3},{2,0},{3,1},{4,6},{5,7},{6,4},{7,5},{8,10},{9,11},{10,... | collective-permute-start | bytes 786440 | tf_op jit(solution)/shard_map/ppermute | solution.py:15
  36.6 0.0 collective-permute-done.9
  36.6 0.5 collective-permute-start.11
  37.2 0.5 collective-permute-done.8
  37.6 0.0 collective-permute-done.7
  37.7 0.1 collective-permute-start.10
  37.8 6.0 %collective-permute-done.13.refs_3_ = bf16[2,256,256]{2,1,0:T(8,128)(2,1)S(1)} collective-permute-done((bf16[2,256,256]{2,1,0:T(8,128)(2,1)S(1)}, bf16[2,256,256]{2,1,0:T(8,128)(2,1)S(1)}, u32[]{:S(2)}, u32[]{:S(2)}) %collective-permute-start.13) | collective-permute-done | bytes 262176 | tf_op jit(solution)/shard_map/ppermute | solution.py:15
  43.8 3.8 %collective-permute-done.12.refs_2_ = bf16[2,256,256]{2,1,0:T(8,128)(2,1)S(1)} collective-permute-done((bf16[2,256,256]{2,1,0:T(8,128)(2,1)S(1)}, bf16[2,256,256]{2,1,0:T(8,128)(2,1)S(1)}, u32[]{:S(2)}, u32[]{:S(2)}) %collective-permute-start.12) | collective-permute-done | bytes 262176 | tf_op jit(solution)/shard_map/ppermute | solution.py:15
  47.6 0.1 collective-permute-done.11.refs_1_
  47.7 0.6 copy-done.9
  48.3 0.1 copy-done.10
  48.4 0.1 copy-done.11
  48.5 3.4 %shard_map.48 = (f32[64,256]{1,0:T(8,128)}, f32[4,64,256]{2,1,0:T(8,128)}, bf16[4,64,256]{2,1,0:T(8,128)(2,1)}) custom-call(bf16[4,64,256]{2,1,0:T(8,128)(2,1)} %copy-done.6, bf16[4,64,256]{2,1,0:T(8,128)(2,1)} %copy-done.11, bf16[2,256,256]{2,1,0:T(8,128)(2,1)} %copy-done.1, bf16[2,256,256]{2,1,0:T(8,128)(2,1)} %copy-done.10, ...), custom_call_target="tpu_custom_call" | custom-call | tf_op jit(solution)/shard_map/pallas_call | solution.py:105
  51.8 0.0 collective-permute-start.14
  51.8 1.6 %collective-permute-done.14 = bf16[4,64,256]{2,1,0:T(8,128)(2,1)S(1)} collective-permute-done((bf16[4,64,256]{2,1,0:T(8,128)(2,1)}, bf16[4,64,256]{2,1,0:T(8,128)(2,1)S(1)}, u32[]{:S(2)}, u32[]{:S(2)}) %collective-permute-start.14) | collective-permute-done | bytes 131104 | tf_op jit(solution)/shard_map/ppermute | solution.py:15
  53.4 1.0 %fusion.1 = (bf16[4,64,256]{2,1,0:T(8,128)(2,1)S(1)}, f32[4,64,256]{2,1,0:T(8,128)S(1)}) fusion(f32[4,64,256]{2,1,0:T(8,128)} %get-tuple-element.17, bf16[4,64,256]{2,1,0:T(8,128)(2,1)S(1)} %collective-permute-done.14), kind=kLoop, calls=%fused_computation.31 | loop fusion | flops 196608 | bytes 786432 | tf_op jit(solution)/shard_map/convert.7
  54.4 3.6 %collective-permute-start.17 = (bf16[64,256]{1,0:T(8,128)(2,1)S(1)}, bf16[64,256]{1,0:T(8,128)(2,1)S(1)}, u32[]{:S(2)}, u32[]{:S(2)}) collective-permute-start(bf16[64,256]{1,0:T(8,128)(2,1)S(1)} %get-tuple-element.37), channel_id=1, source_target_pairs={{0,24},{4,28},{8,16},{12,20},{16,8},{20,12},{24,0},{28,4},{1,25},{... | collective-permute-start | bytes 98312 | tf_op jit(solution)/shard_map/ppermute | solution.py:15
  58.0 0.0 collective-permute-start.16
  58.0 0.8 %collective-permute-start.15 = (bf16[64,256]{1,0:T(8,128)(2,1)S(1)}, bf16[64,256]{1,0:T(8,128)(2,1)S(1)}, u32[]{:S(2)}, u32[]{:S(2)}) collective-permute-start(bf16[64,256]{1,0:T(8,128)(2,1)S(1)} %get-tuple-element.39), channel_id=1, source_target_pairs={{0,8},{4,12},{8,0},{12,4},{16,24},{20,28},{24,16},{28,20},{1,9},{5... | collective-permute-start | bytes 98312 | tf_op jit(solution)/shard_map/ppermute | solution.py:15
  58.9 0.6 slice_bitcast_fusion.4.refs_0_
  59.5 0.7 collective-permute-done.17.refs_3_
  60.2 2.6 %collective-permute-done.16.refs_2_ = bf16[64,256]{1,0:T(8,128)(2,1)S(1)} collective-permute-done((bf16[64,256]{1,0:T(8,128)(2,1)S(1)}, bf16[64,256]{1,0:T(8,128)(2,1)S(1)}, u32[]{:S(2)}, u32[]{:S(2)}) %collective-permute-start.16) | collective-permute-done | bytes 32800 | tf_op jit(solution)/shard_map/ppermute | solution.py:15
  62.8 0.0 collective-permute-done.15.refs_1_
  62.8 0.6 copy-done.14
  63.4 0.0 copy-done.15
  63.4 2.5 %shard_map.49 = (f32[64,256]{1,0:T(8,128)}, f32[4,64,256]{2,1,0:T(8,128)}, bf16[4,64,256]{2,1,0:T(8,128)(2,1)}) custom-call(f32[64,256]{1,0:T(8,128)} %slice_bitcast_fusion.4.refs_0_, bf16[64,256]{1,0:T(8,128)(2,1)} %copy-done.15, bf16[64,256]{1,0:T(8,128)(2,1)} %copy-done.14, bf16[64,256]{1,0:T(8,128)(2,1)} %copy-done.13, bf16[2,256,256]{2,1,0:T(8,128)(2,1)} %copy-done, ...), custom_call_target="tpu_custom_call" | custom-call | tf_op jit(solution)/shard_map/pallas_call | solution.py:105
  66.0 0.0 collective-permute-start.18
  66.0 1.6 %collective-permute-done.18 = bf16[4,64,256]{2,1,0:T(8,128)(2,1)S(1)} collective-permute-done((bf16[4,64,256]{2,1,0:T(8,128)(2,1)}, bf16[4,64,256]{2,1,0:T(8,128)(2,1)S(1)}, u32[]{:S(2)}, u32[]{:S(2)}) %collective-permute-start.18) | collective-permute-done | bytes 131104 | tf_op jit(solution)/shard_map/ppermute | solution.py:15
  67.5 1.0 %fusion = (bf16[4,64,256]{2,1,0:T(8,128)(2,1)S(1)}, f32[4,64,256]{2,1,0:T(8,128)S(1)}) fusion(f32[4,64,256]{2,1,0:T(8,128)} %get-tuple-element.20, bf16[4,64,256]{2,1,0:T(8,128)(2,1)S(1)} %collective-permute-done.18), kind=kLoop, calls=%fused_computation.30 | loop fusion | flops 196608 | bytes 786432 | tf_op jit(solution)/shard_map/convert.4
  68.5 1.5 %collective-permute-start.21 = (bf16[64,256]{1,0:T(8,128)(2,1)S(1)}, bf16[64,256]{1,0:T(8,128)(2,1)S(1)}, u32[]{:S(2)}, u32[]{:S(2)}) collective-permute-start(bf16[64,256]{1,0:T(8,128)(2,1)S(1)} %get-tuple-element.34), channel_id=1, source_target_pairs={{0,24},{4,28},{8,16},{12,20},{16,8},{20,12},{24,0},{28,4},{1,25},{... | collective-permute-start | bytes 98312 | tf_op jit(solution)/shard_map/ppermute | solution.py:15
  70.1 0.6 collective-permute-start.20
  70.7 2.3 %collective-permute-start.19 = (bf16[64,256]{1,0:T(8,128)(2,1)S(1)}, bf16[64,256]{1,0:T(8,128)(2,1)S(1)}, u32[]{:S(2)}, u32[]{:S(2)}) collective-permute-start(bf16[64,256]{1,0:T(8,128)(2,1)S(1)} %get-tuple-element.36), channel_id=1, source_target_pairs={{0,8},{4,12},{8,0},{12,4},{16,24},{20,28},{24,16},{28,20},{1,9},{5... | collective-permute-start | bytes 98312 | tf_op jit(solution)/shard_map/ppermute | solution.py:15
  73.0 0.6 slice_bitcast_fusion.3.refs_0_
  73.6 1.1 %collective-permute-done.21.refs_3_ = bf16[64,256]{1,0:T(8,128)(2,1)S(1)} collective-permute-done((bf16[64,256]{1,0:T(8,128)(2,1)S(1)}, bf16[64,256]{1,0:T(8,128)(2,1)S(1)}, u32[]{:S(2)}, u32[]{:S(2)}) %collective-permute-start.21) | collective-permute-done | bytes 32800 | tf_op jit(solution)/shard_map/ppermute | solution.py:15
  74.7 0.3 collective-permute-done.20.refs_2_
  75.0 0.3 collective-permute-done.19.refs_1_
  75.3 0.3 copy-done.19
  75.6 0.3 copy-done.20
  75.9 1.9 %shard_map.50 = f32[3,1,64,256]{3,2,1,0:T(8,128)} custom-call(f32[64,256]{1,0:T(8,128)} %slice_bitcast_fusion.3.refs_0_, bf16[64,256]{1,0:T(8,128)(2,1)} %copy-done.20, bf16[64,256]{1,0:T(8,128)(2,1)} %copy-done.19, bf16[64,256]{1,0:T(8,128)(2,1)} %copy-done.18, f32[64,256]{1,0:T(8,128)} %get-tuple-element.22.refs_4_, ...), custom_call_target="tpu_custom_call" | custom-call | tf_op jit(solution)/shard_map/pallas_call | solution.py:105
  (46 shorter events, 0.2 us)
Async XLA Ops:
  1.4 9.9 %copy-start.5 = (bf16[2,1,2,256,256]{4,3,2,1,0:T(8,128)(2,1)S(1)}, bf16[2,1,2,256,256]{4,3,2,1,0:T(8,128)(2,1)}, u32[]{:S(2)}) copy-start(bf16[2,1,2,256,256]{4,3,2,1,0:T(8,128)(2,1)} %param.6) | copy-start | bytes 1572868
  5.0 9.9 %collective-permute-start.2 = (bf16[64,256]{1,0:T(8,128)(2,1)}, bf16[64,256]{1,0:T(8,128)(2,1)S(1)}, u32[]{:S(2)}, u32[]{:S(2)}) collective-permute-start(bf16[64,256]{1,0:T(8,128)(2,1)} %get-tuple-element.15), channel_id=1, source_target_pairs={{0,24},{4,28},{8,16},{12,20},{16,8},{20,12},{24,0},{28,4},{1,25},{... | collective-permute-start | bytes 98312 | tf_op jit(solution)/shard_map/ppermute | solution.py:15
  10.1 5.1 %collective-permute-start.1 = (bf16[64,256]{1,0:T(8,128)(2,1)}, bf16[64,256]{1,0:T(8,128)(2,1)S(1)}, u32[]{:S(2)}, u32[]{:S(2)}) collective-permute-start(bf16[64,256]{1,0:T(8,128)(2,1)} %get-tuple-element.15), channel_id=1, source_target_pairs={{0,16},{4,20},{8,24},{12,28},{16,0},{20,4},{24,8},{28,12},{1,17},{... | collective-permute-start | bytes 98312 | tf_op jit(solution)/shard_map/ppermute | solution.py:15
  10.1 5.1 %collective-permute-start = (bf16[64,256]{1,0:T(8,128)(2,1)}, bf16[64,256]{1,0:T(8,128)(2,1)S(1)}, u32[]{:S(2)}, u32[]{:S(2)}) collective-permute-start(bf16[64,256]{1,0:T(8,128)(2,1)} %get-tuple-element.15), channel_id=1, source_target_pairs={{0,8},{4,12},{8,0},{12,4},{16,24},{20,28},{24,16},{28,20},{1,9},{5... | collective-permute-start | bytes 98312 | tf_op jit(solution)/shard_map/ppermute | solution.py:15
  10.7 0.7 slice-start
  11.5 3.7 %copy-start.16 = (bf16[64,256]{1,0:T(8,128)(2,1)S(1)}, bf16[64,256]{1,0:T(8,128)(2,1)}, u32[]{:S(2)}) copy-start(bf16[64,256]{1,0:T(8,128)(2,1)} %get-tuple-element.15) | copy-start | bytes 98308
  11.6 14.2 %copy-start = (bf16[2,256,256]{2,1,0:T(8,128)(2,1)}, bf16[2,256,256]{2,1,0:T(8,128)(2,1)S(1)}, u32[]{:S(2)}) copy-start(bf16[2,256,256]{2,1,0:T(8,128)(2,1)S(1)} %multiply_reduce_fusion.1.refs_0_.refs_4_) | copy-start | bytes 786436
  11.6 10.2 %collective-permute-start.6 = (bf16[2,256,256]{2,1,0:T(8,128)(2,1)S(1)}, bf16[2,256,256]{2,1,0:T(8,128)(2,1)S(1)}, u32[]{:S(2)}, u32[]{:S(2)}) collective-permute-start(bf16[2,256,256]{2,1,0:T(8,128)(2,1)S(1)} %multiply_reduce_fusion.1.refs_0_.refs_4_), channel_id=1, source_target_pairs={{0,3},{1,2},{2,1},{3,0},{4,7},{5,6},{6,5},{7,4},{8,11},{9,10},{10,... | collective-permute-start | bytes 786440 | tf_op jit(solution)/shard_map/ppermute | solution.py:15
  14.4 11.3 %collective-permute-start.5 = (bf16[2,256,256]{2,1,0:T(8,128)(2,1)S(1)}, bf16[2,256,256]{2,1,0:T(8,128)(2,1)S(1)}, u32[]{:S(2)}, u32[]{:S(2)}) collective-permute-start(bf16[2,256,256]{2,1,0:T(8,128)(2,1)S(1)} %multiply_reduce_fusion.1.refs_0_.refs_4_), channel_id=1, source_target_pairs={{0,2},{1,3},{2,0},{3,1},{4,6},{5,7},{6,4},{7,5},{8,10},{9,11},{10,... | collective-permute-start | bytes 786440 | tf_op jit(solution)/shard_map/ppermute | solution.py:15
  14.9 10.9 %collective-permute-start.4 = (bf16[2,256,256]{2,1,0:T(8,128)(2,1)S(1)}, bf16[2,256,256]{2,1,0:T(8,128)(2,1)S(1)}, u32[]{:S(2)}, u32[]{:S(2)}) collective-permute-start(bf16[2,256,256]{2,1,0:T(8,128)(2,1)S(1)} %multiply_reduce_fusion.1.refs_0_.refs_4_), channel_id=1, source_target_pairs={{0,1},{1,0},{2,3},{3,2},{4,5},{5,4},{6,7},{7,6},{8,9},{9,8},{10,11... | collective-permute-start | bytes 786440 | tf_op jit(solution)/shard_map/ppermute | solution.py:15
  15.2 10.6 %copy-start.7 = (bf16[4,64,256]{2,1,0:T(8,128)(2,1)}, bf16[4,64,256]{2,1,0:T(8,128)(2,1)S(1)}, u32[]{:S(2)}) copy-start(bf16[4,64,256]{2,1,0:T(8,128)(2,1)S(1)} %pad_maximum_fusion.near) | copy-start | bytes 393220
  15.2 1.4 %collective-permute-start.3 = (bf16[4,64,256]{2,1,0:T(8,128)(2,1)S(1)}, bf16[4,64,256]{2,1,0:T(8,128)(2,1)S(1)}, u32[]{:S(2)}, u32[]{:S(2)}) collective-permute-start(bf16[4,64,256]{2,1,0:T(8,128)(2,1)S(1)} %pad_maximum_fusion.near), channel_id=1, source_target_pairs={{0,4},{4,0},{8,12},{12,8},{16,20},{20,16},{24,28},{28,24},{1,5},{5... | collective-permute-start | bytes 393224 | tf_op jit(solution)/shard_map/ppermute | solution.py:15
  16.6 9.2 %copy-start.12 = (bf16[4,64,256]{2,1,0:T(8,128)(2,1)}, bf16[4,64,256]{2,1,0:T(8,128)(2,1)S(1)}, u32[]{:S(2)}) copy-start(bf16[4,64,256]{2,1,0:T(8,128)(2,1)S(1)} %collective-permute-done.3.far) | copy-start | bytes 393220
  21.8 4.0 %copy-start.2 = (bf16[2,256,256]{2,1,0:T(8,128)(2,1)}, bf16[2,256,256]{2,1,0:T(8,128)(2,1)S(1)}, u32[]{:S(2)}) copy-start(bf16[2,256,256]{2,1,0:T(8,128)(2,1)S(1)} %collective-permute-done.6.refs_3_.refs_7_) | copy-start | bytes 786436
  25.7 0.7 copy-start.3
  25.8 0.7 copy-start.4
  29.1 7.6 %collective-permute-start.9 = (bf16[64,256]{1,0:T(8,128)(2,1)}, bf16[64,256]{1,0:T(8,128)(2,1)S(1)}, u32[]{:S(2)}, u32[]{:S(2)}) collective-permute-start(bf16[64,256]{1,0:T(8,128)(2,1)} %get-tuple-element.16), channel_id=1, source_target_pairs={{0,24},{4,28},{8,16},{12,20},{16,8},{20,12},{24,0},{28,4},{1,25},{... | collective-permute-start | bytes 98312 | tf_op jit(solution)/shard_map/ppermute | solution.py:15
  32.6 5.0 %collective-permute-start.8 = (bf16[64,256]{1,0:T(8,128)(2,1)}, bf16[64,256]{1,0:T(8,128)(2,1)S(1)}, u32[]{:S(2)}, u32[]{:S(2)}) collective-permute-start(bf16[64,256]{1,0:T(8,128)(2,1)} %get-tuple-element.16), channel_id=1, source_target_pairs={{0,16},{4,20},{8,24},{12,28},{16,0},{20,4},{24,8},{28,12},{1,17},{... | collective-permute-start | bytes 98312 | tf_op jit(solution)/shard_map/ppermute | solution.py:15
  32.6 5.0 %collective-permute-start.7 = (bf16[64,256]{1,0:T(8,128)(2,1)}, bf16[64,256]{1,0:T(8,128)(2,1)S(1)}, u32[]{:S(2)}, u32[]{:S(2)}) collective-permute-start(bf16[64,256]{1,0:T(8,128)(2,1)} %get-tuple-element.16), channel_id=1, source_target_pairs={{0,8},{4,12},{8,0},{12,4},{16,24},{20,28},{24,16},{28,20},{1,9},{5... | collective-permute-start | bytes 98312 | tf_op jit(solution)/shard_map/ppermute | solution.py:15
  33.5 4.2 %copy-start.17 = (bf16[64,256]{1,0:T(8,128)(2,1)S(1)}, bf16[64,256]{1,0:T(8,128)(2,1)}, u32[]{:S(2)}) copy-start(bf16[64,256]{1,0:T(8,128)(2,1)} %get-tuple-element.16) | copy-start | bytes 98308
  33.6 14.1 %copy-start.1 = (bf16[2,256,256]{2,1,0:T(8,128)(2,1)}, bf16[2,256,256]{2,1,0:T(8,128)(2,1)S(1)}, u32[]{:S(2)}) copy-start(bf16[2,256,256]{2,1,0:T(8,128)(2,1)S(1)} %multiply_reduce_fusion.refs_0_) | copy-start | bytes 786436
  33.6 10.2 %collective-permute-start.13 = (bf16[2,256,256]{2,1,0:T(8,128)(2,1)S(1)}, bf16[2,256,256]{2,1,0:T(8,128)(2,1)S(1)}, u32[]{:S(2)}, u32[]{:S(2)}) collective-permute-start(bf16[2,256,256]{2,1,0:T(8,128)(2,1)S(1)} %multiply_reduce_fusion.refs_0_), channel_id=1, source_target_pairs={{0,3},{1,2},{2,1},{3,0},{4,7},{5,6},{6,5},{7,4},{8,11},{9,10},{10,... | collective-permute-start | bytes 786440 | tf_op jit(solution)/shard_map/ppermute | solution.py:15
  35.4 12.2 %collective-permute-start.12 = (bf16[2,256,256]{2,1,0:T(8,128)(2,1)S(1)}, bf16[2,256,256]{2,1,0:T(8,128)(2,1)S(1)}, u32[]{:S(2)}, u32[]{:S(2)}) collective-permute-start(bf16[2,256,256]{2,1,0:T(8,128)(2,1)S(1)} %multiply_reduce_fusion.refs_0_), channel_id=1, source_target_pairs={{0,2},{1,3},{2,0},{3,1},{4,6},{5,7},{6,4},{7,5},{8,10},{9,11},{10,... | collective-permute-start | bytes 786440 | tf_op jit(solution)/shard_map/ppermute | solution.py:15
  36.6 11.0 %collective-permute-start.11 = (bf16[2,256,256]{2,1,0:T(8,128)(2,1)S(1)}, bf16[2,256,256]{2,1,0:T(8,128)(2,1)S(1)}, u32[]{:S(2)}, u32[]{:S(2)}) collective-permute-start(bf16[2,256,256]{2,1,0:T(8,128)(2,1)S(1)} %multiply_reduce_fusion.refs_0_), channel_id=1, source_target_pairs={{0,1},{1,0},{2,3},{3,2},{4,5},{5,4},{6,7},{7,6},{8,9},{9,8},{10,11... | collective-permute-start | bytes 786440 | tf_op jit(solution)/shard_map/ppermute | solution.py:15
  37.7 10.0 %copy-start.6 = (bf16[4,64,256]{2,1,0:T(8,128)(2,1)}, bf16[4,64,256]{2,1,0:T(8,128)(2,1)S(1)}, u32[]{:S(2)}) copy-start(bf16[4,64,256]{2,1,0:T(8,128)(2,1)S(1)} %pad_maximum_fusion.1.near) | copy-start | bytes 393220
  37.7 10.0 %collective-permute-start.10 = (bf16[4,64,256]{2,1,0:T(8,128)(2,1)S(1)}, bf16[4,64,256]{2,1,0:T(8,128)(2,1)S(1)}, u32[]{:S(2)}, u32[]{:S(2)}) collective-permute-start(bf16[4,64,256]{2,1,0:T(8,128)(2,1)S(1)} %pad_maximum_fusion.1.near), channel_id=1, source_target_pairs={{0,4},{4,0},{8,12},{12,8},{16,20},{20,16},{24,28},{28,24},{1,5},{5... | collective-permute-start | bytes 393224 | tf_op jit(solution)/shard_map/ppermute | solution.py:15
  43.8 3.9 %copy-start.8 = (bf16[2,256,256]{2,1,0:T(8,128)(2,1)}, bf16[2,256,256]{2,1,0:T(8,128)(2,1)S(1)}, u32[]{:S(2)}) copy-start(bf16[2,256,256]{2,1,0:T(8,128)(2,1)S(1)} %collective-permute-done.13.refs_3_) | copy-start | bytes 786436
  47.6 0.7 copy-start.9
  47.7 0.7 copy-start.10
  47.7 0.8 copy-start.11
  51.8 1.6 %collective-permute-start.14 = (bf16[4,64,256]{2,1,0:T(8,128)(2,1)}, bf16[4,64,256]{2,1,0:T(8,128)(2,1)S(1)}, u32[]{:S(2)}, u32[]{:S(2)}) collective-permute-start(bf16[4,64,256]{2,1,0:T(8,128)(2,1)} %get-tuple-element.18), channel_id=1, source_target_pairs={{0,4},{4,0},{8,12},{12,8},{16,20},{20,16},{24,28},{28,24},{1,5},{5... | collective-permute-start | bytes 393224 | tf_op jit(solution)/shard_map/ppermute | solution.py:15
  54.4 5.8 %collective-permute-start.17 = (bf16[64,256]{1,0:T(8,128)(2,1)S(1)}, bf16[64,256]{1,0:T(8,128)(2,1)S(1)}, u32[]{:S(2)}, u32[]{:S(2)}) collective-permute-start(bf16[64,256]{1,0:T(8,128)(2,1)S(1)} %get-tuple-element.37), channel_id=1, source_target_pairs={{0,24},{4,28},{8,16},{12,20},{16,8},{20,12},{24,0},{28,4},{1,25},{... | collective-permute-start | bytes 98312 | tf_op jit(solution)/shard_map/ppermute | solution.py:15
  58.0 4.8 %collective-permute-start.16 = (bf16[64,256]{1,0:T(8,128)(2,1)S(1)}, bf16[64,256]{1,0:T(8,128)(2,1)S(1)}, u32[]{:S(2)}, u32[]{:S(2)}) collective-permute-start(bf16[64,256]{1,0:T(8,128)(2,1)S(1)} %get-tuple-element.38), channel_id=1, source_target_pairs={{0,16},{4,20},{8,24},{12,28},{16,0},{20,4},{24,8},{28,12},{1,17},{... | collective-permute-start | bytes 98312 | tf_op jit(solution)/shard_map/ppermute | solution.py:15
  58.0 4.8 %collective-permute-start.15 = (bf16[64,256]{1,0:T(8,128)(2,1)S(1)}, bf16[64,256]{1,0:T(8,128)(2,1)S(1)}, u32[]{:S(2)}, u32[]{:S(2)}) collective-permute-start(bf16[64,256]{1,0:T(8,128)(2,1)S(1)} %get-tuple-element.39), channel_id=1, source_target_pairs={{0,8},{4,12},{8,0},{12,4},{16,24},{20,28},{24,16},{28,20},{1,9},{5... | collective-permute-start | bytes 98312 | tf_op jit(solution)/shard_map/ppermute | solution.py:15
  60.2 2.7 %copy-start.13 = (bf16[64,256]{1,0:T(8,128)(2,1)}, bf16[64,256]{1,0:T(8,128)(2,1)S(1)}, u32[]{:S(2)}) copy-start(bf16[64,256]{1,0:T(8,128)(2,1)S(1)} %collective-permute-done.17.refs_3_) | copy-start | bytes 98308
  62.8 0.6 copy-start.14
  62.8 0.6 copy-start.15
  66.0 1.6 %collective-permute-start.18 = (bf16[4,64,256]{2,1,0:T(8,128)(2,1)}, bf16[4,64,256]{2,1,0:T(8,128)(2,1)S(1)}, u32[]{:S(2)}, u32[]{:S(2)}) collective-permute-start(bf16[4,64,256]{2,1,0:T(8,128)(2,1)} %get-tuple-element.21), channel_id=1, source_target_pairs={{0,4},{4,0},{8,12},{12,8},{16,20},{20,16},{24,28},{28,24},{1,5},{5... | collective-permute-start | bytes 393224 | tf_op jit(solution)/shard_map/ppermute | solution.py:15
  68.5 6.1 %collective-permute-start.21 = (bf16[64,256]{1,0:T(8,128)(2,1)S(1)}, bf16[64,256]{1,0:T(8,128)(2,1)S(1)}, u32[]{:S(2)}, u32[]{:S(2)}) collective-permute-start(bf16[64,256]{1,0:T(8,128)(2,1)S(1)} %get-tuple-element.34), channel_id=1, source_target_pairs={{0,24},{4,28},{8,16},{12,20},{16,8},{20,12},{24,0},{28,4},{1,25},{... | collective-permute-start | bytes 98312 | tf_op jit(solution)/shard_map/ppermute | solution.py:15
  70.1 4.9 %collective-permute-start.20 = (bf16[64,256]{1,0:T(8,128)(2,1)S(1)}, bf16[64,256]{1,0:T(8,128)(2,1)S(1)}, u32[]{:S(2)}, u32[]{:S(2)}) collective-permute-start(bf16[64,256]{1,0:T(8,128)(2,1)S(1)} %get-tuple-element.35), channel_id=1, source_target_pairs={{0,16},{4,20},{8,24},{12,28},{16,0},{20,4},{24,8},{28,12},{1,17},{... | collective-permute-start | bytes 98312 | tf_op jit(solution)/shard_map/ppermute | solution.py:15
  70.7 4.6 %collective-permute-start.19 = (bf16[64,256]{1,0:T(8,128)(2,1)S(1)}, bf16[64,256]{1,0:T(8,128)(2,1)S(1)}, u32[]{:S(2)}, u32[]{:S(2)}) collective-permute-start(bf16[64,256]{1,0:T(8,128)(2,1)S(1)} %get-tuple-element.36), channel_id=1, source_target_pairs={{0,8},{4,12},{8,0},{12,4},{16,24},{20,28},{24,16},{28,20},{1,9},{5... | collective-permute-start | bytes 98312 | tf_op jit(solution)/shard_map/ppermute | solution.py:15
  74.7 0.6 copy-start.18
  75.0 0.6 copy-start.19
  75.3 0.6 copy-start.20

commit v2 on v1

v2 whole, which is shorter than its diff:
```python
import functools

import jax
import jax.numpy as jnp
from jax import lax
from jax.experimental import pallas as pl
from jax.experimental.pallas import tpu as pltpu
from jax.sharding import PartitionSpec as P


F32 = jnp.float32
BF16 = jnp.bfloat16
VMEM_LIMIT = 16 * 2**20
FIRST_LIMIT = int(62 * 2**20)


def send_order(cols):
    return sorted(range(1, cols), key=lambda step: (step & 1 == 0, -step))


def swap(value, axis, size, mask):
    return lax.ppermute(value, axis, [(i, i ^ mask) for i in range(size)])


def dot_t(a, b):
    return lax.dot_general(a, b, (((1,), (1,)), ((), ())), preferred_element_type=F32)


def dot_n(a, b):
    return lax.dot_general(a, b, (((1,), (0,)), ((), ())), preferred_element_type=F32)


def update(near, far, tile_refs, repeat):
    cols = len(tile_refs)
    row = lax.axis_index("row")
    col = lax.axis_index("col")
    total = None
    for step, tile_ref in enumerate(tile_refs):
        for group in range(repeat):
            place = row ^ ((col ^ step) + cols * group)
            offset = place // 2
            odd = jnp.broadcast_to(place % 2, near.shape[1:]) == 1
            segment = jnp.where(odd, far[offset], near[offset])
            term = dot_t(segment, tile_ref[group])
            total = term if total is None else total + term
    return total


def spread(solved, tile_refs, repeat, parts, keep_ref, send_ref):
    cols = len(tile_refs)
    row = lax.axis_index("row")
    col = lax.axis_index("col")
    for step, tile_ref in enumerate(tile_refs):
        for group in range(repeat):
            place = row ^ ((col ^ step) + cols * group)
            parts[place % 2, place // 2] = dot_n(solved, tile_ref[group])
    keep_ref[...] = parts[0]
    send_ref[...] = parts[1].astype(BF16)


def first_kernel(cols, pattern, rhs, dinv, tiles, out, out_b, *rest):
    levels = tiles.shape[0]
    owns, (rhs_v, dinv_v, tiles_v, sems) = rest[:levels], rest[levels:]
    pairs = [(rhs.at[0, 0], rhs_v), (dinv.at[0, 0], dinv_v)]
    pairs += [(tiles.at[level, 0], tiles_v.at[level]) for level in range(levels)]
    copies = [
        pltpu.make_async_copy(source, target, sems.at[index])
        for index, (source, target) in enumerate(pairs)
    ]
    for copy in copies:
        copy.start()
    copies[0].wait()
    copies[1].wait()
    solved = dot_t(rhs_v[...], dinv_v[...])
    out[...] = solved
    out_b[...] = solved.astype(BF16)
    for level, own in enumerate(owns):
        copies[2 + level].wait()
        for group in range(own.shape[0]):
            total = jnp.zeros(own.shape[1:], F32)
            for slot in range(tiles_v.shape[1]):
                here = (pattern[1, level, 0, slot] // cols == group).astype(F32)
                total = total + tiles_v[level, slot].astype(F32) * here
            own[group] = total.astype(BF16)


def forward_kernel(level, repeat, cols, near, far, *refs):
    tile_refs, (rhs, dinv, out, out_b) = refs[:cols], refs[cols:]
    current = rhs[level, 0].astype(F32) - update(near, far, tile_refs, repeat)
    solved = dot_t(current.astype(BF16), dinv[level, 0])
    out[...] = solved
    out_b[...] = solved.astype(BF16)


def turn_kernel(level, repeat, cols, near, far, *refs):
    tile_refs, (rhs, dinv, out, keep, send, parts) = refs[:cols], refs[cols:]
    current = rhs[level, 0].astype(F32) - update(near, far, tile_refs, repeat)
    forward = dot_t(current.astype(BF16), dinv[level, 0])
    solved = dot_n(forward.astype(BF16), dinv[level, 0])
    out[...] = solved
    spread(solved.astype(BF16), tile_refs, repeat, parts, keep, send)


def remainder(count, refs):
    total = refs[0][...].astype(F32)
    for ref in refs[1:count]:
        total = total + ref[...].astype(F32)
    return total


def backward_kernel(level, repeat, cols, count, *refs):
    arrived, tile_refs = refs[:count], refs[count : count + cols]
    forward, dinv, out, keep, send, parts = refs[count + cols :]
    rest = forward[...] - remainder(count, arrived)
    solved = dot_n(rest.astype(BF16), dinv[level, 0])
    out[...] = solved
    spread(solved.astype(BF16), tile_refs, repeat, parts, keep, send)


def last_kernel(count, upper_count, *refs):
    arrived = refs[:count]
    forward, dinv = refs[count : count + 2]
    upper = refs[count + 2 : count + 2 + upper_count]
    out = refs[-1]
    rest = forward[...] - remainder(count, arrived)
    out[0, 0] = dot_n(rest.astype(BF16), dinv[0, 0])
    for index, ref in enumerate(upper):
        out[index + 1, 0] = ref[...]


def call(kernel, outs, scratch, *args, scalars=(), space=pltpu.VMEM, limit=VMEM_LIMIT):
    return pl.pallas_call(
        kernel,
        out_shape=outs,
        in_specs=[pl.BlockSpec(memory_space=pltpu.SMEM)] * len(scalars)
        + [pl.BlockSpec(memory_space=space)] * len(args),
        out_specs=jax.tree.map(lambda _: pl.BlockSpec(memory_space=pltpu.VMEM), outs),
        scratch_shapes=scratch,
        compiler_params=pltpu.CompilerParams(vmem_limit_bytes=limit),
    )(*scalars, *args)


def per_device(rhs, dinv, tiles, pattern):
    levels, blocks, nrhs, bs = rhs.shape
    assert blocks == 1
    cols = lax.axis_size("col")
    rows = lax.axis_size("row")
    repeat = rows // cols
    chips = rows // 2

    seg = jax.ShapeDtypeStruct((nrhs, bs), F32)
    seg_b = jax.ShapeDtypeStruct((nrhs, bs), BF16)
    chip_segs = jax.ShapeDtypeStruct((chips, nrhs, bs), F32)
    chip_segs_b = jax.ShapeDtypeStruct((chips, nrhs, bs), BF16)
    parts = [pltpu.VMEM((2, chips, nrhs, bs), F32)]

    def gathered_tiles(own):
        found = [own] + [None] * (cols - 1)
        for step in send_order(cols):
            found[step] = swap(own, "col", cols, step)
        return found

    def gather(mine):
        near = [mine]
        for chip in range(1, chips):
            near.append(swap(mine, "row", rows, 2 * chip))
        near = jnp.stack(near)
        return near, swap(near, "row", rows, 1)

    def scatter(keep, send):
        total = keep + swap(send, "row", rows, 1).astype(F32)
        return [total[0]] + [
            swap(total[chip].astype(BF16), "row", rows, 2 * chip) for chip in range(1, chips)
        ]

    own_tiles = jax.ShapeDtypeStruct((repeat, bs, bs), BF16)
    forward, mine, *owns = call(
        functools.partial(first_kernel, cols),
        (seg, seg_b) + (own_tiles,) * (levels - 1),
        [
            pltpu.VMEM((nrhs, bs), BF16),
            pltpu.VMEM((bs, bs), BF16),
            pltpu.VMEM((levels - 1,) + tiles.shape[2:], BF16),
            pltpu.SemaphoreType.DMA((levels + 1,)),
        ],
        rhs, dinv, tiles, scalars=(pattern,), space=pl.ANY, limit=FIRST_LIMIT,
    )
    level_tiles = [gathered_tiles(own) for own in owns]
    forwards = [forward]
    for level in range(1, levels - 1):
        near, far = gather(mine)
        forward, mine = call(
            functools.partial(forward_kernel, level, repeat, cols),
            (seg, seg_b), [], near, far, *level_tiles[level - 1], rhs, dinv,
        )
        forwards.append(forward)
    top = levels - 1
    near, far = gather(mine)
    solved, keep, send = call(
        functools.partial(turn_kernel, top, repeat, cols),
        (seg, chip_segs, chip_segs_b), parts, near, far, *level_tiles[top - 1], rhs, dinv,
    )
    upper = [solved]
    for level in range(levels - 2, 0, -1):
        arrived = scatter(keep, send)
        solved, keep, send = call(
            functools.partial(backward_kernel, level, repeat, cols, chips),
            (seg, chip_segs, chip_segs_b), parts, *arrived, *level_tiles[level - 1], forwards[level], dinv,
        )
        upper.insert(0, solved)
    arrived = scatter(keep, send)
    return call(
        functools.partial(last_kernel, chips, len(upper)),
        jax.ShapeDtypeStruct(rhs.shape, F32), [], *arrived, forwards[0], dinv, *upper,
    )


def solution(mesh):
    in_specs = (
        P(None, "row", None, None),
        P(None, "row", None, None),
        P(None, "row", "col", None, None),
        P(None, None, "row", "col"),
    )
    out_specs = P(None, "row", None, None)

    return jax.shard_map(
        per_device, mesh=mesh, in_specs=in_specs, out_specs=out_specs, check_vma=False
    )
```

time: 78.2 us -> 62.8 us (0.80)
  local copies, waits for them, and re-layouts: 7.87 us -> 0.05 us
  Pallas kernels: 12.1 us -> 6.05 us
  other arithmetic: 2.4 us -> 0.86 us
    pallas_call x5, Pallas kernels: 12.1 us -> 6.05 us  [call(): pl.pallas_call(kernel, out_shape=outs, in_specs=[pl.BlockSpec(memory_spac...]
    squeeze x2 -> x0, local copies, waits for them, and re-layouts: 3.26 us -> none  [the longest x1 1.82 us: per_device(): dinv[top, 0]]
    unnamed x42 -> x10, local copies, waits for them, and re-layouts: 2.67 us -> 0.02 us
    another operation x2, other arithmetic: 1.98 us -> 0.07 us
    squeeze x2, local copies, waits for them, and re-layouts: 1.24 us -> 0.01 us  [scatter(): total[0]]
  transfers between devices with their start and end apart: 22 -> 22, of which waited for: 15 -> 16; matrix products, arithmetic and copies ran while one was open for 2% -> 1% of each run, Pallas kernels for 0% -> 0%
where the time goes in v2:
time: 62.8 us; the launch traced here: 62.6 us
  waiting for transfers between devices  29.1 us (46%)
  starting transfers between devices  26.4 us (42%)
  Pallas kernels  6.05 us (10%)
  other arithmetic  0.86 us (1%)
    ppermute x22, waiting for transfers between devices, swap(): return lax.ppermute(value, axis, [(i, i ^ mask) for i in range(size)])  29.1 us
    ppermute x22, starting transfers between devices, swap(): return lax.ppermute(value, axis, [(i, i ^ mask) for i in range(size)])  26.4 us
    pallas_call x5, Pallas kernels, call(): pl.pallas_call(kernel, out_shape=outs, in_specs=[pl.BlockSpec(memory_spac...  6.05 us
  transfers between devices with their start and end apart: 22, of which 16 were waited for; matrix products, arithmetic and copies ran while one was open for 1% of the time, Pallas kernels for 0%

profile of v2, /device:TPU:0, one launch (start us, length us, event | category | flops | bytes accessed | tf_op | source)
XLA Modules:
  0.0 62.6 jit_solution(7546158326021494528)
XLA Ops:
  0.0 0.0 copy-start
  0.0 0.0 copy-start.2
  0.0 2.9 %shard_map.46 = (f32[64,256]{1,0:T(8,128)}, bf16[64,256]{1,0:T(8,128)(2,1)}, bf16[2,256,256]{2,1,0:T(8,128)(2,1)}, bf16[2,256,256]{2,1,0:T(8,128)(2,1)}) custom-call(s32[2,2,1,2]{3,2,1,0:T(1,128)} %pattern.1, bf16[3,1,64,256]{3,2,1,0:T(8,128)(2,1)} %refs_4_.3, bf16[3,1,256,256]{3,2,1,0:T(8,128)(2,1)} %refs_5_.5, bf16[2,1,2,256,256]{4,3,2,1,0:T(8,128)(2,1)} %tiles.1), custom_call_target="tpu_custom_call" | custom-call | tf_op jit(solution)/shard_map/pallas_call | solution.py:132
  2.9 0.0 copy-start.1
  2.9 5.1 %collective-permute-start.2 = (bf16[64,256]{1,0:T(8,128)(2,1)}, bf16[64,256]{1,0:T(8,128)(2,1)S(1)}, u32[]{:S(2)}, u32[]{:S(2)}) collective-permute-start(bf16[64,256]{1,0:T(8,128)(2,1)} %get-tuple-element.17), channel_id=1, source_target_pairs={{0,24},{4,28},{8,16},{12,20},{16,8},{20,12},{24,0},{28,4},{1,25},{... | collective-permute-start | bytes 98312 | tf_op jit(solution)/shard_map/ppermute | solution.py:22
  8.0 0.0 collective-permute-start.1
  8.0 0.6 %collective-permute-start = (bf16[64,256]{1,0:T(8,128)(2,1)}, bf16[64,256]{1,0:T(8,128)(2,1)S(1)}, u32[]{:S(2)}, u32[]{:S(2)}) collective-permute-start(bf16[64,256]{1,0:T(8,128)(2,1)} %get-tuple-element.17), channel_id=1, source_target_pairs={{0,8},{4,12},{8,0},{12,4},{16,24},{20,28},{24,16},{28,20},{1,9},{5... | collective-permute-start | bytes 98312 | tf_op jit(solution)/shard_map/ppermute | solution.py:22
  8.7 2.6 %collective-permute-start.6 = (bf16[2,256,256]{2,1,0:T(8,128)(2,1)}, bf16[2,256,256]{2,1,0:T(8,128)(2,1)S(1)}, u32[]{:S(2)}, u32[]{:S(2)}) collective-permute-start(bf16[2,256,256]{2,1,0:T(8,128)(2,1)} %get-tuple-element.18.refs_0_.refs_4_), channel_id=1, source_target_pairs={{0,3},{1,2},{2,1},{3,0},{4,7},{5,6},{6,5},{7,4},{8,11},{9,10},{10,... | collective-permute-start | bytes 786440 | tf_op jit(solution)/shard_map/ppermute | solution.py:22
  11.3 0.5 collective-permute-start.5
  11.8 0.0 collective-permute-done.2
  11.8 0.4 collective-permute-start.4
  12.2 0.9 %collective-permute-done.1 = bf16[64,256]{1,0:T(8,128)(2,1)S(1)} collective-permute-done((bf16[64,256]{1,0:T(8,128)(2,1)}, bf16[64,256]{1,0:T(8,128)(2,1)S(1)}, u32[]{:S(2)}, u32[]{:S(2)}) %collective-permute-start.1) | collective-permute-done | bytes 32800 | tf_op jit(solution)/shard_map/ppermute | solution.py:22
  13.1 0.0 collective-permute-done
  13.1 0.8 %pad_maximum_fusion.near = bf16[4,64,256]{2,1,0:T(8,128)(2,1)S(1)} fusion(bf16[1,64,256]{2,1,0:T(8,128)(2,1)S(1)} %bitcast.26, bf16[1,64,256]{2,1,0:T(8,128)(2,1)S(1)} %bitcast.28, bf16[1,64,256]{2,1,0:T(8,128)(2,1)S(1)} %bitcast.30, bf16[1,64,256]{2,1,0:T(8,128)(2,1)} %bitcast.25), kind=kLoop, calls=%fused_computation.2 | loop fusion | flops 196608 | bytes 262144 | tf_op jit(solution)/shard_map/stack | solution.py:167
  13.8 0.0 copy-start.3
  13.9 0.1 collective-permute-start.3
  13.9 1.3 %collective-permute-done.3.far = bf16[4,64,256]{2,1,0:T(8,128)(2,1)S(1)} collective-permute-done((bf16[4,64,256]{2,1,0:T(8,128)(2,1)S(1)}, bf16[4,64,256]{2,1,0:T(8,128)(2,1)S(1)}, u32[]{:S(2)}, u32[]{:S(2)}) %collective-permute-start.3) | collective-permute-done | bytes 131104 | tf_op jit(solution)/shard_map/ppermute | solution.py:22
  15.3 3.7 %collective-permute-done.6.refs_3_.refs_7_ = bf16[2,256,256]{2,1,0:T(8,128)(2,1)S(1)} collective-permute-done((bf16[2,256,256]{2,1,0:T(8,128)(2,1)}, bf16[2,256,256]{2,1,0:T(8,128)(2,1)S(1)}, u32[]{:S(2)}, u32[]{:S(2)}) %collective-permute-start.6) | collective-permute-done | bytes 262176 | tf_op jit(solution)/shard_map/ppermute | solution.py:22
  19.0 3.9 %collective-permute-done.5.refs_2_.refs_6_ = bf16[2,256,256]{2,1,0:T(8,128)(2,1)S(1)} collective-permute-done((bf16[2,256,256]{2,1,0:T(8,128)(2,1)}, bf16[2,256,256]{2,1,0:T(8,128)(2,1)S(1)}, u32[]{:S(2)}, u32[]{:S(2)}) %collective-permute-start.5) | collective-permute-done | bytes 262176 | tf_op jit(solution)/shard_map/ppermute | solution.py:22
  22.9 0.1 collective-permute-done.4.refs_1_.refs_5_
  23.0 0.0 copy-done
  23.0 0.0 copy-done.2
  23.0 0.0 copy-done.1
  23.0 0.6 shard_map.47
  23.6 3.5 %collective-permute-start.9 = (bf16[64,256]{1,0:T(8,128)(2,1)S(1)}, bf16[64,256]{1,0:T(8,128)(2,1)S(1)}, u32[]{:S(2)}, u32[]{:S(2)}) collective-permute-start(bf16[64,256]{1,0:T(8,128)(2,1)S(1)} %get-tuple-element.19), channel_id=1, source_target_pairs={{0,24},{4,28},{8,16},{12,20},{16,8},{20,12},{24,0},{28,4},{1,25},{... | collective-permute-start | bytes 98312 | tf_op jit(solution)/shard_map/ppermute | solution.py:22
  27.2 0.0 collective-permute-start.8
  27.2 0.9 %collective-permute-start.7 = (bf16[64,256]{1,0:T(8,128)(2,1)S(1)}, bf16[64,256]{1,0:T(8,128)(2,1)S(1)}, u32[]{:S(2)}, u32[]{:S(2)}) collective-permute-start(bf16[64,256]{1,0:T(8,128)(2,1)S(1)} %get-tuple-element.19), channel_id=1, source_target_pairs={{0,8},{4,12},{8,0},{12,4},{16,24},{20,28},{24,16},{28,20},{1,9},{5... | collective-permute-start | bytes 98312 | tf_op jit(solution)/shard_map/ppermute | solution.py:22
  28.1 0.0 copy-done.3
  28.1 1.7 %collective-permute-start.13 = (bf16[2,256,256]{2,1,0:T(8,128)(2,1)S(1)}, bf16[2,256,256]{2,1,0:T(8,128)(2,1)S(1)}, u32[]{:S(2)}, u32[]{:S(2)}) collective-permute-start(bf16[2,256,256]{2,1,0:T(8,128)(2,1)S(1)} %copy-done.3), channel_id=1, source_target_pairs={{0,3},{1,2},{2,1},{3,0},{4,7},{5,6},{6,5},{7,4},{8,11},{9,10},{10,... | collective-permute-start | bytes 786440 | tf_op jit(solution)/shard_map/ppermute | solution.py:22
  29.7 1.3 %collective-permute-start.12 = (bf16[2,256,256]{2,1,0:T(8,128)(2,1)S(1)}, bf16[2,256,256]{2,1,0:T(8,128)(2,1)S(1)}, u32[]{:S(2)}, u32[]{:S(2)}) collective-permute-start(bf16[2,256,256]{2,1,0:T(8,128)(2,1)S(1)} %copy-done.3), channel_id=1, source_target_pairs={{0,2},{1,3},{2,0},{3,1},{4,6},{5,7},{6,4},{7,5},{8,10},{9,11},{10,... | collective-permute-start | bytes 786440 | tf_op jit(solution)/shard_map/ppermute | solution.py:22
  31.0 0.0 collective-permute-done.9
  31.0 0.5 collective-permute-start.11
  31.6 0.4 collective-permute-done.8
  32.0 0.0 collective-permute-done.7
  32.0 0.1 collective-permute-start.10
  32.1 6.1 %collective-permute-done.13.refs_3_ = bf16[2,256,256]{2,1,0:T(8,128)(2,1)S(1)} collective-permute-done((bf16[2,256,256]{2,1,0:T(8,128)(2,1)S(1)}, bf16[2,256,256]{2,1,0:T(8,128)(2,1)S(1)}, u32[]{:S(2)}, u32[]{:S(2)}) %collective-permute-start.13) | collective-permute-done | bytes 262176 | tf_op jit(solution)/shard_map/ppermute | solution.py:22
  38.2 3.7 %collective-permute-done.12.refs_2_ = bf16[2,256,256]{2,1,0:T(8,128)(2,1)S(1)} collective-permute-done((bf16[2,256,256]{2,1,0:T(8,128)(2,1)S(1)}, bf16[2,256,256]{2,1,0:T(8,128)(2,1)S(1)}, u32[]{:S(2)}, u32[]{:S(2)}) %collective-permute-start.12) | collective-permute-done | bytes 262176 | tf_op jit(solution)/shard_map/ppermute | solution.py:22
  41.9 0.1 collective-permute-done.11.refs_1_
  42.0 0.0 collective-permute-done.10.far
  42.0 1.2 %shard_map.48 = (f32[64,256]{1,0:T(8,128)S(1)}, f32[4,64,256]{2,1,0:T(8,128)S(1)}, bf16[4,64,256]{2,1,0:T(8,128)(2,1)S(1)}) custom-call(bf16[4,64,256]{2,1,0:T(8,128)(2,1)S(1)} %pad_maximum_fusion.1.near, bf16[4,64,256]{2,1,0:T(8,128)(2,1)S(1)} %collective-permute-done.10.far, bf16[2,256,256]{2,1,0:T(8,128)(2,1)S(1)} %copy-done.3, ...), custom_call_target="tpu_custom_call" | custom-call | tf_op jit(solution)/shard_map/pallas_call | solution.py:132
  43.3 0.1 collective-permute-start.14
  43.3 1.3 %collective-permute-done.14 = bf16[4,64,256]{2,1,0:T(8,128)(2,1)S(1)} collective-permute-done((bf16[4,64,256]{2,1,0:T(8,128)(2,1)S(1)}, bf16[4,64,256]{2,1,0:T(8,128)(2,1)S(1)}, u32[]{:S(2)}, u32[]{:S(2)}) %collective-permute-start.14) | collective-permute-done | bytes 131104 | tf_op jit(solution)/shard_map/ppermute | solution.py:22
  44.7 3.5 %collective-permute-start.17 = (bf16[64,256]{1,0:T(8,128)(2,1)S(1)}, bf16[64,256]{1,0:T(8,128)(2,1)S(1)}, u32[]{:S(2)}, u32[]{:S(2)}) collective-permute-start(bf16[64,256]{1,0:T(8,128)(2,1)S(1)} %get-tuple-element.36), channel_id=1, source_target_pairs={{0,24},{4,28},{8,16},{12,20},{16,8},{20,12},{24,0},{28,4},{1,25},{... | collective-permute-start | bytes 98312 | tf_op jit(solution)/shard_map/ppermute | solution.py:22
  48.3 0.0 collective-permute-start.16
  48.3 0.9 %collective-permute-start.15 = (bf16[64,256]{1,0:T(8,128)(2,1)S(1)}, bf16[64,256]{1,0:T(8,128)(2,1)S(1)}, u32[]{:S(2)}, u32[]{:S(2)}) collective-permute-start(bf16[64,256]{1,0:T(8,128)(2,1)S(1)} %get-tuple-element.38), channel_id=1, source_target_pairs={{0,8},{4,12},{8,0},{12,4},{16,24},{20,28},{24,16},{28,20},{1,9},{5... | collective-permute-start | bytes 98312 | tf_op jit(solution)/shard_map/ppermute | solution.py:22
  49.2 1.4 %collective-permute-done.17.refs_3_ = bf16[64,256]{1,0:T(8,128)(2,1)S(1)} collective-permute-done((bf16[64,256]{1,0:T(8,128)(2,1)S(1)}, bf16[64,256]{1,0:T(8,128)(2,1)S(1)}, u32[]{:S(2)}, u32[]{:S(2)}) %collective-permute-start.17) | collective-permute-done | bytes 32800 | tf_op jit(solution)/shard_map/ppermute | solution.py:22
  50.6 2.5 %collective-permute-done.16.refs_2_ = bf16[64,256]{1,0:T(8,128)(2,1)S(1)} collective-permute-done((bf16[64,256]{1,0:T(8,128)(2,1)S(1)}, bf16[64,256]{1,0:T(8,128)(2,1)S(1)}, u32[]{:S(2)}, u32[]{:S(2)}) %collective-permute-start.16) | collective-permute-done | bytes 32800 | tf_op jit(solution)/shard_map/ppermute | solution.py:22
  53.1 0.0 collective-permute-done.15.refs_1_
  53.1 0.5 shard_map.49
  53.6 0.1 collective-permute-start.18
  53.6 1.3 %collective-permute-done.18 = bf16[4,64,256]{2,1,0:T(8,128)(2,1)S(1)} collective-permute-done((bf16[4,64,256]{2,1,0:T(8,128)(2,1)S(1)}, bf16[4,64,256]{2,1,0:T(8,128)(2,1)S(1)}, u32[]{:S(2)}, u32[]{:S(2)}) %collective-permute-start.18) | collective-permute-done | bytes 131104 | tf_op jit(solution)/shard_map/ppermute | solution.py:22
  55.0 1.5 %collective-permute-start.21 = (bf16[64,256]{1,0:T(8,128)(2,1)S(1)}, bf16[64,256]{1,0:T(8,128)(2,1)S(1)}, u32[]{:S(2)}, u32[]{:S(2)}) collective-permute-start(bf16[64,256]{1,0:T(8,128)(2,1)S(1)} %get-tuple-element.33), channel_id=1, source_target_pairs={{0,24},{4,28},{8,16},{12,20},{16,8},{20,12},{24,0},{28,4},{1,25},{... | collective-permute-start | bytes 98312 | tf_op jit(solution)/shard_map/ppermute | solution.py:22
  56.6 0.6 collective-permute-start.20
  57.2 2.3 %collective-permute-start.19 = (bf16[64,256]{1,0:T(8,128)(2,1)S(1)}, bf16[64,256]{1,0:T(8,128)(2,1)S(1)}, u32[]{:S(2)}, u32[]{:S(2)}) collective-permute-start(bf16[64,256]{1,0:T(8,128)(2,1)S(1)} %get-tuple-element.35), channel_id=1, source_target_pairs={{0,8},{4,12},{8,0},{12,4},{16,24},{20,28},{24,16},{28,20},{1,9},{5... | collective-permute-start | bytes 98312 | tf_op jit(solution)/shard_map/ppermute | solution.py:22
  59.5 0.0 copy-start.4
  59.5 1.6 %collective-permute-done.21.refs_3_ = bf16[64,256]{1,0:T(8,128)(2,1)S(1)} collective-permute-done((bf16[64,256]{1,0:T(8,128)(2,1)S(1)}, bf16[64,256]{1,0:T(8,128)(2,1)S(1)}, u32[]{:S(2)}, u32[]{:S(2)}) %collective-permute-start.21) | collective-permute-done | bytes 32800 | tf_op jit(solution)/shard_map/ppermute | solution.py:22
  61.1 0.4 collective-permute-done.20.refs_2_
  61.5 0.3 collective-permute-done.19.refs_1_
  61.8 0.0 copy-done.4
  61.8 0.8 %shard_map.50 = f32[3,1,64,256]{3,2,1,0:T(8,128)} custom-call(f32[64,256]{1,0:T(8,128)S(1)} %slice_bitcast_fusion.refs_0_, bf16[64,256]{1,0:T(8,128)(2,1)S(1)} %collective-permute-done.19.refs_1_, bf16[64,256]{1,0:T(8,128)(2,1)S(1)} %collective-permute-done.20.refs_2_, bf16[64,256]{1,0:T(8,128)(2,1)S(1)} %collective-permute-done.21.refs_3_, ...), custom_call_target="tpu_custom_call" | custom-call | tf_op jit(solution)/shard_map/pallas_call | solution.py:132
  (7 shorter events, 0.1 us)
Async XLA Ops:
  0.0 23.0 %copy-start = (bf16[3,1,256,256]{3,2,1,0:T(8,128)(2,1)S(1)}, bf16[3,1,256,256]{3,2,1,0:T(8,128)(2,1)}, u32[]{:S(2)}) copy-start(bf16[3,1,256,256]{3,2,1,0:T(8,128)(2,1)} %refs_5_.5) | copy-start | bytes 1179652
  0.0 23.0 %copy-start.2 = (bf16[3,1,64,256]{3,2,1,0:T(8,128)(2,1)S(1)}, bf16[3,1,64,256]{3,2,1,0:T(8,128)(2,1)}, u32[]{:S(2)}) copy-start(bf16[3,1,64,256]{3,2,1,0:T(8,128)(2,1)} %refs_4_.3) | copy-start | bytes 294916
  2.9 20.1 %copy-start.1 = (bf16[2,256,256]{2,1,0:T(8,128)(2,1)S(1)}, bf16[2,256,256]{2,1,0:T(8,128)(2,1)}, u32[]{:S(2)}) copy-start(bf16[2,256,256]{2,1,0:T(8,128)(2,1)} %get-tuple-element.18.refs_0_.refs_4_) | copy-start | bytes 786436
  2.9 8.9 %collective-permute-start.2 = (bf16[64,256]{1,0:T(8,128)(2,1)}, bf16[64,256]{1,0:T(8,128)(2,1)S(1)}, u32[]{:S(2)}, u32[]{:S(2)}) collective-permute-start(bf16[64,256]{1,0:T(8,128)(2,1)} %get-tuple-element.17), channel_id=1, source_target_pairs={{0,24},{4,28},{8,16},{12,20},{16,8},{20,12},{24,0},{28,4},{1,25},{... | collective-permute-start | bytes 98312 | tf_op jit(solution)/shard_map/ppermute | solution.py:22
  8.0 5.0 %collective-permute-start.1 = (bf16[64,256]{1,0:T(8,128)(2,1)}, bf16[64,256]{1,0:T(8,128)(2,1)S(1)}, u32[]{:S(2)}, u32[]{:S(2)}) collective-permute-start(bf16[64,256]{1,0:T(8,128)(2,1)} %get-tuple-element.17), channel_id=1, source_target_pairs={{0,16},{4,20},{8,24},{12,28},{16,0},{20,4},{24,8},{28,12},{1,17},{... | collective-permute-start | bytes 98312 | tf_op jit(solution)/shard_map/ppermute | solution.py:22
  8.0 5.0 %collective-permute-start = (bf16[64,256]{1,0:T(8,128)(2,1)}, bf16[64,256]{1,0:T(8,128)(2,1)S(1)}, u32[]{:S(2)}, u32[]{:S(2)}) collective-permute-start(bf16[64,256]{1,0:T(8,128)(2,1)} %get-tuple-element.17), channel_id=1, source_target_pairs={{0,8},{4,12},{8,0},{12,4},{16,24},{20,28},{24,16},{28,20},{1,9},{5... | collective-permute-start | bytes 98312 | tf_op jit(solution)/shard_map/ppermute | solution.py:22
  8.7 10.3 %collective-permute-start.6 = (bf16[2,256,256]{2,1,0:T(8,128)(2,1)}, bf16[2,256,256]{2,1,0:T(8,128)(2,1)S(1)}, u32[]{:S(2)}, u32[]{:S(2)}) collective-permute-start(bf16[2,256,256]{2,1,0:T(8,128)(2,1)} %get-tuple-element.18.refs_0_.refs_4_), channel_id=1, source_target_pairs={{0,3},{1,2},{2,1},{3,0},{4,7},{5,6},{6,5},{7,4},{8,11},{9,10},{10,... | collective-permute-start | bytes 786440 | tf_op jit(solution)/shard_map/ppermute | solution.py:22
  11.3 11.6 %collective-permute-start.5 = (bf16[2,256,256]{2,1,0:T(8,128)(2,1)}, bf16[2,256,256]{2,1,0:T(8,128)(2,1)S(1)}, u32[]{:S(2)}, u32[]{:S(2)}) collective-permute-start(bf16[2,256,256]{2,1,0:T(8,128)(2,1)} %get-tuple-element.18.refs_0_.refs_4_), channel_id=1, source_target_pairs={{0,2},{1,3},{2,0},{3,1},{4,6},{5,7},{6,4},{7,5},{8,10},{9,11},{10,... | collective-permute-start | bytes 786440 | tf_op jit(solution)/shard_map/ppermute | solution.py:22
  11.8 11.2 %collective-permute-start.4 = (bf16[2,256,256]{2,1,0:T(8,128)(2,1)}, bf16[2,256,256]{2,1,0:T(8,128)(2,1)S(1)}, u32[]{:S(2)}, u32[]{:S(2)}) collective-permute-start(bf16[2,256,256]{2,1,0:T(8,128)(2,1)} %get-tuple-element.18.refs_0_.refs_4_), channel_id=1, source_target_pairs={{0,1},{1,0},{2,3},{3,2},{4,5},{5,4},{6,7},{7,6},{8,9},{9,8},{10,11... | collective-permute-start | bytes 786440 | tf_op jit(solution)/shard_map/ppermute | solution.py:22
  13.8 14.2 %copy-start.3 = (bf16[2,256,256]{2,1,0:T(8,128)(2,1)S(1)}, bf16[2,256,256]{2,1,0:T(8,128)(2,1)}, u32[]{:S(2)}) copy-start(bf16[2,256,256]{2,1,0:T(8,128)(2,1)} %get-tuple-element.20.refs_0_) | copy-start | bytes 786436
  13.9 1.4 %collective-permute-start.3 = (bf16[4,64,256]{2,1,0:T(8,128)(2,1)S(1)}, bf16[4,64,256]{2,1,0:T(8,128)(2,1)S(1)}, u32[]{:S(2)}, u32[]{:S(2)}) collective-permute-start(bf16[4,64,256]{2,1,0:T(8,128)(2,1)S(1)} %pad_maximum_fusion.near), channel_id=1, source_target_pairs={{0,4},{4,0},{8,12},{12,8},{16,20},{20,16},{24,28},{28,24},{1,5},{5... | collective-permute-start | bytes 393224 | tf_op jit(solution)/shard_map/ppermute | solution.py:22
  23.6 7.4 %collective-permute-start.9 = (bf16[64,256]{1,0:T(8,128)(2,1)S(1)}, bf16[64,256]{1,0:T(8,128)(2,1)S(1)}, u32[]{:S(2)}, u32[]{:S(2)}) collective-permute-start(bf16[64,256]{1,0:T(8,128)(2,1)S(1)} %get-tuple-element.19), channel_id=1, source_target_pairs={{0,24},{4,28},{8,16},{12,20},{16,8},{20,12},{24,0},{28,4},{1,25},{... | collective-permute-start | bytes 98312 | tf_op jit(solution)/shard_map/ppermute | solution.py:22
  27.2 4.8 %collective-permute-start.8 = (bf16[64,256]{1,0:T(8,128)(2,1)S(1)}, bf16[64,256]{1,0:T(8,128)(2,1)S(1)}, u32[]{:S(2)}, u32[]{:S(2)}) collective-permute-start(bf16[64,256]{1,0:T(8,128)(2,1)S(1)} %get-tuple-element.19), channel_id=1, source_target_pairs={{0,16},{4,20},{8,24},{12,28},{16,0},{20,4},{24,8},{28,12},{1,17},{... | collective-permute-start | bytes 98312 | tf_op jit(solution)/shard_map/ppermute | solution.py:22
  27.2 4.8 %collective-permute-start.7 = (bf16[64,256]{1,0:T(8,128)(2,1)S(1)}, bf16[64,256]{1,0:T(8,128)(2,1)S(1)}, u32[]{:S(2)}, u32[]{:S(2)}) collective-permute-start(bf16[64,256]{1,0:T(8,128)(2,1)S(1)} %get-tuple-element.19), channel_id=1, source_target_pairs={{0,8},{4,12},{8,0},{12,4},{16,24},{20,28},{24,16},{28,20},{1,9},{5... | collective-permute-start | bytes 98312 | tf_op jit(solution)/shard_map/ppermute | solution.py:22
  28.1 10.1 %collective-permute-start.13 = (bf16[2,256,256]{2,1,0:T(8,128)(2,1)S(1)}, bf16[2,256,256]{2,1,0:T(8,128)(2,1)S(1)}, u32[]{:S(2)}, u32[]{:S(2)}) collective-permute-start(bf16[2,256,256]{2,1,0:T(8,128)(2,1)S(1)} %copy-done.3), channel_id=1, source_target_pairs={{0,3},{1,2},{2,1},{3,0},{4,7},{5,6},{6,5},{7,4},{8,11},{9,10},{10,... | collective-permute-start | bytes 786440 | tf_op jit(solution)/shard_map/ppermute | solution.py:22
  29.7 12.2 %collective-permute-start.12 = (bf16[2,256,256]{2,1,0:T(8,128)(2,1)S(1)}, bf16[2,256,256]{2,1,0:T(8,128)(2,1)S(1)}, u32[]{:S(2)}, u32[]{:S(2)}) collective-permute-start(bf16[2,256,256]{2,1,0:T(8,128)(2,1)S(1)} %copy-done.3), channel_id=1, source_target_pairs={{0,2},{1,3},{2,0},{3,1},{4,6},{5,7},{6,4},{7,5},{8,10},{9,11},{10,... | collective-permute-start | bytes 786440 | tf_op jit(solution)/shard_map/ppermute | solution.py:22
  31.0 11.0 %collective-permute-start.11 = (bf16[2,256,256]{2,1,0:T(8,128)(2,1)S(1)}, bf16[2,256,256]{2,1,0:T(8,128)(2,1)S(1)}, u32[]{:S(2)}, u32[]{:S(2)}) collective-permute-start(bf16[2,256,256]{2,1,0:T(8,128)(2,1)S(1)} %copy-done.3), channel_id=1, source_target_pairs={{0,1},{1,0},{2,3},{3,2},{4,5},{5,4},{6,7},{7,6},{8,9},{9,8},{10,11... | collective-permute-start | bytes 786440 | tf_op jit(solution)/shard_map/ppermute | solution.py:22
  32.0 10.0 %collective-permute-start.10 = (bf16[4,64,256]{2,1,0:T(8,128)(2,1)S(1)}, bf16[4,64,256]{2,1,0:T(8,128)(2,1)S(1)}, u32[]{:S(2)}, u32[]{:S(2)}) collective-permute-start(bf16[4,64,256]{2,1,0:T(8,128)(2,1)S(1)} %pad_maximum_fusion.1.near), channel_id=1, source_target_pairs={{0,4},{4,0},{8,12},{12,8},{16,20},{20,16},{24,28},{28,24},{1,5},{5... | collective-permute-start | bytes 393224 | tf_op jit(solution)/shard_map/ppermute | solution.py:22
  43.3 1.4 %collective-permute-start.14 = (bf16[4,64,256]{2,1,0:T(8,128)(2,1)S(1)}, bf16[4,64,256]{2,1,0:T(8,128)(2,1)S(1)}, u32[]{:S(2)}, u32[]{:S(2)}) collective-permute-start(bf16[4,64,256]{2,1,0:T(8,128)(2,1)S(1)} %get-tuple-element.22), channel_id=1, source_target_pairs={{0,4},{4,0},{8,12},{12,8},{16,20},{20,16},{24,28},{28,24},{1,5},{5... | collective-permute-start | bytes 393224 | tf_op jit(solution)/shard_map/ppermute | solution.py:22
  44.7 5.8 %collective-permute-start.17 = (bf16[64,256]{1,0:T(8,128)(2,1)S(1)}, bf16[64,256]{1,0:T(8,128)(2,1)S(1)}, u32[]{:S(2)}, u32[]{:S(2)}) collective-permute-start(bf16[64,256]{1,0:T(8,128)(2,1)S(1)} %get-tuple-element.36), channel_id=1, source_target_pairs={{0,24},{4,28},{8,16},{12,20},{16,8},{20,12},{24,0},{28,4},{1,25},{... | collective-permute-start | bytes 98312 | tf_op jit(solution)/shard_map/ppermute | solution.py:22
  48.3 4.8 %collective-permute-start.16 = (bf16[64,256]{1,0:T(8,128)(2,1)S(1)}, bf16[64,256]{1,0:T(8,128)(2,1)S(1)}, u32[]{:S(2)}, u32[]{:S(2)}) collective-permute-start(bf16[64,256]{1,0:T(8,128)(2,1)S(1)} %get-tuple-element.37), channel_id=1, source_target_pairs={{0,16},{4,20},{8,24},{12,28},{16,0},{20,4},{24,8},{28,12},{1,17},{... | collective-permute-start | bytes 98312 | tf_op jit(solution)/shard_map/ppermute | solution.py:22
  48.3 4.8 %collective-permute-start.15 = (bf16[64,256]{1,0:T(8,128)(2,1)S(1)}, bf16[64,256]{1,0:T(8,128)(2,1)S(1)}, u32[]{:S(2)}, u32[]{:S(2)}) collective-permute-start(bf16[64,256]{1,0:T(8,128)(2,1)S(1)} %get-tuple-element.38), channel_id=1, source_target_pairs={{0,8},{4,12},{8,0},{12,4},{16,24},{20,28},{24,16},{28,20},{1,9},{5... | collective-permute-start | bytes 98312 | tf_op jit(solution)/shard_map/ppermute | solution.py:22
  53.6 1.4 %collective-permute-start.18 = (bf16[4,64,256]{2,1,0:T(8,128)(2,1)S(1)}, bf16[4,64,256]{2,1,0:T(8,128)(2,1)S(1)}, u32[]{:S(2)}, u32[]{:S(2)}) collective-permute-start(bf16[4,64,256]{2,1,0:T(8,128)(2,1)S(1)} %get-tuple-element.25), channel_id=1, source_target_pairs={{0,4},{4,0},{8,12},{12,8},{16,20},{20,16},{24,28},{28,24},{1,5},{5... | collective-permute-start | bytes 393224 | tf_op jit(solution)/shard_map/ppermute | solution.py:22
  55.0 6.1 %collective-permute-start.21 = (bf16[64,256]{1,0:T(8,128)(2,1)S(1)}, bf16[64,256]{1,0:T(8,128)(2,1)S(1)}, u32[]{:S(2)}, u32[]{:S(2)}) collective-permute-start(bf16[64,256]{1,0:T(8,128)(2,1)S(1)} %get-tuple-element.33), channel_id=1, source_target_pairs={{0,24},{4,28},{8,16},{12,20},{16,8},{20,12},{24,0},{28,4},{1,25},{... | collective-permute-start | bytes 98312 | tf_op jit(solution)/shard_map/ppermute | solution.py:22
  56.6 4.9 %collective-permute-start.20 = (bf16[64,256]{1,0:T(8,128)(2,1)S(1)}, bf16[64,256]{1,0:T(8,128)(2,1)S(1)}, u32[]{:S(2)}, u32[]{:S(2)}) collective-permute-start(bf16[64,256]{1,0:T(8,128)(2,1)S(1)} %get-tuple-element.34), channel_id=1, source_target_pairs={{0,16},{4,20},{8,24},{12,28},{16,0},{20,4},{24,8},{28,12},{1,17},{... | collective-permute-start | bytes 98312 | tf_op jit(solution)/shard_map/ppermute | solution.py:22
  57.2 4.6 %collective-permute-start.19 = (bf16[64,256]{1,0:T(8,128)(2,1)S(1)}, bf16[64,256]{1,0:T(8,128)(2,1)S(1)}, u32[]{:S(2)}, u32[]{:S(2)}) collective-permute-start(bf16[64,256]{1,0:T(8,128)(2,1)S(1)} %get-tuple-element.35), channel_id=1, source_target_pairs={{0,8},{4,12},{8,0},{12,4},{16,24},{20,28},{24,16},{28,20},{1,9},{5... | collective-permute-start | bytes 98312 | tf_op jit(solution)/shard_map/ppermute | solution.py:22
  59.5 2.3 %copy-start.4 = (f32[64,256]{1,0:T(8,128)S(1)}, f32[64,256]{1,0:T(8,128)}, u32[]{:S(2)}) copy-start(f32[64,256]{1,0:T(8,128)} %get-tuple-element.26.refs_4_) | copy-start | bytes 196612

commit v3 on v1

v3 whole, which is shorter than its diff:
```python
import functools

import jax
import jax.numpy as jnp
from jax import lax
from jax.experimental import pallas as pl
from jax.experimental.pallas import tpu as pltpu
from jax.sharding import PartitionSpec as P


F32 = jnp.float32
BF16 = jnp.bfloat16
VMEM_LIMIT = 16 * 2**20


def send_order(cols):
    return sorted(range(1, cols), key=lambda step: -step)


def swap(value, axis, size, mask):
    return lax.ppermute(value, axis, [(i, i ^ mask) for i in range(size)])


def dot_t(a, b):
    return lax.dot_general(a, b, (((1,), (1,)), ((), ())), preferred_element_type=F32)


def dot_n(a, b):
    return lax.dot_general(a, b, (((1,), (0,)), ((), ())), preferred_element_type=F32)


def update(near, far, tile_refs, steps, repeat, cols):
    row = lax.axis_index("row")
    col = lax.axis_index("col")
    total = None
    for step, tile_ref in zip(steps, tile_refs):
        for group in range(repeat):
            place = row ^ ((col ^ step) + cols * group)
            odd = jnp.broadcast_to(place % 2, near.shape[1:]) == 1
            segment = jnp.where(odd, far[place // 2], near[place // 2])
            term = dot_t(segment, tile_ref[group])
            total = term if total is None else total + term
    return total


def pick(tile_refs, pair, group, first):
    even, odd = tile_refs[2 * pair], tile_refs[2 * pair + 1]
    odd_first = jnp.broadcast_to(first, even.shape[1:]) == 1
    return jnp.where(odd_first, odd[group], even[group])


def spread(solved, parity, tile_refs, repeat, out):
    cols = len(tile_refs)
    row = lax.axis_index("row")
    col = lax.axis_index("col")
    first = (row + col + parity) % 2
    for pair in range(cols // 2):
        for group in range(repeat):
            place = row ^ ((col ^ (2 * pair + first)) + cols * group)
            tile = pick(tile_refs, pair, group, first)
            out[place // 2] = dot_n(solved, tile).astype(out.dtype)


def first_kernel(rhs, dinv, out, out_b):
    solved = dot_t(rhs[0, 0], dinv[0, 0])
    out[...] = solved
    out_b[...] = solved.astype(BF16)


def early_kernel(repeat, cols, steps, near, far, *refs):
    refs[-1][...] = update(near, far, refs[:-1], steps, repeat, cols)


def forward_kernel(level, repeat, cols, steps, part, near, far, *refs):
    tile_refs, (rhs, dinv, out, out_b) = refs[: len(steps)], refs[len(steps) :]
    late = update(near, far, tile_refs, steps, repeat, cols)
    current = rhs[level, 0].astype(F32) - (part[...] + late)
    solved = dot_t(current.astype(BF16), dinv[level, 0])
    out[...] = solved
    out_b[...] = solved.astype(BF16)


def turn_kernel(level, repeat, cols, steps, part, near, far, *refs):
    tile_refs, (rhs, dinv, out, out_b, send) = refs[:cols], refs[cols:]
    late = update(near, far, [tile_refs[step] for step in steps], steps, repeat, cols)
    current = rhs[level, 0].astype(F32) - (part[...] + late)
    forward = dot_t(current.astype(BF16), dinv[level, 0])
    solved = dot_n(forward.astype(BF16), dinv[level, 0])
    out[...] = solved
    solved = solved.astype(BF16)
    out_b[...] = solved
    spread(solved, 1, tile_refs, repeat, send)


def keep_kernel(repeat, solved, *refs):
    spread(solved[...], 0, refs[:-1], repeat, refs[-1])


def remainder(count, refs):
    total = refs[0][...].astype(F32)
    for ref in refs[1:count]:
        total = total + ref[...].astype(F32)
    return total


def backward_kernel(level, repeat, cols, count, *refs):
    arrived, tile_refs = refs[:count], refs[count : count + cols]
    forward, dinv, out, out_b, send = refs[count + cols :]
    rest = forward[...] - remainder(count, arrived)
    solved = dot_n(rest.astype(BF16), dinv[level, 0])
    out[...] = solved
    solved = solved.astype(BF16)
    out_b[...] = solved
    spread(solved, 1, tile_refs, repeat, send)


def last_kernel(count, upper_count, *refs):
    arrived = refs[:count]
    forward, dinv = refs[count : count + 2]
    upper = refs[count + 2 : count + 2 + upper_count]
    out = refs[-1]
    rest = forward[...] - remainder(count, arrived)
    out[0, 0] = dot_n(rest.astype(BF16), dinv[0, 0])
    for index, ref in enumerate(upper):
        out[index + 1, 0] = ref[...]


def call(kernel, outs, scratch, *args):
    return pl.pallas_call(
        kernel,
        out_shape=outs,
        in_specs=[pl.BlockSpec(memory_space=pltpu.VMEM)] * len(args),
        out_specs=jax.tree.map(lambda _: pl.BlockSpec(memory_space=pltpu.VMEM), outs),
        scratch_shapes=scratch,
        compiler_params=pltpu.CompilerParams(vmem_limit_bytes=VMEM_LIMIT),
    )(*args)


def per_device(rhs, dinv, tiles, pattern):
    levels, blocks, nrhs, bs = rhs.shape
    assert blocks == 1
    cols = lax.axis_size("col")
    rows = lax.axis_size("row")
    repeat = rows // cols
    chips = rows // 2

    seg = jax.ShapeDtypeStruct((nrhs, bs), F32)
    seg_b = jax.ShapeDtypeStruct((nrhs, bs), BF16)
    chip_segs = jax.ShapeDtypeStruct((chips, nrhs, bs), F32)
    chip_segs_b = jax.ShapeDtypeStruct((chips, nrhs, bs), BF16)

    def gathered_tiles(level, after):
        groups = jnp.arange(repeat, dtype=jnp.int32)[:, None, None, None]
        raw, slots = tiles[level, 0], pattern[1, level, 0]
        if after is not None:
            raw, slots, _ = lax.optimization_barrier((raw, slots, after))
        here = (slots // cols)[None, :, None, None] == groups
        own = jnp.sum(jnp.where(here, raw[None].astype(F32), 0.0), axis=1).astype(BF16)
        found = [own] + [None] * (cols - 1)
        for step in send_order(cols):
            found[step] = swap(own, "col", cols, step)
        return found

    def gather(mine):
        near = [mine]
        for chip in range(1, chips):
            near.append(swap(mine, "row", rows, 2 * chip))
        near = jnp.stack(near)
        return near, swap(near, "row", rows, 1)

    def scatter(solved, send, found_tiles):
        other = swap(send, "row", rows, 1)
        keep = call(functools.partial(keep_kernel, repeat), chip_segs, [], solved, *found_tiles)
        total = keep + other.astype(F32)
        found = [total[0]]
        for chip in range(1, chips):
            found.append(swap(total[chip].astype(BF16), "row", rows, 2 * chip))
        return found

    late_steps = send_order(cols)[-2:]
    early_steps = [step for step in range(cols) if step not in late_steps]

    def early_part(near, far, found_tiles):
        kernel = functools.partial(early_kernel, repeat, cols, early_steps)
        return call(kernel, seg, [], near, far, *[found_tiles[step] for step in early_steps])

    level_tiles = []
    for level in range(levels - 1):
        level_tiles.append(gathered_tiles(level, level_tiles[-1][0] if level_tiles else None))
    forward, mine = call(first_kernel, (seg, seg_b), [], rhs, dinv)
    forwards = [forward]
    for level in range(1, levels - 1):
        near, far = gather(mine)
        found_tiles = level_tiles[level - 1]
        forward, mine = call(
            functools.partial(forward_kernel, level, repeat, cols, late_steps),
            (seg, seg_b), [], early_part(near, far, found_tiles), near, far,
            *[found_tiles[step] for step in late_steps], rhs, dinv,
        )
        forwards.append(forward)
    top = levels - 1
    near, far = gather(mine)
    found_tiles = level_tiles[top - 1]
    solved, solved_b, send = call(
        functools.partial(turn_kernel, top, repeat, cols, late_steps),
        (seg, seg_b, chip_segs_b), [], early_part(near, far, found_tiles), near, far,
        *found_tiles, rhs, dinv,
    )
    upper = [solved]
    for level in range(levels - 2, 0, -1):
        arrived = scatter(solved_b, send, found_tiles)
        found_tiles = level_tiles[level - 1]
        solved, solved_b, send = call(
            functools.partial(backward_kernel, level, repeat, cols, chips),
            (seg, seg_b, chip_segs_b), [], *arrived, *found_tiles, forwards[level], dinv,
        )
        upper.insert(0, solved)
    arrived = scatter(solved_b, send, found_tiles)
    return call(
        functools.partial(last_kernel, chips, len(upper)),
        jax.ShapeDtypeStruct(rhs.shape, F32), [], *arrived, forwards[0], dinv, *upper,
    )


def solution(mesh):
    in_specs = (
        P(None, "row", None, None),
        P(None, "row", None, None),
        P(None, "row", "col", None, None),
        P(None, None, "row", "col"),
    )
    out_specs = P(None, "row", None, None)

    return jax.shard_map(
        per_device, mesh=mesh, in_specs=in_specs, out_specs=out_specs, check_vma=False
    )
```

time: 78.2 us -> 61 us (0.78)
  Pallas kernels: 12.1 us -> 3.66 us
  local copies, waits for them, and re-layouts: 7.87 us -> 1.93 us
  waiting for transfers between devices: 29 us -> 26.9 us
  other arithmetic: 2.4 us -> 1.55 us
    pallas_call x5 -> x9, Pallas kernels: 12.1 us -> 3.66 us  [call(): pl.pallas_call(kernel, out_shape=outs, in_specs=[pl.BlockSpec(memory_spac...]
    squeeze x4 -> x3, local copies, waits for them, and re-layouts: 4.49 us -> 0.01 us  [the longest x2 0.01 us: scatter(): found = [total[0]]]
    ppermute x22, waiting for transfers between devices: 29 us -> 26.9 us  [swap(): return lax.ppermute(value, axis, [(i, i ^ mask) for i in range(size)])]
    another operation x2, other arithmetic: 1.98 us -> 0.07 us
    squeeze x0 -> x1, other arithmetic: none -> 1.09 us  [gathered_tiles(): raw, slots = (tiles[level, 0], pattern[1, level, 0])]
    unnamed x42 -> x8, local copies, waits for them, and re-layouts: 2.67 us -> 1.9 us
  transfers between devices with their start and end apart: 22 -> 22, of which waited for: 15 -> 12; matrix products, arithmetic and copies ran while one was open for 2% -> 2% of each run, Pallas kernels for 0% -> 2%
where the time goes in v3:
time: 61 us; the launch traced here: 60.8 us
  waiting for transfers between devices  26.9 us (44%)
  starting transfers between devices  26.5 us (43%)
  Pallas kernels  3.66 us (6%)
  local copies, waits for them, and re-layouts  1.93 us (3%)
  other arithmetic  1.55 us (3%)
    ppermute x22, waiting for transfers between devices, swap(): return lax.ppermute(value, axis, [(i, i ^ mask) for i in range(size)])  26.9 us
    ppermute x22, starting transfers between devices, swap(): return lax.ppermute(value, axis, [(i, i ^ mask) for i in range(size)])  26.5 us
    pallas_call x9, Pallas kernels, call(): pl.pallas_call(kernel, out_shape=outs, in_specs=[pl.BlockSpec(memory_spac...  3.66 us
    unnamed x8, local copies, waits for them, and re-layouts  1.9 us
  transfers between devices with their start and end apart: 22, of which 12 were waited for; matrix products, arithmetic and copies ran while one was open for 2% of the time, Pallas kernels for 2%

profile of v3, /device:TPU:0, one launch (start us, length us, event | category | flops | bytes accessed | tf_op | source)
XLA Modules:
  0.0 60.8 jit_solution(3646074423332535298)
XLA Ops:
  0.0 0.0 copy-start
  0.0 1.0 %copy-done = bf16[3,1,256,256]{3,2,1,0:T(8,128)(2,1)S(1)} copy-done((bf16[3,1,256,256]{3,2,1,0:T(8,128)(2,1)S(1)}, bf16[3,1,256,256]{3,2,1,0:T(8,128)(2,1)}, u32[]{:S(2)}) %copy-start) | copy-done | bytes 393240
  1.0 0.0 copy-start.2
  1.0 0.9 %copy-done.2 = bf16[3,1,64,256]{3,2,1,0:T(8,128)(2,1)S(1)} copy-done((bf16[3,1,64,256]{3,2,1,0:T(8,128)(2,1)S(1)}, bf16[3,1,64,256]{3,2,1,0:T(8,128)(2,1)}, u32[]{:S(2)}) %copy-start.2) | copy-done | bytes 98328
  1.9 0.0 copy-start.3
  1.9 0.2 shard_map.46
  2.0 5.1 %collective-permute-start.2 = (bf16[64,256]{1,0:T(8,128)(2,1)S(1)}, bf16[64,256]{1,0:T(8,128)(2,1)S(1)}, u32[]{:S(2)}, u32[]{:S(2)}) collective-permute-start(bf16[64,256]{1,0:T(8,128)(2,1)S(1)} %get-tuple-element.17), channel_id=1, source_target_pairs={{0,24},{4,28},{8,16},{12,20},{16,8},{20,12},{24,0},{28,4},{1,25},{... | collective-permute-start | bytes 98312 | tf_op jit(solution)/shard_map/ppermute | solution.py:21
  7.2 0.0 collective-permute-start.1
  7.2 0.6 %collective-permute-start = (bf16[64,256]{1,0:T(8,128)(2,1)S(1)}, bf16[64,256]{1,0:T(8,128)(2,1)S(1)}, u32[]{:S(2)}, u32[]{:S(2)}) collective-permute-start(bf16[64,256]{1,0:T(8,128)(2,1)S(1)} %get-tuple-element.17), channel_id=1, source_target_pairs={{0,8},{4,12},{8,0},{12,4},{16,24},{20,28},{24,16},{28,20},{1,9},{5... | collective-permute-start | bytes 98312 | tf_op jit(solution)/shard_map/ppermute | solution.py:21
  7.8 0.0 copy-done.3
  7.8 1.1 %slice_bitcast_fusion = (bf16[2,256,256]{2,1,0:T(8,128)(2,1)S(1)}, f32[2,256,256]{2,1,0:T(8,128)S(1)}) fusion(bf16[2,1,2,256,256]{4,3,2,1,0:T(8,128)(2,1)} %param.6), kind=kLoop, calls=%fused_computation.5 | loop fusion | flops 131072 | bytes 1310720 | tf_op jit(solution)/shard_map/squeeze | solution.py:154
  8.9 0.1 select_reduce_fusion.1.refs_0_.refs_4_
  9.1 1.7 %collective-permute-start.6 = (bf16[2,256,256]{2,1,0:T(8,128)(2,1)S(1)}, bf16[2,256,256]{2,1,0:T(8,128)(2,1)S(1)}, u32[]{:S(2)}, u32[]{:S(2)}) collective-permute-start(bf16[2,256,256]{2,1,0:T(8,128)(2,1)S(1)} %select_reduce_fusion.1.refs_0_.refs_4_), channel_id=1, source_target_pairs={{0,1},{1,0},{2,3},{3,2},{4,5},{5,4},{6,7},{7,6},{8,9},{9,8},{10,11... | collective-permute-start | bytes 786440 | tf_op jit(solution)/shard_map/ppermute | solution.py:21
  10.8 1.5 %collective-permute-start.5 = (bf16[2,256,256]{2,1,0:T(8,128)(2,1)S(1)}, bf16[2,256,256]{2,1,0:T(8,128)(2,1)S(1)}, u32[]{:S(2)}, u32[]{:S(2)}) collective-permute-start(bf16[2,256,256]{2,1,0:T(8,128)(2,1)S(1)} %select_reduce_fusion.1.refs_0_.refs_4_), channel_id=1, source_target_pairs={{0,2},{1,3},{2,0},{3,1},{4,6},{5,7},{6,4},{7,5},{8,10},{9,11},{10,... | collective-permute-start | bytes 786440 | tf_op jit(solution)/shard_map/ppermute | solution.py:21
  12.3 0.0 collective-permute-done.2
  12.4 0.4 collective-permute-start.4
  12.7 0.0 collective-permute-done.1
  12.8 0.0 collective-permute-done
  12.8 0.1 collective-permute-start.3
  12.9 0.0 copy-start.1
  12.9 1.3 %collective-permute-done.3.far = bf16[4,64,256]{2,1,0:T(8,128)(2,1)S(1)} collective-permute-done((bf16[4,64,256]{2,1,0:T(8,128)(2,1)S(1)}, bf16[4,64,256]{2,1,0:T(8,128)(2,1)S(1)}, u32[]{:S(2)}, u32[]{:S(2)}) %collective-permute-start.3) | collective-permute-done | bytes 131104 | tf_op jit(solution)/shard_map/ppermute | solution.py:21
  14.2 9.1 %collective-permute-done.4.refs_1_.refs_7_.refs_3_ = bf16[2,256,256]{2,1,0:T(8,128)(2,1)S(1)} collective-permute-done((bf16[2,256,256]{2,1,0:T(8,128)(2,1)S(1)}, bf16[2,256,256]{2,1,0:T(8,128)(2,1)S(1)}, u32[]{:S(2)}, u32[]{:S(2)}) %collective-permute-start.4) | collective-permute-done | bytes 262176 | tf_op jit(solution)/shard_map/ppermute | solution.py:21
  23.3 0.3 shard_map.47.part
  23.6 0.0 collective-permute-done.6.refs_1_.refs_5_
  23.6 0.0 collective-permute-done.5.refs_0_.refs_6_.refs_2_
  23.6 0.0 copy-done.1
  23.6 0.5 shard_map.48
  24.1 3.5 %collective-permute-start.9 = (bf16[64,256]{1,0:T(8,128)(2,1)S(1)}, bf16[64,256]{1,0:T(8,128)(2,1)S(1)}, u32[]{:S(2)}, u32[]{:S(2)}) collective-permute-start(bf16[64,256]{1,0:T(8,128)(2,1)S(1)} %get-tuple-element.18), channel_id=1, source_target_pairs={{0,24},{4,28},{8,16},{12,20},{16,8},{20,12},{24,0},{28,4},{1,25},{... | collective-permute-start | bytes 98312 | tf_op jit(solution)/shard_map/ppermute | solution.py:21
  27.6 0.0 collective-permute-start.8
  27.6 0.9 %collective-permute-start.7 = (bf16[64,256]{1,0:T(8,128)(2,1)S(1)}, bf16[64,256]{1,0:T(8,128)(2,1)S(1)}, u32[]{:S(2)}, u32[]{:S(2)}) collective-permute-start(bf16[64,256]{1,0:T(8,128)(2,1)S(1)} %get-tuple-element.18), channel_id=1, source_target_pairs={{0,8},{4,12},{8,0},{12,4},{16,24},{20,28},{24,16},{28,20},{1,9},{5... | collective-permute-start | bytes 98312 | tf_op jit(solution)/shard_map/ppermute | solution.py:21
  28.5 0.1 select_reduce_fusion.refs_0_
  28.7 1.5 %collective-permute-start.11 = (bf16[2,256,256]{2,1,0:T(8,128)(2,1)S(1)}, bf16[2,256,256]{2,1,0:T(8,128)(2,1)S(1)}, u32[]{:S(2)}, u32[]{:S(2)}) collective-permute-start(bf16[2,256,256]{2,1,0:T(8,128)(2,1)S(1)} %select_reduce_fusion.refs_0_), channel_id=1, source_target_pairs={{0,3},{1,2},{2,1},{3,0},{4,7},{5,6},{6,5},{7,4},{8,11},{9,10},{10,... | collective-permute-start | bytes 786440 | tf_op jit(solution)/shard_map/ppermute | solution.py:21
  30.2 1.4 %collective-permute-start.13 = (bf16[2,256,256]{2,1,0:T(8,128)(2,1)S(1)}, bf16[2,256,256]{2,1,0:T(8,128)(2,1)S(1)}, u32[]{:S(2)}, u32[]{:S(2)}) collective-permute-start(bf16[2,256,256]{2,1,0:T(8,128)(2,1)S(1)} %select_reduce_fusion.refs_0_), channel_id=1, source_target_pairs={{0,2},{1,3},{2,0},{3,1},{4,6},{5,7},{6,4},{7,5},{8,10},{9,11},{10,... | collective-permute-start | bytes 786440 | tf_op jit(solution)/shard_map/ppermute | solution.py:21
  31.6 0.0 collective-permute-done.9
  31.6 0.6 %collective-permute-start.12 = (bf16[2,256,256]{2,1,0:T(8,128)(2,1)S(1)}, bf16[2,256,256]{2,1,0:T(8,128)(2,1)S(1)}, u32[]{:S(2)}, u32[]{:S(2)}) collective-permute-start(bf16[2,256,256]{2,1,0:T(8,128)(2,1)S(1)} %select_reduce_fusion.refs_0_), channel_id=1, source_target_pairs={{0,1},{1,0},{2,3},{3,2},{4,5},{5,4},{6,7},{7,6},{8,9},{9,8},{10,11... | collective-permute-start | bytes 786440 | tf_op jit(solution)/shard_map/ppermute | solution.py:21
  32.2 0.2 collective-permute-done.8
  32.4 0.0 collective-permute-done.7
  32.4 0.1 collective-permute-start.10
  32.5 5.6 %collective-permute-done.11.refs_1_.refs_3_ = bf16[2,256,256]{2,1,0:T(8,128)(2,1)S(1)} collective-permute-done((bf16[2,256,256]{2,1,0:T(8,128)(2,1)S(1)}, bf16[2,256,256]{2,1,0:T(8,128)(2,1)S(1)}, u32[]{:S(2)}, u32[]{:S(2)}) %collective-permute-start.11) | collective-permute-done | bytes 262176 | tf_op jit(solution)/shard_map/ppermute | solution.py:21
  38.2 0.0 collective-permute-done.10.far
  38.2 0.3 shard_map.49.part
  38.4 2.4 %collective-permute-done.13.refs_2_ = bf16[2,256,256]{2,1,0:T(8,128)(2,1)S(1)} collective-permute-done((bf16[2,256,256]{2,1,0:T(8,128)(2,1)S(1)}, bf16[2,256,256]{2,1,0:T(8,128)(2,1)S(1)}, u32[]{:S(2)}, u32[]{:S(2)}) %collective-permute-start.13) | collective-permute-done | bytes 262176 | tf_op jit(solution)/shard_map/ppermute | solution.py:21
  40.8 0.0 collective-permute-done.12.refs_1_
  40.8 0.9 %shard_map.50 = (f32[64,256]{1,0:T(8,128)S(1)}, bf16[64,256]{1,0:T(8,128)(2,1)S(1)}, bf16[4,64,256]{2,1,0:T(8,128)(2,1)S(1)}) custom-call(f32[64,256]{1,0:T(8,128)S(1)} %shard_map.49.part, bf16[4,64,256]{2,1,0:T(8,128)(2,1)S(1)} %pad_maximum_fusion.1.near, bf16[4,64,256]{2,1,0:T(8,128)(2,1)S(1)} %collective-permute-done.10.far, ...), custom_call_target="tpu_custom_call" | custom-call | tf_op jit(solution)/shard_map/pallas_call | solution.py:129
  41.7 0.1 collective-permute-start.14
  41.8 0.2 shard_map.51
  42.0 1.1 %collective-permute-done.14 = bf16[4,64,256]{2,1,0:T(8,128)(2,1)S(1)} collective-permute-done((bf16[4,64,256]{2,1,0:T(8,128)(2,1)S(1)}, bf16[4,64,256]{2,1,0:T(8,128)(2,1)S(1)}, u32[]{:S(2)}, u32[]{:S(2)}) %collective-permute-start.14) | collective-permute-done | bytes 131104 | tf_op jit(solution)/shard_map/ppermute | solution.py:21
  43.2 3.4 %collective-permute-start.17 = (bf16[64,256]{1,0:T(8,128)(2,1)S(1)}, bf16[64,256]{1,0:T(8,128)(2,1)S(1)}, u32[]{:S(2)}, u32[]{:S(2)}) collective-permute-start(bf16[64,256]{1,0:T(8,128)(2,1)S(1)} %get-tuple-element.38), channel_id=1, source_target_pairs={{0,24},{4,28},{8,16},{12,20},{16,8},{20,12},{24,0},{28,4},{1,25},{... | collective-permute-start | bytes 98312 | tf_op jit(solution)/shard_map/ppermute | solution.py:21
  46.6 0.0 collective-permute-start.16
  46.6 1.0 %collective-permute-start.15 = (bf16[64,256]{1,0:T(8,128)(2,1)S(1)}, bf16[64,256]{1,0:T(8,128)(2,1)S(1)}, u32[]{:S(2)}, u32[]{:S(2)}) collective-permute-start(bf16[64,256]{1,0:T(8,128)(2,1)S(1)} %get-tuple-element.40), channel_id=1, source_target_pairs={{0,8},{4,12},{8,0},{12,4},{16,24},{20,28},{24,16},{28,20},{1,9},{5... | collective-permute-start | bytes 98312 | tf_op jit(solution)/shard_map/ppermute | solution.py:21
  47.6 1.5 %collective-permute-done.17.refs_3_ = bf16[64,256]{1,0:T(8,128)(2,1)S(1)} collective-permute-done((bf16[64,256]{1,0:T(8,128)(2,1)S(1)}, bf16[64,256]{1,0:T(8,128)(2,1)S(1)}, u32[]{:S(2)}, u32[]{:S(2)}) %collective-permute-start.17) | collective-permute-done | bytes 32800 | tf_op jit(solution)/shard_map/ppermute | solution.py:21
  49.1 2.3 %collective-permute-done.16.refs_2_ = bf16[64,256]{1,0:T(8,128)(2,1)S(1)} collective-permute-done((bf16[64,256]{1,0:T(8,128)(2,1)S(1)}, bf16[64,256]{1,0:T(8,128)(2,1)S(1)}, u32[]{:S(2)}, u32[]{:S(2)}) %collective-permute-start.16) | collective-permute-done | bytes 32800 | tf_op jit(solution)/shard_map/ppermute | solution.py:21
  51.4 0.0 collective-permute-done.15.refs_1_
  51.4 0.3 shard_map.52
  51.7 0.1 collective-permute-start.18
  51.8 0.2 shard_map.53
  52.0 1.1 %collective-permute-done.18 = bf16[4,64,256]{2,1,0:T(8,128)(2,1)S(1)} collective-permute-done((bf16[4,64,256]{2,1,0:T(8,128)(2,1)S(1)}, bf16[4,64,256]{2,1,0:T(8,128)(2,1)S(1)}, u32[]{:S(2)}, u32[]{:S(2)}) %collective-permute-start.18) | collective-permute-done | bytes 131104 | tf_op jit(solution)/shard_map/ppermute | solution.py:21
  53.2 1.5 %collective-permute-start.21 = (bf16[64,256]{1,0:T(8,128)(2,1)S(1)}, bf16[64,256]{1,0:T(8,128)(2,1)S(1)}, u32[]{:S(2)}, u32[]{:S(2)}) collective-permute-start(bf16[64,256]{1,0:T(8,128)(2,1)S(1)} %get-tuple-element.35), channel_id=1, source_target_pairs={{0,24},{4,28},{8,16},{12,20},{16,8},{20,12},{24,0},{28,4},{1,25},{... | collective-permute-start | bytes 98312 | tf_op jit(solution)/shard_map/ppermute | solution.py:21
  54.7 0.6 %collective-permute-start.20 = (bf16[64,256]{1,0:T(8,128)(2,1)S(1)}, bf16[64,256]{1,0:T(8,128)(2,1)S(1)}, u32[]{:S(2)}, u32[]{:S(2)}) collective-permute-start(bf16[64,256]{1,0:T(8,128)(2,1)S(1)} %get-tuple-element.36), channel_id=1, source_target_pairs={{0,16},{4,20},{8,24},{12,28},{16,0},{20,4},{24,8},{28,12},{1,17},{... | collective-permute-start | bytes 98312 | tf_op jit(solution)/shard_map/ppermute | solution.py:21
  55.4 2.3 %collective-permute-start.19 = (bf16[64,256]{1,0:T(8,128)(2,1)S(1)}, bf16[64,256]{1,0:T(8,128)(2,1)S(1)}, u32[]{:S(2)}, u32[]{:S(2)}) collective-permute-start(bf16[64,256]{1,0:T(8,128)(2,1)S(1)} %get-tuple-element.37), channel_id=1, source_target_pairs={{0,8},{4,12},{8,0},{12,4},{16,24},{20,28},{24,16},{28,20},{1,9},{5... | collective-permute-start | bytes 98312 | tf_op jit(solution)/shard_map/ppermute | solution.py:21
  57.7 1.6 %collective-permute-done.21.refs_3_ = bf16[64,256]{1,0:T(8,128)(2,1)S(1)} collective-permute-done((bf16[64,256]{1,0:T(8,128)(2,1)S(1)}, bf16[64,256]{1,0:T(8,128)(2,1)S(1)}, u32[]{:S(2)}, u32[]{:S(2)}) %collective-permute-start.21) | collective-permute-done | bytes 32800 | tf_op jit(solution)/shard_map/ppermute | solution.py:21
  59.3 0.4 collective-permute-done.20.refs_2_
  59.7 0.3 collective-permute-done.19.refs_1_
  60.0 0.8 %shard_map.54 = f32[3,1,64,256]{3,2,1,0:T(8,128)} custom-call(f32[64,256]{1,0:T(8,128)S(1)} %slice_bitcast_fusion.1.refs_0_, bf16[64,256]{1,0:T(8,128)(2,1)S(1)} %collective-permute-done.19.refs_1_, bf16[64,256]{1,0:T(8,128)(2,1)S(1)} %collective-permute-done.20.refs_2_, bf16[64,256]{1,0:T(8,128)(2,1)S(1)} %collective-permute-done.21.refs_3_, ...), custom_call_target="tpu_custom_call" | custom-call | tf_op jit(solution)/shard_map/pallas_call | solution.py:129
  (14 shorter events, 0.2 us)
Async XLA Ops:
  0.0 1.0 %copy-start = (bf16[3,1,256,256]{3,2,1,0:T(8,128)(2,1)S(1)}, bf16[3,1,256,256]{3,2,1,0:T(8,128)(2,1)}, u32[]{:S(2)}) copy-start(bf16[3,1,256,256]{3,2,1,0:T(8,128)(2,1)} %refs_5_.3) | copy-start | bytes 1179652
  1.0 0.9 %copy-start.2 = (bf16[3,1,64,256]{3,2,1,0:T(8,128)(2,1)S(1)}, bf16[3,1,64,256]{3,2,1,0:T(8,128)(2,1)}, u32[]{:S(2)}) copy-start(bf16[3,1,64,256]{3,2,1,0:T(8,128)(2,1)} %refs_4_.1) | copy-start | bytes 294916
  1.9 5.9 %copy-start.3 = (s32[2,2,1,2]{3,2,1,0:T(1,128)S(1)}, s32[2,2,1,2]{3,2,1,0:T(1,128)}, u32[]{:S(2)}) copy-start(s32[2,2,1,2]{3,2,1,0:T(1,128)} %param.7) | copy-start | bytes 100
  2.0 10.3 %collective-permute-start.2 = (bf16[64,256]{1,0:T(8,128)(2,1)S(1)}, bf16[64,256]{1,0:T(8,128)(2,1)S(1)}, u32[]{:S(2)}, u32[]{:S(2)}) collective-permute-start(bf16[64,256]{1,0:T(8,128)(2,1)S(1)} %get-tuple-element.17), channel_id=1, source_target_pairs={{0,24},{4,28},{8,16},{12,20},{16,8},{20,12},{24,0},{28,4},{1,25},{... | collective-permute-start | bytes 98312 | tf_op jit(solution)/shard_map/ppermute | solution.py:21
  7.2 5.6 %collective-permute-start.1 = (bf16[64,256]{1,0:T(8,128)(2,1)S(1)}, bf16[64,256]{1,0:T(8,128)(2,1)S(1)}, u32[]{:S(2)}, u32[]{:S(2)}) collective-permute-start(bf16[64,256]{1,0:T(8,128)(2,1)S(1)} %get-tuple-element.17), channel_id=1, source_target_pairs={{0,16},{4,20},{8,24},{12,28},{16,0},{20,4},{24,8},{28,12},{1,17},{... | collective-permute-start | bytes 98312 | tf_op jit(solution)/shard_map/ppermute | solution.py:21
  7.2 5.6 %collective-permute-start = (bf16[64,256]{1,0:T(8,128)(2,1)S(1)}, bf16[64,256]{1,0:T(8,128)(2,1)S(1)}, u32[]{:S(2)}, u32[]{:S(2)}) collective-permute-start(bf16[64,256]{1,0:T(8,128)(2,1)S(1)} %get-tuple-element.17), channel_id=1, source_target_pairs={{0,8},{4,12},{8,0},{12,4},{16,24},{20,28},{24,16},{28,20},{1,9},{5... | collective-permute-start | bytes 98312 | tf_op jit(solution)/shard_map/ppermute | solution.py:21
  9.1 14.5 %collective-permute-start.6 = (bf16[2,256,256]{2,1,0:T(8,128)(2,1)S(1)}, bf16[2,256,256]{2,1,0:T(8,128)(2,1)S(1)}, u32[]{:S(2)}, u32[]{:S(2)}) collective-permute-start(bf16[2,256,256]{2,1,0:T(8,128)(2,1)S(1)} %select_reduce_fusion.1.refs_0_.refs_4_), channel_id=1, source_target_pairs={{0,1},{1,0},{2,3},{3,2},{4,5},{5,4},{6,7},{7,6},{8,9},{9,8},{10,11... | collective-permute-start | bytes 786440 | tf_op jit(solution)/shard_map/ppermute | solution.py:21
  10.8 12.8 %collective-permute-start.5 = (bf16[2,256,256]{2,1,0:T(8,128)(2,1)S(1)}, bf16[2,256,256]{2,1,0:T(8,128)(2,1)S(1)}, u32[]{:S(2)}, u32[]{:S(2)}) collective-permute-start(bf16[2,256,256]{2,1,0:T(8,128)(2,1)S(1)} %select_reduce_fusion.1.refs_0_.refs_4_), channel_id=1, source_target_pairs={{0,2},{1,3},{2,0},{3,1},{4,6},{5,7},{6,4},{7,5},{8,10},{9,11},{10,... | collective-permute-start | bytes 786440 | tf_op jit(solution)/shard_map/ppermute | solution.py:21
  12.4 10.9 %collective-permute-start.4 = (bf16[2,256,256]{2,1,0:T(8,128)(2,1)S(1)}, bf16[2,256,256]{2,1,0:T(8,128)(2,1)S(1)}, u32[]{:S(2)}, u32[]{:S(2)}) collective-permute-start(bf16[2,256,256]{2,1,0:T(8,128)(2,1)S(1)} %select_reduce_fusion.1.refs_0_.refs_4_), channel_id=1, source_target_pairs={{0,3},{1,2},{2,1},{3,0},{4,7},{5,6},{6,5},{7,4},{8,11},{9,10},{10,... | collective-permute-start | bytes 786440 | tf_op jit(solution)/shard_map/ppermute | solution.py:21
  12.8 1.4 %collective-permute-start.3 = (bf16[4,64,256]{2,1,0:T(8,128)(2,1)S(1)}, bf16[4,64,256]{2,1,0:T(8,128)(2,1)S(1)}, u32[]{:S(2)}, u32[]{:S(2)}) collective-permute-start(bf16[4,64,256]{2,1,0:T(8,128)(2,1)S(1)} %pad_maximum_fusion.near), channel_id=1, source_target_pairs={{0,4},{4,0},{8,12},{12,8},{16,20},{20,16},{24,28},{28,24},{1,5},{5... | collective-permute-start | bytes 393224 | tf_op jit(solution)/shard_map/ppermute | solution.py:21
  12.9 10.7 %copy-start.1 = (bf16[3,1,256,256]{3,2,1,0:T(8,128)(2,1)S(1)}, bf16[3,1,256,256]{3,2,1,0:T(8,128)(2,1)}, u32[]{:S(2)}) copy-start(bf16[3,1,256,256]{3,2,1,0:T(8,128)(2,1)} %refs_5_.3) | copy-start | bytes 1179652
  24.1 7.5 %collective-permute-start.9 = (bf16[64,256]{1,0:T(8,128)(2,1)S(1)}, bf16[64,256]{1,0:T(8,128)(2,1)S(1)}, u32[]{:S(2)}, u32[]{:S(2)}) collective-permute-start(bf16[64,256]{1,0:T(8,128)(2,1)S(1)} %get-tuple-element.18), channel_id=1, source_target_pairs={{0,24},{4,28},{8,16},{12,20},{16,8},{20,12},{24,0},{28,4},{1,25},{... | collective-permute-start | bytes 98312 | tf_op jit(solution)/shard_map/ppermute | solution.py:21
  27.6 4.8 %collective-permute-start.8 = (bf16[64,256]{1,0:T(8,128)(2,1)S(1)}, bf16[64,256]{1,0:T(8,128)(2,1)S(1)}, u32[]{:S(2)}, u32[]{:S(2)}) collective-permute-start(bf16[64,256]{1,0:T(8,128)(2,1)S(1)} %get-tuple-element.18), channel_id=1, source_target_pairs={{0,16},{4,20},{8,24},{12,28},{16,0},{20,4},{24,8},{28,12},{1,17},{... | collective-permute-start | bytes 98312 | tf_op jit(solution)/shard_map/ppermute | solution.py:21
  27.6 4.8 %collective-permute-start.7 = (bf16[64,256]{1,0:T(8,128)(2,1)S(1)}, bf16[64,256]{1,0:T(8,128)(2,1)S(1)}, u32[]{:S(2)}, u32[]{:S(2)}) collective-permute-start(bf16[64,256]{1,0:T(8,128)(2,1)S(1)} %get-tuple-element.18), channel_id=1, source_target_pairs={{0,8},{4,12},{8,0},{12,4},{16,24},{20,28},{24,16},{28,20},{1,9},{5... | collective-permute-start | bytes 98312 | tf_op jit(solution)/shard_map/ppermute | solution.py:21
  28.7 9.5 %collective-permute-start.11 = (bf16[2,256,256]{2,1,0:T(8,128)(2,1)S(1)}, bf16[2,256,256]{2,1,0:T(8,128)(2,1)S(1)}, u32[]{:S(2)}, u32[]{:S(2)}) collective-permute-start(bf16[2,256,256]{2,1,0:T(8,128)(2,1)S(1)} %select_reduce_fusion.refs_0_), channel_id=1, source_target_pairs={{0,3},{1,2},{2,1},{3,0},{4,7},{5,6},{6,5},{7,4},{8,11},{9,10},{10,... | collective-permute-start | bytes 786440 | tf_op jit(solution)/shard_map/ppermute | solution.py:21
  30.2 10.7 %collective-permute-start.13 = (bf16[2,256,256]{2,1,0:T(8,128)(2,1)S(1)}, bf16[2,256,256]{2,1,0:T(8,128)(2,1)S(1)}, u32[]{:S(2)}, u32[]{:S(2)}) collective-permute-start(bf16[2,256,256]{2,1,0:T(8,128)(2,1)S(1)} %select_reduce_fusion.refs_0_), channel_id=1, source_target_pairs={{0,2},{1,3},{2,0},{3,1},{4,6},{5,7},{6,4},{7,5},{8,10},{9,11},{10,... | collective-permute-start | bytes 786440 | tf_op jit(solution)/shard_map/ppermute | solution.py:21
  31.6 9.2 %collective-permute-start.12 = (bf16[2,256,256]{2,1,0:T(8,128)(2,1)S(1)}, bf16[2,256,256]{2,1,0:T(8,128)(2,1)S(1)}, u32[]{:S(2)}, u32[]{:S(2)}) collective-permute-start(bf16[2,256,256]{2,1,0:T(8,128)(2,1)S(1)} %select_reduce_fusion.refs_0_), channel_id=1, source_target_pairs={{0,1},{1,0},{2,3},{3,2},{4,5},{5,4},{6,7},{7,6},{8,9},{9,8},{10,11... | collective-permute-start | bytes 786440 | tf_op jit(solution)/shard_map/ppermute | solution.py:21
  32.4 5.7 %collective-permute-start.10 = (bf16[4,64,256]{2,1,0:T(8,128)(2,1)S(1)}, bf16[4,64,256]{2,1,0:T(8,128)(2,1)S(1)}, u32[]{:S(2)}, u32[]{:S(2)}) collective-permute-start(bf16[4,64,256]{2,1,0:T(8,128)(2,1)S(1)} %pad_maximum_fusion.1.near), channel_id=1, source_target_pairs={{0,4},{4,0},{8,12},{12,8},{16,20},{20,16},{24,28},{28,24},{1,5},{5... | collective-permute-start | bytes 393224 | tf_op jit(solution)/shard_map/ppermute | solution.py:21
  41.7 1.4 %collective-permute-start.14 = (bf16[4,64,256]{2,1,0:T(8,128)(2,1)S(1)}, bf16[4,64,256]{2,1,0:T(8,128)(2,1)S(1)}, u32[]{:S(2)}, u32[]{:S(2)}) collective-permute-start(bf16[4,64,256]{2,1,0:T(8,128)(2,1)S(1)} %get-tuple-element.22), channel_id=1, source_target_pairs={{0,4},{4,0},{8,12},{12,8},{16,20},{20,16},{24,28},{28,24},{1,5},{5... | collective-permute-start | bytes 393224 | tf_op jit(solution)/shard_map/ppermute | solution.py:21
  43.2 6.0 %collective-permute-start.17 = (bf16[64,256]{1,0:T(8,128)(2,1)S(1)}, bf16[64,256]{1,0:T(8,128)(2,1)S(1)}, u32[]{:S(2)}, u32[]{:S(2)}) collective-permute-start(bf16[64,256]{1,0:T(8,128)(2,1)S(1)} %get-tuple-element.38), channel_id=1, source_target_pairs={{0,24},{4,28},{8,16},{12,20},{16,8},{20,12},{24,0},{28,4},{1,25},{... | collective-permute-start | bytes 98312 | tf_op jit(solution)/shard_map/ppermute | solution.py:21
  46.6 4.8 %collective-permute-start.16 = (bf16[64,256]{1,0:T(8,128)(2,1)S(1)}, bf16[64,256]{1,0:T(8,128)(2,1)S(1)}, u32[]{:S(2)}, u32[]{:S(2)}) collective-permute-start(bf16[64,256]{1,0:T(8,128)(2,1)S(1)} %get-tuple-element.39), channel_id=1, source_target_pairs={{0,16},{4,20},{8,24},{12,28},{16,0},{20,4},{24,8},{28,12},{1,17},{... | collective-permute-start | bytes 98312 | tf_op jit(solution)/shard_map/ppermute | solution.py:21
  46.6 4.8 %collective-permute-start.15 = (bf16[64,256]{1,0:T(8,128)(2,1)S(1)}, bf16[64,256]{1,0:T(8,128)(2,1)S(1)}, u32[]{:S(2)}, u32[]{:S(2)}) collective-permute-start(bf16[64,256]{1,0:T(8,128)(2,1)S(1)} %get-tuple-element.40), channel_id=1, source_target_pairs={{0,8},{4,12},{8,0},{12,4},{16,24},{20,28},{24,16},{28,20},{1,9},{5... | collective-permute-start | bytes 98312 | tf_op jit(solution)/shard_map/ppermute | solution.py:21
  51.7 1.4 %collective-permute-start.18 = (bf16[4,64,256]{2,1,0:T(8,128)(2,1)S(1)}, bf16[4,64,256]{2,1,0:T(8,128)(2,1)S(1)}, u32[]{:S(2)}, u32[]{:S(2)}) collective-permute-start(bf16[4,64,256]{2,1,0:T(8,128)(2,1)S(1)} %get-tuple-element.25), channel_id=1, source_target_pairs={{0,4},{4,0},{8,12},{12,8},{16,20},{20,16},{24,28},{28,24},{1,5},{5... | collective-permute-start | bytes 393224 | tf_op jit(solution)/shard_map/ppermute | solution.py:21
  53.2 6.1 %collective-permute-start.21 = (bf16[64,256]{1,0:T(8,128)(2,1)S(1)}, bf16[64,256]{1,0:T(8,128)(2,1)S(1)}, u32[]{:S(2)}, u32[]{:S(2)}) collective-permute-start(bf16[64,256]{1,0:T(8,128)(2,1)S(1)} %get-tuple-element.35), channel_id=1, source_target_pairs={{0,24},{4,28},{8,16},{12,20},{16,8},{20,12},{24,0},{28,4},{1,25},{... | collective-permute-start | bytes 98312 | tf_op jit(solution)/shard_map/ppermute | solution.py:21
  54.7 4.9 %collective-permute-start.20 = (bf16[64,256]{1,0:T(8,128)(2,1)S(1)}, bf16[64,256]{1,0:T(8,128)(2,1)S(1)}, u32[]{:S(2)}, u32[]{:S(2)}) collective-permute-start(bf16[64,256]{1,0:T(8,128)(2,1)S(1)} %get-tuple-element.36), channel_id=1, source_target_pairs={{0,16},{4,20},{8,24},{12,28},{16,0},{20,4},{24,8},{28,12},{1,17},{... | collective-permute-start | bytes 98312 | tf_op jit(solution)/shard_map/ppermute | solution.py:21
  55.4 4.6 %collective-permute-start.19 = (bf16[64,256]{1,0:T(8,128)(2,1)S(1)}, bf16[64,256]{1,0:T(8,128)(2,1)S(1)}, u32[]{:S(2)}, u32[]{:S(2)}) collective-permute-start(bf16[64,256]{1,0:T(8,128)(2,1)S(1)} %get-tuple-element.37), channel_id=1, source_target_pairs={{0,8},{4,12},{8,0},{12,4},{16,24},{20,28},{24,16},{28,20},{1,9},{5... | collective-permute-start | bytes 98312 | tf_op jit(solution)/shard_map/ppermute | solution.py:21

commit v4 on v3

--- a/solution.py
+++ b/solution.py
@@ -13,8 +13,10 @@
 VMEM_LIMIT = 16 * 2**20
 
 
-def send_order(cols):
-    return sorted(range(1, cols), key=lambda step: -step)
+def send_order(cols, level):
+    if level == 0:
+        return sorted(range(1, cols), reverse=True)
+    return list(range(1, cols))
 
 
 def swap(value, axis, size, mask):
@@ -67,6 +69,17 @@
     out_b[...] = solved.astype(BF16)
 
 
+def pick_kernel(level, cols, pattern, raw, own):
+    shape = own.shape[1:]
+    for group in range(own.shape[0]):
+        total = jnp.zeros(shape, F32)
+        for slot in range(raw.shape[0]):
+            place = jnp.broadcast_to(pattern[1, level, :, slot : slot + 1], shape)
+            here = (place >= cols * group) & (place < cols * (group + 1))
+            total = total + jnp.where(here, raw[slot].astype(F32), 0.0)
+        own[group] = total.astype(BF16)
+
+
 def early_kernel(repeat, cols, steps, near, far, *refs):
     refs[-1][...] = update(near, far, refs[:-1], steps, repeat, cols)
 
@@ -150,14 +163,15 @@
     chip_segs_b = jax.ShapeDtypeStruct((chips, nrhs, bs), BF16)
 
     def gathered_tiles(level, after):
-        groups = jnp.arange(repeat, dtype=jnp.int32)[:, None, None, None]
-        raw, slots = tiles[level, 0], pattern[1, level, 0]
+        source = tiles
         if after is not None:
-            raw, slots, _ = lax.optimization_barrier((raw, slots, after))
-        here = (slots // cols)[None, :, None, None] == groups
-        own = jnp.sum(jnp.where(here, raw[None].astype(F32), 0.0), axis=1).astype(BF16)
+            source, _ = lax.optimization_barrier((tiles, after))
+        own = call(
+            functools.partial(pick_kernel, level, cols),
+            jax.ShapeDtypeStruct((repeat, bs, bs), BF16), [], pattern, source[level, 0],
+        )
         found = [own] + [None] * (cols - 1)
-        for step in send_order(cols):
+        for step in send_order(cols, level):
             found[step] = swap(own, "col", cols, step)
         return found
 
@@ -177,10 +191,10 @@
             found.append(swap(total[chip].astype(BF16), "row", rows, 2 * chip))
         return found
 
-    late_steps = send_order(cols)[-2:]
-    early_steps = [step for step in range(cols) if step not in late_steps]
-
-    def early_part(near, far, found_tiles):
+    late_steps = [send_order(cols, level)[-2:] for level in range(levels - 1)]
+
+    def early_part(level, near, far, found_tiles):
+        early_steps = [step for step in range(cols) if step not in late_steps[level - 1]]
         kernel = functools.partial(early_kernel, repeat, cols, early_steps)
         return call(kernel, seg, [], near, far, *[found_tiles[step] for step in early_steps])
 
@@ -193,17 +207,17 @@
         near, far = gather(mine)
         found_tiles = level_tiles[level - 1]
         forward, mine = call(
-            functools.partial(forward_kernel, level, repeat, cols, late_steps),
-            (seg, seg_b), [], early_part(near, far, found_tiles), near, far,
-            *[found_tiles[step] for step in late_steps], rhs, dinv,
+            functools.partial(forward_kernel, level, repeat, cols, late_steps[level - 1]),
+            (seg, seg_b), [], early_part(level, near, far, found_tiles), near, far,
+            *[found_tiles[step] for step in late_steps[level - 1]], rhs, dinv,
         )
         forwards.append(forward)
     top = levels - 1
     near, far = gather(mine)
     found_tiles = level_tiles[top - 1]
     solved, solved_b, send = call(
-        functools.partial(turn_kernel, top, repeat, cols, late_steps),
-        (seg, seg_b, chip_segs_b), [], early_part(near, far, found_tiles), near, far,
+        functools.partial(turn_kernel, top, repeat, cols, late_steps[top - 1]),
+        (seg, seg_b, chip_segs_b), [], early_part(top, near, far, found_tiles), near, far,
         *found_tiles, rhs, dinv,
     )
     upper = [solved]

time: 61 us -> 64 us (1.049)
  waiting for transfers between devices: 26.9 us -> 30 us
  other arithmetic: 1.55 us -> 0.11 us
  local copies, waits for them, and re-layouts: 1.93 us -> 2.92 us
    ppermute x22, waiting for transfers between devices: 26.9 us -> 30 us  [swap(): return lax.ppermute(value, axis, [(i, i ^ mask) for i in range(size)])]
    squeeze x1 -> x0, other arithmetic: 1.09 us -> none  [gathered_tiles(): raw, slots = (tiles[level, 0], pattern[1, level, 0])]
    squeeze x1 -> x2, local copies, waits for them, and re-layouts: 0.01 us -> 0.98 us  [gathered_tiles(): source[level, 0]]
    pallas_call x9 -> x11, Pallas kernels: 3.66 us -> 4.05 us  [call(): pl.pallas_call(kernel, out_shape=outs, in_specs=[pl.BlockSpec(memory_spac...]
    unnamed x8 -> x12, local copies, waits for them, and re-layouts: 1.9 us -> 1.91 us
  transfers between devices with their start and end apart: 22 -> 22, of which waited for: 12 -> 14; matrix products, arithmetic and copies ran while one was open for 2% -> 2% of each run, Pallas kernels for 2% -> 2%
where the time goes in v4:
time: 64 us; the launch traced here: 63.8 us
  waiting for transfers between devices  30 us (47%)
  starting transfers between devices  26.5 us (41%)
  Pallas kernels  4.05 us (6%)
  local copies, waits for them, and re-layouts  2.92 us (5%)
    ppermute x22, waiting for transfers between devices, swap(): return lax.ppermute(value, axis, [(i, i ^ mask) for i in range(size)])  30 us
    ppermute x22, starting transfers between devices, swap(): return lax.ppermute(value, axis, [(i, i ^ mask) for i in range(size)])  26.5 us
    pallas_call x11, Pallas kernels, call(): pl.pallas_call(kernel, out_shape=outs, in_specs=[pl.BlockSpec(memory_spac...  4.05 us
    unnamed x12, local copies, waits for them, and re-layouts  1.91 us
  transfers between devices with their start and end apart: 22, of which 14 were waited for; matrix products, arithmetic and copies ran while one was open for 2% of the time, Pallas kernels for 2%

profile of v4, /device:TPU:0, one launch (start us, length us, event | category | flops | bytes accessed | tf_op | source)
XLA Modules:
  0.0 63.8 jit_solution(6702808535431347675)
XLA Ops:
  0.0 1.0 %copy-done = bf16[3,1,256,256]{3,2,1,0:T(8,128)(2,1)S(1)} copy-done((bf16[3,1,256,256]{3,2,1,0:T(8,128)(2,1)S(1)}, bf16[3,1,256,256]{3,2,1,0:T(8,128)(2,1)}, u32[]{:S(2)}) %copy-start) | copy-done | bytes 393240
  1.0 0.9 %copy-done.2 = bf16[3,1,64,256]{3,2,1,0:T(8,128)(2,1)S(1)} copy-done((bf16[3,1,64,256]{3,2,1,0:T(8,128)(2,1)S(1)}, bf16[3,1,64,256]{3,2,1,0:T(8,128)(2,1)}, u32[]{:S(2)}) %copy-start.2) | copy-done | bytes 98328
  1.9 0.2 shard_map.46
  2.1 5.1 %collective-permute-start.2 = (bf16[64,256]{1,0:T(8,128)(2,1)S(1)}, bf16[64,256]{1,0:T(8,128)(2,1)S(1)}, u32[]{:S(2)}, u32[]{:S(2)}) collective-permute-start(bf16[64,256]{1,0:T(8,128)(2,1)S(1)} %get-tuple-element.16), channel_id=1, source_target_pairs={{0,24},{4,28},{8,16},{12,20},{16,8},{20,12},{24,0},{28,4},{1,25},{... | collective-permute-start | bytes 98312 | tf_op jit(solution)/shard_map/ppermute | solution.py:23
  7.2 0.0 collective-permute-start.1
  7.2 0.6 %collective-permute-start = (bf16[64,256]{1,0:T(8,128)(2,1)S(1)}, bf16[64,256]{1,0:T(8,128)(2,1)S(1)}, u32[]{:S(2)}, u32[]{:S(2)}) collective-permute-start(bf16[64,256]{1,0:T(8,128)(2,1)S(1)} %get-tuple-element.16), channel_id=1, source_target_pairs={{0,8},{4,12},{8,0},{12,4},{16,24},{20,28},{24,16},{28,20},{1,9},{5... | collective-permute-start | bytes 98312 | tf_op jit(solution)/shard_map/ppermute | solution.py:23
  7.9 1.0 %slice_bitcast_fusion.1.raw = bf16[2,256,256]{2,1,0:T(8,128)(2,1)S(1)} fusion(bf16[2,1,2,256,256]{4,3,2,1,0:T(8,128)(2,1)} %param.6), kind=kLoop, calls=%fused_computation.3 | loop fusion | bytes 524288 | tf_op jit(solution)/shard_map/squeeze | solution.py:171
  8.8 0.0 copy-done.4
  8.8 0.2 shard_map.47.refs_0_.refs_4_
  9.0 2.7 %collective-permute-start.4 = (bf16[2,256,256]{2,1,0:T(8,128)(2,1)S(1)}, bf16[2,256,256]{2,1,0:T(8,128)(2,1)S(1)}, u32[]{:S(2)}, u32[]{:S(2)}) collective-permute-start(bf16[2,256,256]{2,1,0:T(8,128)(2,1)S(1)} %shard_map.47.refs_0_.refs_4_), channel_id=1, source_target_pairs={{0,3},{1,2},{2,1},{3,0},{4,7},{5,6},{6,5},{7,4},{8,11},{9,10},{10,... | collective-permute-start | bytes 786440 | tf_op jit(solution)/shard_map/ppermute | solution.py:23
  11.7 0.5 collective-permute-start.6
  12.2 0.0 collective-permute-done.2
  12.2 0.4 collective-permute-start.5
  12.6 0.0 collective-permute-done.1
  12.6 0.0 collective-permute-done
  12.6 0.0 copy-start.1
  12.6 0.0 copy-start.3
  12.7 0.1 collective-permute-start.3
  12.7 1.3 %collective-permute-done.3.far = bf16[4,64,256]{2,1,0:T(8,128)(2,1)S(1)} collective-permute-done((bf16[4,64,256]{2,1,0:T(8,128)(2,1)S(1)}, bf16[4,64,256]{2,1,0:T(8,128)(2,1)S(1)}, u32[]{:S(2)}, u32[]{:S(2)}) %collective-permute-start.3) | collective-permute-done | bytes 131104 | tf_op jit(solution)/shard_map/ppermute | solution.py:23
  14.1 5.2 %collective-permute-done.4.refs_1_.refs_7_.refs_3_ = bf16[2,256,256]{2,1,0:T(8,128)(2,1)S(1)} collective-permute-done((bf16[2,256,256]{2,1,0:T(8,128)(2,1)S(1)}, bf16[2,256,256]{2,1,0:T(8,128)(2,1)S(1)}, u32[]{:S(2)}, u32[]{:S(2)}) %collective-permute-start.4) | collective-permute-done | bytes 262176 | tf_op jit(solution)/shard_map/ppermute | solution.py:23
  19.2 0.3 shard_map.48.part
  19.5 0.0 copy-start.5
  19.5 3.7 %collective-permute-done.6.refs_1_.refs_5_ = bf16[2,256,256]{2,1,0:T(8,128)(2,1)S(1)} collective-permute-done((bf16[2,256,256]{2,1,0:T(8,128)(2,1)S(1)}, bf16[2,256,256]{2,1,0:T(8,128)(2,1)S(1)}, u32[]{:S(2)}, u32[]{:S(2)}) %collective-permute-start.6) | collective-permute-done | bytes 262176 | tf_op jit(solution)/shard_map/ppermute | solution.py:23
  23.2 0.0 collective-permute-done.5.refs_0_.refs_6_.refs_2_
  23.2 0.0 copy-done.3
  23.2 0.5 shard_map.49
  23.7 3.5 %collective-permute-start.9 = (bf16[64,256]{1,0:T(8,128)(2,1)S(1)}, bf16[64,256]{1,0:T(8,128)(2,1)S(1)}, u32[]{:S(2)}, u32[]{:S(2)}) collective-permute-start(bf16[64,256]{1,0:T(8,128)(2,1)S(1)} %get-tuple-element.17), channel_id=1, source_target_pairs={{0,24},{4,28},{8,16},{12,20},{16,8},{20,12},{24,0},{28,4},{1,25},{... | collective-permute-start | bytes 98312 | tf_op jit(solution)/shard_map/ppermute | solution.py:23
  27.2 0.0 collective-permute-start.8
  27.2 0.9 %collective-permute-start.7 = (bf16[64,256]{1,0:T(8,128)(2,1)S(1)}, bf16[64,256]{1,0:T(8,128)(2,1)S(1)}, u32[]{:S(2)}, u32[]{:S(2)}) collective-permute-start(bf16[64,256]{1,0:T(8,128)(2,1)S(1)} %get-tuple-element.17), channel_id=1, source_target_pairs={{0,8},{4,12},{8,0},{12,4},{16,24},{20,28},{24,16},{28,20},{1,9},{5... | collective-permute-start | bytes 98312 | tf_op jit(solution)/shard_map/ppermute | solution.py:23
  28.1 0.0 copy-done.5
  28.2 0.2 shard_map.50.refs_0_
  28.4 1.6 %collective-permute-start.11 = (bf16[2,256,256]{2,1,0:T(8,128)(2,1)S(1)}, bf16[2,256,256]{2,1,0:T(8,128)(2,1)S(1)}, u32[]{:S(2)}, u32[]{:S(2)}) collective-permute-start(bf16[2,256,256]{2,1,0:T(8,128)(2,1)S(1)} %shard_map.50.refs_0_), channel_id=1, source_target_pairs={{0,1},{1,0},{2,3},{3,2},{4,5},{5,4},{6,7},{7,6},{8,9},{9,8},{10,11... | collective-permute-start | bytes 786440 | tf_op jit(solution)/shard_map/ppermute | solution.py:23
  29.9 1.4 %collective-permute-start.13 = (bf16[2,256,256]{2,1,0:T(8,128)(2,1)S(1)}, bf16[2,256,256]{2,1,0:T(8,128)(2,1)S(1)}, u32[]{:S(2)}, u32[]{:S(2)}) collective-permute-start(bf16[2,256,256]{2,1,0:T(8,128)(2,1)S(1)} %shard_map.50.refs_0_), channel_id=1, source_target_pairs={{0,3},{1,2},{2,1},{3,0},{4,7},{5,6},{6,5},{7,4},{8,11},{9,10},{10,... | collective-permute-start | bytes 786440 | tf_op jit(solution)/shard_map/ppermute | solution.py:23
  31.3 0.0 collective-permute-done.9
  31.3 0.6 collective-permute-start.12
  31.9 0.1 collective-permute-done.8
  32.0 0.0 collective-permute-done.7
  32.1 0.1 collective-permute-start.10
  32.1 5.5 %collective-permute-done.11.refs_1_ = bf16[2,256,256]{2,1,0:T(8,128)(2,1)S(1)} collective-permute-done((bf16[2,256,256]{2,1,0:T(8,128)(2,1)S(1)}, bf16[2,256,256]{2,1,0:T(8,128)(2,1)S(1)}, u32[]{:S(2)}, u32[]{:S(2)}) %collective-permute-start.11) | collective-permute-done | bytes 262176 | tf_op jit(solution)/shard_map/ppermute | solution.py:23
  37.6 0.0 collective-permute-done.10.far
  37.6 0.3 shard_map.51.part
  37.9 4.5 %collective-permute-done.13.refs_3_ = bf16[2,256,256]{2,1,0:T(8,128)(2,1)S(1)} collective-permute-done((bf16[2,256,256]{2,1,0:T(8,128)(2,1)S(1)}, bf16[2,256,256]{2,1,0:T(8,128)(2,1)S(1)}, u32[]{:S(2)}, u32[]{:S(2)}) %collective-permute-start.13) | collective-permute-done | bytes 262176 | tf_op jit(solution)/shard_map/ppermute | solution.py:23
  42.4 1.4 %collective-permute-done.12.refs_2_ = bf16[2,256,256]{2,1,0:T(8,128)(2,1)S(1)} collective-permute-done((bf16[2,256,256]{2,1,0:T(8,128)(2,1)S(1)}, bf16[2,256,256]{2,1,0:T(8,128)(2,1)S(1)}, u32[]{:S(2)}, u32[]{:S(2)}) %collective-permute-start.12) | collective-permute-done | bytes 262176 | tf_op jit(solution)/shard_map/ppermute | solution.py:23
  43.8 0.9 %shard_map.52 = (f32[64,256]{1,0:T(8,128)S(1)}, bf16[64,256]{1,0:T(8,128)(2,1)S(1)}, bf16[4,64,256]{2,1,0:T(8,128)(2,1)S(1)}) custom-call(f32[64,256]{1,0:T(8,128)S(1)} %shard_map.51.part, bf16[4,64,256]{2,1,0:T(8,128)(2,1)S(1)} %pad_maximum_fusion.1.near, bf16[4,64,256]{2,1,0:T(8,128)(2,1)S(1)} %collective-permute-done.10.far, ...), custom_call_target="tpu_custom_call" | custom-call | tf_op jit(solution)/shard_map/pallas_call | solution.py:142
  44.6 0.1 collective-permute-start.14
  44.7 0.2 shard_map.53
  44.9 1.1 %collective-permute-done.14 = bf16[4,64,256]{2,1,0:T(8,128)(2,1)S(1)} collective-permute-done((bf16[4,64,256]{2,1,0:T(8,128)(2,1)S(1)}, bf16[4,64,256]{2,1,0:T(8,128)(2,1)S(1)}, u32[]{:S(2)}, u32[]{:S(2)}) %collective-permute-start.14) | collective-permute-done | bytes 131104 | tf_op jit(solution)/shard_map/ppermute | solution.py:23
  46.1 3.5 %collective-permute-start.17 = (bf16[64,256]{1,0:T(8,128)(2,1)S(1)}, bf16[64,256]{1,0:T(8,128)(2,1)S(1)}, u32[]{:S(2)}, u32[]{:S(2)}) collective-permute-start(bf16[64,256]{1,0:T(8,128)(2,1)S(1)} %get-tuple-element.34), channel_id=1, source_target_pairs={{0,24},{4,28},{8,16},{12,20},{16,8},{20,12},{24,0},{28,4},{1,25},{... | collective-permute-start | bytes 98312 | tf_op jit(solution)/shard_map/ppermute | solution.py:23
  49.6 0.0 collective-permute-start.16
  49.6 0.9 %collective-permute-start.15 = (bf16[64,256]{1,0:T(8,128)(2,1)S(1)}, bf16[64,256]{1,0:T(8,128)(2,1)S(1)}, u32[]{:S(2)}, u32[]{:S(2)}) collective-permute-start(bf16[64,256]{1,0:T(8,128)(2,1)S(1)} %get-tuple-element.36), channel_id=1, source_target_pairs={{0,8},{4,12},{8,0},{12,4},{16,24},{20,28},{24,16},{28,20},{1,9},{5... | collective-permute-start | bytes 98312 | tf_op jit(solution)/shard_map/ppermute | solution.py:23
  50.6 1.4 %collective-permute-done.17.refs_3_ = bf16[64,256]{1,0:T(8,128)(2,1)S(1)} collective-permute-done((bf16[64,256]{1,0:T(8,128)(2,1)S(1)}, bf16[64,256]{1,0:T(8,128)(2,1)S(1)}, u32[]{:S(2)}, u32[]{:S(2)}) %collective-permute-start.17) | collective-permute-done | bytes 32800 | tf_op jit(solution)/shard_map/ppermute | solution.py:23
  51.9 2.5 %collective-permute-done.16.refs_2_ = bf16[64,256]{1,0:T(8,128)(2,1)S(1)} collective-permute-done((bf16[64,256]{1,0:T(8,128)(2,1)S(1)}, bf16[64,256]{1,0:T(8,128)(2,1)S(1)}, u32[]{:S(2)}, u32[]{:S(2)}) %collective-permute-start.16) | collective-permute-done | bytes 32800 | tf_op jit(solution)/shard_map/ppermute | solution.py:23
  54.4 0.0 collective-permute-done.15.refs_1_
  54.4 0.3 shard_map.54
  54.8 0.1 collective-permute-start.18
  54.9 0.2 shard_map.55
  55.1 1.1 %collective-permute-done.18 = bf16[4,64,256]{2,1,0:T(8,128)(2,1)S(1)} collective-permute-done((bf16[4,64,256]{2,1,0:T(8,128)(2,1)S(1)}, bf16[4,64,256]{2,1,0:T(8,128)(2,1)S(1)}, u32[]{:S(2)}, u32[]{:S(2)}) %collective-permute-start.18) | collective-permute-done | bytes 131104 | tf_op jit(solution)/shard_map/ppermute | solution.py:23
  56.2 1.5 %collective-permute-start.21 = (bf16[64,256]{1,0:T(8,128)(2,1)S(1)}, bf16[64,256]{1,0:T(8,128)(2,1)S(1)}, u32[]{:S(2)}, u32[]{:S(2)}) collective-permute-start(bf16[64,256]{1,0:T(8,128)(2,1)S(1)} %get-tuple-element.31), channel_id=1, source_target_pairs={{0,24},{4,28},{8,16},{12,20},{16,8},{20,12},{24,0},{28,4},{1,25},{... | collective-permute-start | bytes 98312 | tf_op jit(solution)/shard_map/ppermute | solution.py:23
  57.8 0.6 collective-permute-start.20
  58.4 2.3 %collective-permute-start.19 = (bf16[64,256]{1,0:T(8,128)(2,1)S(1)}, bf16[64,256]{1,0:T(8,128)(2,1)S(1)}, u32[]{:S(2)}, u32[]{:S(2)}) collective-permute-start(bf16[64,256]{1,0:T(8,128)(2,1)S(1)} %get-tuple-element.33), channel_id=1, source_target_pairs={{0,8},{4,12},{8,0},{12,4},{16,24},{20,28},{24,16},{28,20},{1,9},{5... | collective-permute-start | bytes 98312 | tf_op jit(solution)/shard_map/ppermute | solution.py:23
  60.7 1.6 %collective-permute-done.21.refs_3_ = bf16[64,256]{1,0:T(8,128)(2,1)S(1)} collective-permute-done((bf16[64,256]{1,0:T(8,128)(2,1)S(1)}, bf16[64,256]{1,0:T(8,128)(2,1)S(1)}, u32[]{:S(2)}, u32[]{:S(2)}) %collective-permute-start.21) | collective-permute-done | bytes 32800 | tf_op jit(solution)/shard_map/ppermute | solution.py:23
  62.4 0.4 collective-permute-done.20.refs_2_
  62.7 0.3 collective-permute-done.19.refs_1_
  63.0 0.8 %shard_map.56 = f32[3,1,64,256]{3,2,1,0:T(8,128)} custom-call(f32[64,256]{1,0:T(8,128)S(1)} %slice_bitcast_fusion.2.refs_0_, bf16[64,256]{1,0:T(8,128)(2,1)S(1)} %collective-permute-done.19.refs_1_, bf16[64,256]{1,0:T(8,128)(2,1)S(1)} %collective-permute-done.20.refs_2_, bf16[64,256]{1,0:T(8,128)(2,1)S(1)} %collective-permute-done.21.refs_3_, ...), custom_call_target="tpu_custom_call" | custom-call | tf_op jit(solution)/shard_map/pallas_call | solution.py:142
  (13 shorter events, 0.2 us)
Async XLA Ops:
  0.0 1.0 %copy-start = (bf16[3,1,256,256]{3,2,1,0:T(8,128)(2,1)S(1)}, bf16[3,1,256,256]{3,2,1,0:T(8,128)(2,1)}, u32[]{:S(2)}) copy-start(bf16[3,1,256,256]{3,2,1,0:T(8,128)(2,1)} %refs_5_.3) | copy-start | bytes 1179652
  1.0 0.9 %copy-start.2 = (bf16[3,1,64,256]{3,2,1,0:T(8,128)(2,1)S(1)}, bf16[3,1,64,256]{3,2,1,0:T(8,128)(2,1)}, u32[]{:S(2)}) copy-start(bf16[3,1,64,256]{3,2,1,0:T(8,128)(2,1)} %refs_4_.1) | copy-start | bytes 294916
  2.0 6.8 %copy-start.4 = (s32[2,2,1,2]{3,2,1,0:T(1,128)S(1)}, s32[2,2,1,2]{3,2,1,0:T(1,128)}, u32[]{:S(2)}) copy-start(s32[2,2,1,2]{3,2,1,0:T(1,128)} %pattern.3) | copy-start | bytes 100
  2.1 10.2 %collective-permute-start.2 = (bf16[64,256]{1,0:T(8,128)(2,1)S(1)}, bf16[64,256]{1,0:T(8,128)(2,1)S(1)}, u32[]{:S(2)}, u32[]{:S(2)}) collective-permute-start(bf16[64,256]{1,0:T(8,128)(2,1)S(1)} %get-tuple-element.16), channel_id=1, source_target_pairs={{0,24},{4,28},{8,16},{12,20},{16,8},{20,12},{24,0},{28,4},{1,25},{... | collective-permute-start | bytes 98312 | tf_op jit(solution)/shard_map/ppermute | solution.py:23
  7.2 5.4 %collective-permute-start.1 = (bf16[64,256]{1,0:T(8,128)(2,1)S(1)}, bf16[64,256]{1,0:T(8,128)(2,1)S(1)}, u32[]{:S(2)}, u32[]{:S(2)}) collective-permute-start(bf16[64,256]{1,0:T(8,128)(2,1)S(1)} %get-tuple-element.16), channel_id=1, source_target_pairs={{0,16},{4,20},{8,24},{12,28},{16,0},{20,4},{24,8},{28,12},{1,17},{... | collective-permute-start | bytes 98312 | tf_op jit(solution)/shard_map/ppermute | solution.py:23
  7.2 5.4 %collective-permute-start = (bf16[64,256]{1,0:T(8,128)(2,1)S(1)}, bf16[64,256]{1,0:T(8,128)(2,1)S(1)}, u32[]{:S(2)}, u32[]{:S(2)}) collective-permute-start(bf16[64,256]{1,0:T(8,128)(2,1)S(1)} %get-tuple-element.16), channel_id=1, source_target_pairs={{0,8},{4,12},{8,0},{12,4},{16,24},{20,28},{24,16},{28,20},{1,9},{5... | collective-permute-start | bytes 98312 | tf_op jit(solution)/shard_map/ppermute | solution.py:23
  9.0 10.2 %collective-permute-start.4 = (bf16[2,256,256]{2,1,0:T(8,128)(2,1)S(1)}, bf16[2,256,256]{2,1,0:T(8,128)(2,1)S(1)}, u32[]{:S(2)}, u32[]{:S(2)}) collective-permute-start(bf16[2,256,256]{2,1,0:T(8,128)(2,1)S(1)} %shard_map.47.refs_0_.refs_4_), channel_id=1, source_target_pairs={{0,3},{1,2},{2,1},{3,0},{4,7},{5,6},{6,5},{7,4},{8,11},{9,10},{10,... | collective-permute-start | bytes 786440 | tf_op jit(solution)/shard_map/ppermute | solution.py:23
  11.7 11.5 %collective-permute-start.6 = (bf16[2,256,256]{2,1,0:T(8,128)(2,1)S(1)}, bf16[2,256,256]{2,1,0:T(8,128)(2,1)S(1)}, u32[]{:S(2)}, u32[]{:S(2)}) collective-permute-start(bf16[2,256,256]{2,1,0:T(8,128)(2,1)S(1)} %shard_map.47.refs_0_.refs_4_), channel_id=1, source_target_pairs={{0,1},{1,0},{2,3},{3,2},{4,5},{5,4},{6,7},{7,6},{8,9},{9,8},{10,11... | collective-permute-start | bytes 786440 | tf_op jit(solution)/shard_map/ppermute | solution.py:23
  12.2 11.0 %collective-permute-start.5 = (bf16[2,256,256]{2,1,0:T(8,128)(2,1)S(1)}, bf16[2,256,256]{2,1,0:T(8,128)(2,1)S(1)}, u32[]{:S(2)}, u32[]{:S(2)}) collective-permute-start(bf16[2,256,256]{2,1,0:T(8,128)(2,1)S(1)} %shard_map.47.refs_0_.refs_4_), channel_id=1, source_target_pairs={{0,2},{1,3},{2,0},{3,1},{4,6},{5,7},{6,4},{7,5},{8,10},{9,11},{10,... | collective-permute-start | bytes 786440 | tf_op jit(solution)/shard_map/ppermute | solution.py:23
  12.6 10.6 %copy-start.1 = (bf16[3,1,256,256]{3,2,1,0:T(8,128)(2,1)S(1)}, bf16[3,1,256,256]{3,2,1,0:T(8,128)(2,1)}, u32[]{:S(2)}) copy-start(bf16[3,1,256,256]{3,2,1,0:T(8,128)(2,1)} %refs_5_.3) | copy-start | bytes 1179652
  12.6 10.6 %copy-start.3 = (bf16[3,1,64,256]{3,2,1,0:T(8,128)(2,1)S(1)}, bf16[3,1,64,256]{3,2,1,0:T(8,128)(2,1)}, u32[]{:S(2)}) copy-start(bf16[3,1,64,256]{3,2,1,0:T(8,128)(2,1)} %refs_4_.1) | copy-start | bytes 294916
  12.7 1.4 %collective-permute-start.3 = (bf16[4,64,256]{2,1,0:T(8,128)(2,1)S(1)}, bf16[4,64,256]{2,1,0:T(8,128)(2,1)S(1)}, u32[]{:S(2)}, u32[]{:S(2)}) collective-permute-start(bf16[4,64,256]{2,1,0:T(8,128)(2,1)S(1)} %pad_maximum_fusion.near), channel_id=1, source_target_pairs={{0,4},{4,0},{8,12},{12,8},{16,20},{20,16},{24,28},{28,24},{1,5},{5... | collective-permute-start | bytes 393224 | tf_op jit(solution)/shard_map/ppermute | solution.py:23
  19.5 8.6 %copy-start.5 = (bf16[2,1,2,256,256]{4,3,2,1,0:T(8,128)(2,1)S(1)}, bf16[2,1,2,256,256]{4,3,2,1,0:T(8,128)(2,1)}, u32[]{:S(2)}) copy-start(bf16[2,1,2,256,256]{4,3,2,1,0:T(8,128)(2,1)} %param.6) | copy-start | bytes 1572868
  23.7 7.6 %collective-permute-start.9 = (bf16[64,256]{1,0:T(8,128)(2,1)S(1)}, bf16[64,256]{1,0:T(8,128)(2,1)S(1)}, u32[]{:S(2)}, u32[]{:S(2)}) collective-permute-start(bf16[64,256]{1,0:T(8,128)(2,1)S(1)} %get-tuple-element.17), channel_id=1, source_target_pairs={{0,24},{4,28},{8,16},{12,20},{16,8},{20,12},{24,0},{28,4},{1,25},{... | collective-permute-start | bytes 98312 | tf_op jit(solution)/shard_map/ppermute | solution.py:23
  27.2 4.8 %collective-permute-start.8 = (bf16[64,256]{1,0:T(8,128)(2,1)S(1)}, bf16[64,256]{1,0:T(8,128)(2,1)S(1)}, u32[]{:S(2)}, u32[]{:S(2)}) collective-permute-start(bf16[64,256]{1,0:T(8,128)(2,1)S(1)} %get-tuple-element.17), channel_id=1, source_target_pairs={{0,16},{4,20},{8,24},{12,28},{16,0},{20,4},{24,8},{28,12},{1,17},{... | collective-permute-start | bytes 98312 | tf_op jit(solution)/shard_map/ppermute | solution.py:23
  27.2 4.8 %collective-permute-start.7 = (bf16[64,256]{1,0:T(8,128)(2,1)S(1)}, bf16[64,256]{1,0:T(8,128)(2,1)S(1)}, u32[]{:S(2)}, u32[]{:S(2)}) collective-permute-start(bf16[64,256]{1,0:T(8,128)(2,1)S(1)} %get-tuple-element.17), channel_id=1, source_target_pairs={{0,8},{4,12},{8,0},{12,4},{16,24},{20,28},{24,16},{28,20},{1,9},{5... | collective-permute-start | bytes 98312 | tf_op jit(solution)/shard_map/ppermute | solution.py:23
  28.4 9.2 %collective-permute-start.11 = (bf16[2,256,256]{2,1,0:T(8,128)(2,1)S(1)}, bf16[2,256,256]{2,1,0:T(8,128)(2,1)S(1)}, u32[]{:S(2)}, u32[]{:S(2)}) collective-permute-start(bf16[2,256,256]{2,1,0:T(8,128)(2,1)S(1)} %shard_map.50.refs_0_), channel_id=1, source_target_pairs={{0,1},{1,0},{2,3},{3,2},{4,5},{5,4},{6,7},{7,6},{8,9},{9,8},{10,11... | collective-permute-start | bytes 786440 | tf_op jit(solution)/shard_map/ppermute | solution.py:23
  29.9 12.5 %collective-permute-start.13 = (bf16[2,256,256]{2,1,0:T(8,128)(2,1)S(1)}, bf16[2,256,256]{2,1,0:T(8,128)(2,1)S(1)}, u32[]{:S(2)}, u32[]{:S(2)}) collective-permute-start(bf16[2,256,256]{2,1,0:T(8,128)(2,1)S(1)} %shard_map.50.refs_0_), channel_id=1, source_target_pairs={{0,3},{1,2},{2,1},{3,0},{4,7},{5,6},{6,5},{7,4},{8,11},{9,10},{10,... | collective-permute-start | bytes 786440 | tf_op jit(solution)/shard_map/ppermute | solution.py:23
  31.3 12.4 %collective-permute-start.12 = (bf16[2,256,256]{2,1,0:T(8,128)(2,1)S(1)}, bf16[2,256,256]{2,1,0:T(8,128)(2,1)S(1)}, u32[]{:S(2)}, u32[]{:S(2)}) collective-permute-start(bf16[2,256,256]{2,1,0:T(8,128)(2,1)S(1)} %shard_map.50.refs_0_), channel_id=1, source_target_pairs={{0,2},{1,3},{2,0},{3,1},{4,6},{5,7},{6,4},{7,5},{8,10},{9,11},{10,... | collective-permute-start | bytes 786440 | tf_op jit(solution)/shard_map/ppermute | solution.py:23
  32.1 5.6 %collective-permute-start.10 = (bf16[4,64,256]{2,1,0:T(8,128)(2,1)S(1)}, bf16[4,64,256]{2,1,0:T(8,128)(2,1)S(1)}, u32[]{:S(2)}, u32[]{:S(2)}) collective-permute-start(bf16[4,64,256]{2,1,0:T(8,128)(2,1)S(1)} %pad_maximum_fusion.1.near), channel_id=1, source_target_pairs={{0,4},{4,0},{8,12},{12,8},{16,20},{20,16},{24,28},{28,24},{1,5},{5... | collective-permute-start | bytes 393224 | tf_op jit(solution)/shard_map/ppermute | solution.py:23
  44.6 1.4 %collective-permute-start.14 = (bf16[4,64,256]{2,1,0:T(8,128)(2,1)S(1)}, bf16[4,64,256]{2,1,0:T(8,128)(2,1)S(1)}, u32[]{:S(2)}, u32[]{:S(2)}) collective-permute-start(bf16[4,64,256]{2,1,0:T(8,128)(2,1)S(1)} %get-tuple-element.20), channel_id=1, source_target_pairs={{0,4},{4,0},{8,12},{12,8},{16,20},{20,16},{24,28},{28,24},{1,5},{5... | collective-permute-start | bytes 393224 | tf_op jit(solution)/shard_map/ppermute | solution.py:23
  46.1 5.8 %collective-permute-start.17 = (bf16[64,256]{1,0:T(8,128)(2,1)S(1)}, bf16[64,256]{1,0:T(8,128)(2,1)S(1)}, u32[]{:S(2)}, u32[]{:S(2)}) collective-permute-start(bf16[64,256]{1,0:T(8,128)(2,1)S(1)} %get-tuple-element.34), channel_id=1, source_target_pairs={{0,24},{4,28},{8,16},{12,20},{16,8},{20,12},{24,0},{28,4},{1,25},{... | collective-permute-start | bytes 98312 | tf_op jit(solution)/shard_map/ppermute | solution.py:23
  49.6 4.8 %collective-permute-start.16 = (bf16[64,256]{1,0:T(8,128)(2,1)S(1)}, bf16[64,256]{1,0:T(8,128)(2,1)S(1)}, u32[]{:S(2)}, u32[]{:S(2)}) collective-permute-start(bf16[64,256]{1,0:T(8,128)(2,1)S(1)} %get-tuple-element.35), channel_id=1, source_target_pairs={{0,16},{4,20},{8,24},{12,28},{16,0},{20,4},{24,8},{28,12},{1,17},{... | collective-permute-start | bytes 98312 | tf_op jit(solution)/shard_map/ppermute | solution.py:23
  49.6 4.8 %collective-permute-start.15 = (bf16[64,256]{1,0:T(8,128)(2,1)S(1)}, bf16[64,256]{1,0:T(8,128)(2,1)S(1)}, u32[]{:S(2)}, u32[]{:S(2)}) collective-permute-start(bf16[64,256]{1,0:T(8,128)(2,1)S(1)} %get-tuple-element.36), channel_id=1, source_target_pairs={{0,8},{4,12},{8,0},{12,4},{16,24},{20,28},{24,16},{28,20},{1,9},{5... | collective-permute-start | bytes 98312 | tf_op jit(solution)/shard_map/ppermute | solution.py:23
  54.8 1.4 %collective-permute-start.18 = (bf16[4,64,256]{2,1,0:T(8,128)(2,1)S(1)}, bf16[4,64,256]{2,1,0:T(8,128)(2,1)S(1)}, u32[]{:S(2)}, u32[]{:S(2)}) collective-permute-start(bf16[4,64,256]{2,1,0:T(8,128)(2,1)S(1)} %get-tuple-element.23), channel_id=1, source_target_pairs={{0,4},{4,0},{8,12},{12,8},{16,20},{20,16},{24,28},{28,24},{1,5},{5... | collective-permute-start | bytes 393224 | tf_op jit(solution)/shard_map/ppermute | solution.py:23
  56.2 6.1 %collective-permute-start.21 = (bf16[64,256]{1,0:T(8,128)(2,1)S(1)}, bf16[64,256]{1,0:T(8,128)(2,1)S(1)}, u32[]{:S(2)}, u32[]{:S(2)}) collective-permute-start(bf16[64,256]{1,0:T(8,128)(2,1)S(1)} %get-tuple-element.31), channel_id=1, source_target_pairs={{0,24},{4,28},{8,16},{12,20},{16,8},{20,12},{24,0},{28,4},{1,25},{... | collective-permute-start | bytes 98312 | tf_op jit(solution)/shard_map/ppermute | solution.py:23
  57.8 4.9 %collective-permute-start.20 = (bf16[64,256]{1,0:T(8,128)(2,1)S(1)}, bf16[64,256]{1,0:T(8,128)(2,1)S(1)}, u32[]{:S(2)}, u32[]{:S(2)}) collective-permute-start(bf16[64,256]{1,0:T(8,128)(2,1)S(1)} %get-tuple-element.32), channel_id=1, source_target_pairs={{0,16},{4,20},{8,24},{12,28},{16,0},{20,4},{24,8},{28,12},{1,17},{... | collective-permute-start | bytes 98312 | tf_op jit(solution)/shard_map/ppermute | solution.py:23
  58.4 4.6 %collective-permute-start.19 = (bf16[64,256]{1,0:T(8,128)(2,1)S(1)}, bf16[64,256]{1,0:T(8,128)(2,1)S(1)}, u32[]{:S(2)}, u32[]{:S(2)}) collective-permute-start(bf16[64,256]{1,0:T(8,128)(2,1)S(1)} %get-tuple-element.33), channel_id=1, source_target_pairs={{0,8},{4,12},{8,0},{12,4},{16,24},{20,28},{24,16},{28,20},{1,9},{5... | collective-permute-start | bytes 98312 | tf_op jit(solution)/shard_map/ppermute | solution.py:23

commit v5 on v3

--- a/solution.py
+++ b/solution.py
@@ -67,6 +67,17 @@
     out_b[...] = solved.astype(BF16)
 
 
+def pick_kernel(level, cols, pattern, raw, own):
+    shape = own.shape[1:]
+    for group in range(own.shape[0]):
+        total = jnp.zeros(shape, F32)
+        for slot in range(raw.shape[0]):
+            place = jnp.broadcast_to(pattern[1, level, :, slot : slot + 1], shape)
+            here = (place >= cols * group) & (place < cols * (group + 1))
+            total = total + jnp.where(here, raw[slot].astype(F32), 0.0)
+        own[group] = total.astype(BF16)
+
+
 def early_kernel(repeat, cols, steps, near, far, *refs):
     refs[-1][...] = update(near, far, refs[:-1], steps, repeat, cols)
 
@@ -118,19 +129,28 @@
     arrived = refs[:count]
     forward, dinv = refs[count : count + 2]
     upper = refs[count + 2 : count + 2 + upper_count]
-    out = refs[-1]
+    out, held, sems = refs[count + 2 + upper_count :]
+    copies = [
+        pltpu.make_async_copy(ref, out.at[index + 1, 0], sems.at[index + 1])
+        for index, ref in enumerate(upper)
+    ]
+    for copy in copies:
+        copy.start()
     rest = forward[...] - remainder(count, arrived)
-    out[0, 0] = dot_n(rest.astype(BF16), dinv[0, 0])
-    for index, ref in enumerate(upper):
-        out[index + 1, 0] = ref[...]
-
-
-def call(kernel, outs, scratch, *args):
+    held[...] = dot_n(rest.astype(BF16), dinv[0, 0])
+    final = pltpu.make_async_copy(held, out.at[0, 0], sems.at[0])
+    final.start()
+    for copy in copies:
+        copy.wait()
+    final.wait()
+
+
+def call(kernel, outs, scratch, *args, out_space=pltpu.VMEM):
     return pl.pallas_call(
         kernel,
         out_shape=outs,
         in_specs=[pl.BlockSpec(memory_space=pltpu.VMEM)] * len(args),
-        out_specs=jax.tree.map(lambda _: pl.BlockSpec(memory_space=pltpu.VMEM), outs),
+        out_specs=jax.tree.map(lambda _: pl.BlockSpec(memory_space=out_space), outs),
         scratch_shapes=scratch,
         compiler_params=pltpu.CompilerParams(vmem_limit_bytes=VMEM_LIMIT),
     )(*args)
@@ -150,12 +170,13 @@
     chip_segs_b = jax.ShapeDtypeStruct((chips, nrhs, bs), BF16)
 
     def gathered_tiles(level, after):
-        groups = jnp.arange(repeat, dtype=jnp.int32)[:, None, None, None]
-        raw, slots = tiles[level, 0], pattern[1, level, 0]
+        source = tiles
         if after is not None:
-            raw, slots, _ = lax.optimization_barrier((raw, slots, after))
-        here = (slots // cols)[None, :, None, None] == groups
-        own = jnp.sum(jnp.where(here, raw[None].astype(F32), 0.0), axis=1).astype(BF16)
+            source, _ = lax.optimization_barrier((tiles, after))
+        own = call(
+            functools.partial(pick_kernel, level, cols),
+            jax.ShapeDtypeStruct((repeat, bs, bs), BF16), [], pattern, source[level, 0],
+        )
         found = [own] + [None] * (cols - 1)
         for step in send_order(cols):
             found[step] = swap(own, "col", cols, step)
@@ -218,7 +239,9 @@
     arrived = scatter(solved_b, send, found_tiles)
     return call(
         functools.partial(last_kernel, chips, len(upper)),
-        jax.ShapeDtypeStruct(rhs.shape, F32), [], *arrived, forwards[0], dinv, *upper,
+        jax.ShapeDtypeStruct(rhs.shape, F32),
+        [pltpu.VMEM((nrhs, bs), F32), pltpu.SemaphoreType.DMA((levels,))],
+        *arrived, forwards[0], dinv, *upper, out_space=pl.ANY,
     )
 
 

time: 61 us -> 62.6 us (1.026)
  waiting for transfers between devices: 26.9 us -> 28.6 us
  other arithmetic: 1.55 us -> 0.11 us
  local copies, waits for them, and re-layouts: 1.93 us -> 2.92 us
    ppermute x22, waiting for transfers between devices: 26.9 us -> 28.6 us  [swap(): return lax.ppermute(value, axis, [(i, i ^ mask) for i in range(size)])]
    squeeze x1 -> x0, other arithmetic: 1.09 us -> none  [gathered_tiles(): raw, slots = (tiles[level, 0], pattern[1, level, 0])]
    squeeze x1 -> x2, local copies, waits for them, and re-layouts: 0.01 us -> 0.98 us  [gathered_tiles(): source[level, 0]]
    pallas_call x9 -> x11, Pallas kernels: 3.66 us -> 4.03 us  [call(): pl.pallas_call(kernel, out_shape=outs, in_specs=[pl.BlockSpec(memory_spac...]
    unnamed x8 -> x12, local copies, waits for them, and re-layouts: 1.9 us -> 1.91 us
  transfers between devices with their start and end apart: 22 -> 22, of which waited for: 12 -> 14; matrix products, arithmetic and copies ran while one was open for 2% -> 2% of each run, Pallas kernels for 2% -> 2%
where the time goes in v5:
time: 62.6 us; the launch traced here: 62.4 us
  waiting for transfers between devices  28.6 us (46%)
  starting transfers between devices  26.5 us (42%)
  Pallas kernels  4.03 us (6%)
  local copies, waits for them, and re-layouts  2.92 us (5%)
    ppermute x22, waiting for transfers between devices, swap(): return lax.ppermute(value, axis, [(i, i ^ mask) for i in range(size)])  28.6 us
    ppermute x22, starting transfers between devices, swap(): return lax.ppermute(value, axis, [(i, i ^ mask) for i in range(size)])  26.5 us
    pallas_call x11, Pallas kernels, call(): pl.pallas_call(kernel, out_shape=outs, in_specs=[pl.BlockSpec(memory_spac...  4.03 us
    unnamed x12, local copies, waits for them, and re-layouts  1.91 us
  transfers between devices with their start and end apart: 22, of which 14 were waited for; matrix products, arithmetic and copies ran while one was open for 2% of the time, Pallas kernels for 2%

profile of v5, /device:TPU:0, one launch (start us, length us, event | category | flops | bytes accessed | tf_op | source)
XLA Modules:
  0.0 62.4 jit_solution(3391643058547365218)
XLA Ops:
  0.0 1.0 %copy-done = bf16[3,1,256,256]{3,2,1,0:T(8,128)(2,1)S(1)} copy-done((bf16[3,1,256,256]{3,2,1,0:T(8,128)(2,1)S(1)}, bf16[3,1,256,256]{3,2,1,0:T(8,128)(2,1)}, u32[]{:S(2)}) %copy-start) | copy-done | bytes 393240
  1.0 0.9 %copy-done.2 = bf16[3,1,64,256]{3,2,1,0:T(8,128)(2,1)S(1)} copy-done((bf16[3,1,64,256]{3,2,1,0:T(8,128)(2,1)S(1)}, bf16[3,1,64,256]{3,2,1,0:T(8,128)(2,1)}, u32[]{:S(2)}) %copy-start.2) | copy-done | bytes 98328
  1.9 0.2 shard_map.46
  2.1 5.1 %collective-permute-start.2 = (bf16[64,256]{1,0:T(8,128)(2,1)S(1)}, bf16[64,256]{1,0:T(8,128)(2,1)S(1)}, u32[]{:S(2)}, u32[]{:S(2)}) collective-permute-start(bf16[64,256]{1,0:T(8,128)(2,1)S(1)} %get-tuple-element.16), channel_id=1, source_target_pairs={{0,24},{4,28},{8,16},{12,20},{16,8},{20,12},{24,0},{28,4},{1,25},{... | collective-permute-start | bytes 98312 | tf_op jit(solution)/shard_map/ppermute | solution.py:21
  7.2 0.0 collective-permute-start.1
  7.2 0.6 %collective-permute-start = (bf16[64,256]{1,0:T(8,128)(2,1)S(1)}, bf16[64,256]{1,0:T(8,128)(2,1)S(1)}, u32[]{:S(2)}, u32[]{:S(2)}) collective-permute-start(bf16[64,256]{1,0:T(8,128)(2,1)S(1)} %get-tuple-element.16), channel_id=1, source_target_pairs={{0,8},{4,12},{8,0},{12,4},{16,24},{20,28},{24,16},{28,20},{1,9},{5... | collective-permute-start | bytes 98312 | tf_op jit(solution)/shard_map/ppermute | solution.py:21
  7.9 1.0 %slice_bitcast_fusion.1.raw = bf16[2,256,256]{2,1,0:T(8,128)(2,1)S(1)} fusion(bf16[2,1,2,256,256]{4,3,2,1,0:T(8,128)(2,1)} %param.6), kind=kLoop, calls=%fused_computation.3 | loop fusion | bytes 524288 | tf_op jit(solution)/shard_map/squeeze | solution.py:178
  8.8 0.0 copy-done.4
  8.8 0.2 shard_map.47.refs_0_.refs_4_
  9.0 2.7 %collective-permute-start.4 = (bf16[2,256,256]{2,1,0:T(8,128)(2,1)S(1)}, bf16[2,256,256]{2,1,0:T(8,128)(2,1)S(1)}, u32[]{:S(2)}, u32[]{:S(2)}) collective-permute-start(bf16[2,256,256]{2,1,0:T(8,128)(2,1)S(1)} %shard_map.47.refs_0_.refs_4_), channel_id=1, source_target_pairs={{0,3},{1,2},{2,1},{3,0},{4,7},{5,6},{6,5},{7,4},{8,11},{9,10},{10,... | collective-permute-start | bytes 786440 | tf_op jit(solution)/shard_map/ppermute | solution.py:21
  11.7 0.5 collective-permute-start.6
  12.2 0.0 collective-permute-done.2
  12.2 0.4 collective-permute-start.5
  12.6 0.0 collective-permute-done.1
  12.6 0.0 collective-permute-done
  12.6 0.0 copy-start.1
  12.6 0.0 copy-start.3
  12.7 0.1 collective-permute-start.3
  12.7 1.3 %collective-permute-done.3.far = bf16[4,64,256]{2,1,0:T(8,128)(2,1)S(1)} collective-permute-done((bf16[4,64,256]{2,1,0:T(8,128)(2,1)S(1)}, bf16[4,64,256]{2,1,0:T(8,128)(2,1)S(1)}, u32[]{:S(2)}, u32[]{:S(2)}) %collective-permute-start.3) | collective-permute-done | bytes 131104 | tf_op jit(solution)/shard_map/ppermute | solution.py:21
  14.1 5.2 %collective-permute-done.4.refs_1_.refs_7_.refs_3_ = bf16[2,256,256]{2,1,0:T(8,128)(2,1)S(1)} collective-permute-done((bf16[2,256,256]{2,1,0:T(8,128)(2,1)S(1)}, bf16[2,256,256]{2,1,0:T(8,128)(2,1)S(1)}, u32[]{:S(2)}, u32[]{:S(2)}) %collective-permute-start.4) | collective-permute-done | bytes 262176 | tf_op jit(solution)/shard_map/ppermute | solution.py:21
  19.2 0.3 shard_map.48.part
  19.5 0.0 copy-start.5
  19.5 3.7 %collective-permute-done.6.refs_1_.refs_5_ = bf16[2,256,256]{2,1,0:T(8,128)(2,1)S(1)} collective-permute-done((bf16[2,256,256]{2,1,0:T(8,128)(2,1)S(1)}, bf16[2,256,256]{2,1,0:T(8,128)(2,1)S(1)}, u32[]{:S(2)}, u32[]{:S(2)}) %collective-permute-start.6) | collective-permute-done | bytes 262176 | tf_op jit(solution)/shard_map/ppermute | solution.py:21
  23.2 0.0 collective-permute-done.5.refs_0_.refs_6_.refs_2_
  23.2 0.0 copy-done.3
  23.2 0.5 shard_map.49
  23.7 3.5 %collective-permute-start.9 = (bf16[64,256]{1,0:T(8,128)(2,1)S(1)}, bf16[64,256]{1,0:T(8,128)(2,1)S(1)}, u32[]{:S(2)}, u32[]{:S(2)}) collective-permute-start(bf16[64,256]{1,0:T(8,128)(2,1)S(1)} %get-tuple-element.17), channel_id=1, source_target_pairs={{0,24},{4,28},{8,16},{12,20},{16,8},{20,12},{24,0},{28,4},{1,25},{... | collective-permute-start | bytes 98312 | tf_op jit(solution)/shard_map/ppermute | solution.py:21
  27.2 0.0 collective-permute-start.8
  27.2 0.9 %collective-permute-start.7 = (bf16[64,256]{1,0:T(8,128)(2,1)S(1)}, bf16[64,256]{1,0:T(8,128)(2,1)S(1)}, u32[]{:S(2)}, u32[]{:S(2)}) collective-permute-start(bf16[64,256]{1,0:T(8,128)(2,1)S(1)} %get-tuple-element.17), channel_id=1, source_target_pairs={{0,8},{4,12},{8,0},{12,4},{16,24},{20,28},{24,16},{28,20},{1,9},{5... | collective-permute-start | bytes 98312 | tf_op jit(solution)/shard_map/ppermute | solution.py:21
  28.1 0.0 copy-done.5
  28.2 0.2 shard_map.50.refs_0_
  28.4 2.4 %collective-permute-start.11 = (bf16[2,256,256]{2,1,0:T(8,128)(2,1)S(1)}, bf16[2,256,256]{2,1,0:T(8,128)(2,1)S(1)}, u32[]{:S(2)}, u32[]{:S(2)}) collective-permute-start(bf16[2,256,256]{2,1,0:T(8,128)(2,1)S(1)} %shard_map.50.refs_0_), channel_id=1, source_target_pairs={{0,3},{1,2},{2,1},{3,0},{4,7},{5,6},{6,5},{7,4},{8,11},{9,10},{10,... | collective-permute-start | bytes 786440 | tf_op jit(solution)/shard_map/ppermute | solution.py:21
  30.8 0.6 collective-permute-start.13
  31.4 0.0 collective-permute-done.9
  31.4 0.5 collective-permute-start.12
  31.9 0.1 collective-permute-done.8
  32.0 0.0 collective-permute-done.7
  32.1 0.1 collective-permute-start.10
  32.1 6.4 %collective-permute-done.11.refs_1_.refs_3_ = bf16[2,256,256]{2,1,0:T(8,128)(2,1)S(1)} collective-permute-done((bf16[2,256,256]{2,1,0:T(8,128)(2,1)S(1)}, bf16[2,256,256]{2,1,0:T(8,128)(2,1)S(1)}, u32[]{:S(2)}, u32[]{:S(2)}) %collective-permute-start.11) | collective-permute-done | bytes 262176 | tf_op jit(solution)/shard_map/ppermute | solution.py:21
  38.6 0.0 collective-permute-done.10.far
  38.6 0.3 shard_map.51.part
  38.8 3.4 %collective-permute-done.13.refs_2_ = bf16[2,256,256]{2,1,0:T(8,128)(2,1)S(1)} collective-permute-done((bf16[2,256,256]{2,1,0:T(8,128)(2,1)S(1)}, bf16[2,256,256]{2,1,0:T(8,128)(2,1)S(1)}, u32[]{:S(2)}, u32[]{:S(2)}) %collective-permute-start.13) | collective-permute-done | bytes 262176 | tf_op jit(solution)/shard_map/ppermute | solution.py:21
  42.2 0.1 collective-permute-done.12.refs_1_
  42.3 0.9 %shard_map.52 = (f32[64,256]{1,0:T(8,128)S(1)}, bf16[64,256]{1,0:T(8,128)(2,1)S(1)}, bf16[4,64,256]{2,1,0:T(8,128)(2,1)S(1)}) custom-call(f32[64,256]{1,0:T(8,128)S(1)} %shard_map.51.part, bf16[4,64,256]{2,1,0:T(8,128)(2,1)S(1)} %pad_maximum_fusion.1.near, bf16[4,64,256]{2,1,0:T(8,128)(2,1)S(1)} %collective-permute-done.10.far, ...), custom_call_target="tpu_custom_call" | custom-call | tf_op jit(solution)/shard_map/pallas_call | solution.py:149
  43.2 0.1 collective-permute-start.14
  43.3 0.2 shard_map.53
  43.5 1.1 %collective-permute-done.14 = bf16[4,64,256]{2,1,0:T(8,128)(2,1)S(1)} collective-permute-done((bf16[4,64,256]{2,1,0:T(8,128)(2,1)S(1)}, bf16[4,64,256]{2,1,0:T(8,128)(2,1)S(1)}, u32[]{:S(2)}, u32[]{:S(2)}) %collective-permute-start.14) | collective-permute-done | bytes 131104 | tf_op jit(solution)/shard_map/ppermute | solution.py:21
  44.7 3.5 %collective-permute-start.17 = (bf16[64,256]{1,0:T(8,128)(2,1)S(1)}, bf16[64,256]{1,0:T(8,128)(2,1)S(1)}, u32[]{:S(2)}, u32[]{:S(2)}) collective-permute-start(bf16[64,256]{1,0:T(8,128)(2,1)S(1)} %get-tuple-element.34), channel_id=1, source_target_pairs={{0,24},{4,28},{8,16},{12,20},{16,8},{20,12},{24,0},{28,4},{1,25},{... | collective-permute-start | bytes 98312 | tf_op jit(solution)/shard_map/ppermute | solution.py:21
  48.2 0.0 collective-permute-start.16
  48.2 0.9 %collective-permute-start.15 = (bf16[64,256]{1,0:T(8,128)(2,1)S(1)}, bf16[64,256]{1,0:T(8,128)(2,1)S(1)}, u32[]{:S(2)}, u32[]{:S(2)}) collective-permute-start(bf16[64,256]{1,0:T(8,128)(2,1)S(1)} %get-tuple-element.36), channel_id=1, source_target_pairs={{0,8},{4,12},{8,0},{12,4},{16,24},{20,28},{24,16},{28,20},{1,9},{5... | collective-permute-start | bytes 98312 | tf_op jit(solution)/shard_map/ppermute | solution.py:21
  49.1 1.4 %collective-permute-done.17.refs_3_ = bf16[64,256]{1,0:T(8,128)(2,1)S(1)} collective-permute-done((bf16[64,256]{1,0:T(8,128)(2,1)S(1)}, bf16[64,256]{1,0:T(8,128)(2,1)S(1)}, u32[]{:S(2)}, u32[]{:S(2)}) %collective-permute-start.17) | collective-permute-done | bytes 32800 | tf_op jit(solution)/shard_map/ppermute | solution.py:21
  50.5 2.5 %collective-permute-done.16.refs_2_ = bf16[64,256]{1,0:T(8,128)(2,1)S(1)} collective-permute-done((bf16[64,256]{1,0:T(8,128)(2,1)S(1)}, bf16[64,256]{1,0:T(8,128)(2,1)S(1)}, u32[]{:S(2)}, u32[]{:S(2)}) %collective-permute-start.16) | collective-permute-done | bytes 32800 | tf_op jit(solution)/shard_map/ppermute | solution.py:21
  53.0 0.0 collective-permute-done.15.refs_1_
  53.0 0.3 shard_map.54
  53.4 0.1 collective-permute-start.18
  53.4 0.2 shard_map.55
  53.7 1.1 %collective-permute-done.18 = bf16[4,64,256]{2,1,0:T(8,128)(2,1)S(1)} collective-permute-done((bf16[4,64,256]{2,1,0:T(8,128)(2,1)S(1)}, bf16[4,64,256]{2,1,0:T(8,128)(2,1)S(1)}, u32[]{:S(2)}, u32[]{:S(2)}) %collective-permute-start.18) | collective-permute-done | bytes 131104 | tf_op jit(solution)/shard_map/ppermute | solution.py:21
  54.8 1.5 %collective-permute-start.21 = (bf16[64,256]{1,0:T(8,128)(2,1)S(1)}, bf16[64,256]{1,0:T(8,128)(2,1)S(1)}, u32[]{:S(2)}, u32[]{:S(2)}) collective-permute-start(bf16[64,256]{1,0:T(8,128)(2,1)S(1)} %get-tuple-element.31), channel_id=1, source_target_pairs={{0,24},{4,28},{8,16},{12,20},{16,8},{20,12},{24,0},{28,4},{1,25},{... | collective-permute-start | bytes 98312 | tf_op jit(solution)/shard_map/ppermute | solution.py:21
  56.4 0.6 %collective-permute-start.20 = (bf16[64,256]{1,0:T(8,128)(2,1)S(1)}, bf16[64,256]{1,0:T(8,128)(2,1)S(1)}, u32[]{:S(2)}, u32[]{:S(2)}) collective-permute-start(bf16[64,256]{1,0:T(8,128)(2,1)S(1)} %get-tuple-element.32), channel_id=1, source_target_pairs={{0,16},{4,20},{8,24},{12,28},{16,0},{20,4},{24,8},{28,12},{1,17},{... | collective-permute-start | bytes 98312 | tf_op jit(solution)/shard_map/ppermute | solution.py:21
  57.0 2.3 %collective-permute-start.19 = (bf16[64,256]{1,0:T(8,128)(2,1)S(1)}, bf16[64,256]{1,0:T(8,128)(2,1)S(1)}, u32[]{:S(2)}, u32[]{:S(2)}) collective-permute-start(bf16[64,256]{1,0:T(8,128)(2,1)S(1)} %get-tuple-element.33), channel_id=1, source_target_pairs={{0,8},{4,12},{8,0},{12,4},{16,24},{20,28},{24,16},{28,20},{1,9},{5... | collective-permute-start | bytes 98312 | tf_op jit(solution)/shard_map/ppermute | solution.py:21
  59.3 1.6 %collective-permute-done.21.refs_3_ = bf16[64,256]{1,0:T(8,128)(2,1)S(1)} collective-permute-done((bf16[64,256]{1,0:T(8,128)(2,1)S(1)}, bf16[64,256]{1,0:T(8,128)(2,1)S(1)}, u32[]{:S(2)}, u32[]{:S(2)}) %collective-permute-start.21) | collective-permute-done | bytes 32800 | tf_op jit(solution)/shard_map/ppermute | solution.py:21
  60.9 0.4 collective-permute-done.20.refs_2_
  61.3 0.3 collective-permute-done.19.refs_1_
  61.6 0.8 %shard_map.56 = f32[3,1,64,256]{3,2,1,0:T(8,128)} custom-call(f32[64,256]{1,0:T(8,128)S(1)} %slice_bitcast_fusion.2.refs_0_, bf16[64,256]{1,0:T(8,128)(2,1)S(1)} %collective-permute-done.19.refs_1_, bf16[64,256]{1,0:T(8,128)(2,1)S(1)} %collective-permute-done.20.refs_2_, bf16[64,256]{1,0:T(8,128)(2,1)S(1)} %collective-permute-done.21.refs_3_, ...), custom_call_target="tpu_custom_call" | custom-call | tf_op jit(solution)/shard_map/pallas_call | solution.py:149
  (13 shorter events, 0.2 us)
Async XLA Ops:
  0.0 1.0 %copy-start = (bf16[3,1,256,256]{3,2,1,0:T(8,128)(2,1)S(1)}, bf16[3,1,256,256]{3,2,1,0:T(8,128)(2,1)}, u32[]{:S(2)}) copy-start(bf16[3,1,256,256]{3,2,1,0:T(8,128)(2,1)} %refs_5_.3) | copy-start | bytes 1179652
  1.0 0.9 %copy-start.2 = (bf16[3,1,64,256]{3,2,1,0:T(8,128)(2,1)S(1)}, bf16[3,1,64,256]{3,2,1,0:T(8,128)(2,1)}, u32[]{:S(2)}) copy-start(bf16[3,1,64,256]{3,2,1,0:T(8,128)(2,1)} %refs_4_.1) | copy-start | bytes 294916
  2.0 6.8 %copy-start.4 = (s32[2,2,1,2]{3,2,1,0:T(1,128)S(1)}, s32[2,2,1,2]{3,2,1,0:T(1,128)}, u32[]{:S(2)}) copy-start(s32[2,2,1,2]{3,2,1,0:T(1,128)} %pattern.3) | copy-start | bytes 100
  2.1 10.2 %collective-permute-start.2 = (bf16[64,256]{1,0:T(8,128)(2,1)S(1)}, bf16[64,256]{1,0:T(8,128)(2,1)S(1)}, u32[]{:S(2)}, u32[]{:S(2)}) collective-permute-start(bf16[64,256]{1,0:T(8,128)(2,1)S(1)} %get-tuple-element.16), channel_id=1, source_target_pairs={{0,24},{4,28},{8,16},{12,20},{16,8},{20,12},{24,0},{28,4},{1,25},{... | collective-permute-start | bytes 98312 | tf_op jit(solution)/shard_map/ppermute | solution.py:21
  7.2 5.4 %collective-permute-start.1 = (bf16[64,256]{1,0:T(8,128)(2,1)S(1)}, bf16[64,256]{1,0:T(8,128)(2,1)S(1)}, u32[]{:S(2)}, u32[]{:S(2)}) collective-permute-start(bf16[64,256]{1,0:T(8,128)(2,1)S(1)} %get-tuple-element.16), channel_id=1, source_target_pairs={{0,16},{4,20},{8,24},{12,28},{16,0},{20,4},{24,8},{28,12},{1,17},{... | collective-permute-start | bytes 98312 | tf_op jit(solution)/shard_map/ppermute | solution.py:21
  7.2 5.4 %collective-permute-start = (bf16[64,256]{1,0:T(8,128)(2,1)S(1)}, bf16[64,256]{1,0:T(8,128)(2,1)S(1)}, u32[]{:S(2)}, u32[]{:S(2)}) collective-permute-start(bf16[64,256]{1,0:T(8,128)(2,1)S(1)} %get-tuple-element.16), channel_id=1, source_target_pairs={{0,8},{4,12},{8,0},{12,4},{16,24},{20,28},{24,16},{28,20},{1,9},{5... | collective-permute-start | bytes 98312 | tf_op jit(solution)/shard_map/ppermute | solution.py:21
  9.0 10.2 %collective-permute-start.4 = (bf16[2,256,256]{2,1,0:T(8,128)(2,1)S(1)}, bf16[2,256,256]{2,1,0:T(8,128)(2,1)S(1)}, u32[]{:S(2)}, u32[]{:S(2)}) collective-permute-start(bf16[2,256,256]{2,1,0:T(8,128)(2,1)S(1)} %shard_map.47.refs_0_.refs_4_), channel_id=1, source_target_pairs={{0,3},{1,2},{2,1},{3,0},{4,7},{5,6},{6,5},{7,4},{8,11},{9,10},{10,... | collective-permute-start | bytes 786440 | tf_op jit(solution)/shard_map/ppermute | solution.py:21
  11.7 11.5 %collective-permute-start.6 = (bf16[2,256,256]{2,1,0:T(8,128)(2,1)S(1)}, bf16[2,256,256]{2,1,0:T(8,128)(2,1)S(1)}, u32[]{:S(2)}, u32[]{:S(2)}) collective-permute-start(bf16[2,256,256]{2,1,0:T(8,128)(2,1)S(1)} %shard_map.47.refs_0_.refs_4_), channel_id=1, source_target_pairs={{0,1},{1,0},{2,3},{3,2},{4,5},{5,4},{6,7},{7,6},{8,9},{9,8},{10,11... | collective-permute-start | bytes 786440 | tf_op jit(solution)/shard_map/ppermute | solution.py:21
  12.2 11.0 %collective-permute-start.5 = (bf16[2,256,256]{2,1,0:T(8,128)(2,1)S(1)}, bf16[2,256,256]{2,1,0:T(8,128)(2,1)S(1)}, u32[]{:S(2)}, u32[]{:S(2)}) collective-permute-start(bf16[2,256,256]{2,1,0:T(8,128)(2,1)S(1)} %shard_map.47.refs_0_.refs_4_), channel_id=1, source_target_pairs={{0,2},{1,3},{2,0},{3,1},{4,6},{5,7},{6,4},{7,5},{8,10},{9,11},{10,... | collective-permute-start | bytes 786440 | tf_op jit(solution)/shard_map/ppermute | solution.py:21
  12.6 10.6 %copy-start.1 = (bf16[3,1,256,256]{3,2,1,0:T(8,128)(2,1)S(1)}, bf16[3,1,256,256]{3,2,1,0:T(8,128)(2,1)}, u32[]{:S(2)}) copy-start(bf16[3,1,256,256]{3,2,1,0:T(8,128)(2,1)} %refs_5_.3) | copy-start | bytes 1179652
  12.6 10.6 %copy-start.3 = (bf16[3,1,64,256]{3,2,1,0:T(8,128)(2,1)S(1)}, bf16[3,1,64,256]{3,2,1,0:T(8,128)(2,1)}, u32[]{:S(2)}) copy-start(bf16[3,1,64,256]{3,2,1,0:T(8,128)(2,1)} %refs_4_.1) | copy-start | bytes 294916
  12.7 1.4 %collective-permute-start.3 = (bf16[4,64,256]{2,1,0:T(8,128)(2,1)S(1)}, bf16[4,64,256]{2,1,0:T(8,128)(2,1)S(1)}, u32[]{:S(2)}, u32[]{:S(2)}) collective-permute-start(bf16[4,64,256]{2,1,0:T(8,128)(2,1)S(1)} %pad_maximum_fusion.near), channel_id=1, source_target_pairs={{0,4},{4,0},{8,12},{12,8},{16,20},{20,16},{24,28},{28,24},{1,5},{5... | collective-permute-start | bytes 393224 | tf_op jit(solution)/shard_map/ppermute | solution.py:21
  19.5 8.6 %copy-start.5 = (bf16[2,1,2,256,256]{4,3,2,1,0:T(8,128)(2,1)S(1)}, bf16[2,1,2,256,256]{4,3,2,1,0:T(8,128)(2,1)}, u32[]{:S(2)}) copy-start(bf16[2,1,2,256,256]{4,3,2,1,0:T(8,128)(2,1)} %param.6) | copy-start | bytes 1572868
  23.7 7.7 %collective-permute-start.9 = (bf16[64,256]{1,0:T(8,128)(2,1)S(1)}, bf16[64,256]{1,0:T(8,128)(2,1)S(1)}, u32[]{:S(2)}, u32[]{:S(2)}) collective-permute-start(bf16[64,256]{1,0:T(8,128)(2,1)S(1)} %get-tuple-element.17), channel_id=1, source_target_pairs={{0,24},{4,28},{8,16},{12,20},{16,8},{20,12},{24,0},{28,4},{1,25},{... | collective-permute-start | bytes 98312 | tf_op jit(solution)/shard_map/ppermute | solution.py:21
  27.2 4.8 %collective-permute-start.8 = (bf16[64,256]{1,0:T(8,128)(2,1)S(1)}, bf16[64,256]{1,0:T(8,128)(2,1)S(1)}, u32[]{:S(2)}, u32[]{:S(2)}) collective-permute-start(bf16[64,256]{1,0:T(8,128)(2,1)S(1)} %get-tuple-element.17), channel_id=1, source_target_pairs={{0,16},{4,20},{8,24},{12,28},{16,0},{20,4},{24,8},{28,12},{1,17},{... | collective-permute-start | bytes 98312 | tf_op jit(solution)/shard_map/ppermute | solution.py:21
  27.2 4.8 %collective-permute-start.7 = (bf16[64,256]{1,0:T(8,128)(2,1)S(1)}, bf16[64,256]{1,0:T(8,128)(2,1)S(1)}, u32[]{:S(2)}, u32[]{:S(2)}) collective-permute-start(bf16[64,256]{1,0:T(8,128)(2,1)S(1)} %get-tuple-element.17), channel_id=1, source_target_pairs={{0,8},{4,12},{8,0},{12,4},{16,24},{20,28},{24,16},{28,20},{1,9},{5... | collective-permute-start | bytes 98312 | tf_op jit(solution)/shard_map/ppermute | solution.py:21
  28.4 10.2 %collective-permute-start.11 = (bf16[2,256,256]{2,1,0:T(8,128)(2,1)S(1)}, bf16[2,256,256]{2,1,0:T(8,128)(2,1)S(1)}, u32[]{:S(2)}, u32[]{:S(2)}) collective-permute-start(bf16[2,256,256]{2,1,0:T(8,128)(2,1)S(1)} %shard_map.50.refs_0_), channel_id=1, source_target_pairs={{0,3},{1,2},{2,1},{3,0},{4,7},{5,6},{6,5},{7,4},{8,11},{9,10},{10,... | collective-permute-start | bytes 786440 | tf_op jit(solution)/shard_map/ppermute | solution.py:21
  30.8 11.5 %collective-permute-start.13 = (bf16[2,256,256]{2,1,0:T(8,128)(2,1)S(1)}, bf16[2,256,256]{2,1,0:T(8,128)(2,1)S(1)}, u32[]{:S(2)}, u32[]{:S(2)}) collective-permute-start(bf16[2,256,256]{2,1,0:T(8,128)(2,1)S(1)} %shard_map.50.refs_0_), channel_id=1, source_target_pairs={{0,2},{1,3},{2,0},{3,1},{4,6},{5,7},{6,4},{7,5},{8,10},{9,11},{10,... | collective-permute-start | bytes 786440 | tf_op jit(solution)/shard_map/ppermute | solution.py:21
  31.4 10.9 %collective-permute-start.12 = (bf16[2,256,256]{2,1,0:T(8,128)(2,1)S(1)}, bf16[2,256,256]{2,1,0:T(8,128)(2,1)S(1)}, u32[]{:S(2)}, u32[]{:S(2)}) collective-permute-start(bf16[2,256,256]{2,1,0:T(8,128)(2,1)S(1)} %shard_map.50.refs_0_), channel_id=1, source_target_pairs={{0,1},{1,0},{2,3},{3,2},{4,5},{5,4},{6,7},{7,6},{8,9},{9,8},{10,11... | collective-permute-start | bytes 786440 | tf_op jit(solution)/shard_map/ppermute | solution.py:21
  32.1 6.5 %collective-permute-start.10 = (bf16[4,64,256]{2,1,0:T(8,128)(2,1)S(1)}, bf16[4,64,256]{2,1,0:T(8,128)(2,1)S(1)}, u32[]{:S(2)}, u32[]{:S(2)}) collective-permute-start(bf16[4,64,256]{2,1,0:T(8,128)(2,1)S(1)} %pad_maximum_fusion.1.near), channel_id=1, source_target_pairs={{0,4},{4,0},{8,12},{12,8},{16,20},{20,16},{24,28},{28,24},{1,5},{5... | collective-permute-start | bytes 393224 | tf_op jit(solution)/shard_map/ppermute | solution.py:21
  43.2 1.4 %collective-permute-start.14 = (bf16[4,64,256]{2,1,0:T(8,128)(2,1)S(1)}, bf16[4,64,256]{2,1,0:T(8,128)(2,1)S(1)}, u32[]{:S(2)}, u32[]{:S(2)}) collective-permute-start(bf16[4,64,256]{2,1,0:T(8,128)(2,1)S(1)} %get-tuple-element.20), channel_id=1, source_target_pairs={{0,4},{4,0},{8,12},{12,8},{16,20},{20,16},{24,28},{28,24},{1,5},{5... | collective-permute-start | bytes 393224 | tf_op jit(solution)/shard_map/ppermute | solution.py:21
  44.7 5.8 %collective-permute-start.17 = (bf16[64,256]{1,0:T(8,128)(2,1)S(1)}, bf16[64,256]{1,0:T(8,128)(2,1)S(1)}, u32[]{:S(2)}, u32[]{:S(2)}) collective-permute-start(bf16[64,256]{1,0:T(8,128)(2,1)S(1)} %get-tuple-element.34), channel_id=1, source_target_pairs={{0,24},{4,28},{8,16},{12,20},{16,8},{20,12},{24,0},{28,4},{1,25},{... | collective-permute-start | bytes 98312 | tf_op jit(solution)/shard_map/ppermute | solution.py:21
  48.2 4.8 %collective-permute-start.16 = (bf16[64,256]{1,0:T(8,128)(2,1)S(1)}, bf16[64,256]{1,0:T(8,128)(2,1)S(1)}, u32[]{:S(2)}, u32[]{:S(2)}) collective-permute-start(bf16[64,256]{1,0:T(8,128)(2,1)S(1)} %get-tuple-element.35), channel_id=1, source_target_pairs={{0,16},{4,20},{8,24},{12,28},{16,0},{20,4},{24,8},{28,12},{1,17},{... | collective-permute-start | bytes 98312 | tf_op jit(solution)/shard_map/ppermute | solution.py:21
  48.2 4.8 %collective-permute-start.15 = (bf16[64,256]{1,0:T(8,128)(2,1)S(1)}, bf16[64,256]{1,0:T(8,128)(2,1)S(1)}, u32[]{:S(2)}, u32[]{:S(2)}) collective-permute-start(bf16[64,256]{1,0:T(8,128)(2,1)S(1)} %get-tuple-element.36), channel_id=1, source_target_pairs={{0,8},{4,12},{8,0},{12,4},{16,24},{20,28},{24,16},{28,20},{1,9},{5... | collective-permute-start | bytes 98312 | tf_op jit(solution)/shard_map/ppermute | solution.py:21
  53.4 1.4 %collective-permute-start.18 = (bf16[4,64,256]{2,1,0:T(8,128)(2,1)S(1)}, bf16[4,64,256]{2,1,0:T(8,128)(2,1)S(1)}, u32[]{:S(2)}, u32[]{:S(2)}) collective-permute-start(bf16[4,64,256]{2,1,0:T(8,128)(2,1)S(1)} %get-tuple-element.23), channel_id=1, source_target_pairs={{0,4},{4,0},{8,12},{12,8},{16,20},{20,16},{24,28},{28,24},{1,5},{5... | collective-permute-start | bytes 393224 | tf_op jit(solution)/shard_map/ppermute | solution.py:21
  54.8 6.1 %collective-permute-start.21 = (bf16[64,256]{1,0:T(8,128)(2,1)S(1)}, bf16[64,256]{1,0:T(8,128)(2,1)S(1)}, u32[]{:S(2)}, u32[]{:S(2)}) collective-permute-start(bf16[64,256]{1,0:T(8,128)(2,1)S(1)} %get-tuple-element.31), channel_id=1, source_target_pairs={{0,24},{4,28},{8,16},{12,20},{16,8},{20,12},{24,0},{28,4},{1,25},{... | collective-permute-start | bytes 98312 | tf_op jit(solution)/shard_map/ppermute | solution.py:21
  56.4 4.9 %collective-permute-start.20 = (bf16[64,256]{1,0:T(8,128)(2,1)S(1)}, bf16[64,256]{1,0:T(8,128)(2,1)S(1)}, u32[]{:S(2)}, u32[]{:S(2)}) collective-permute-start(bf16[64,256]{1,0:T(8,128)(2,1)S(1)} %get-tuple-element.32), channel_id=1, source_target_pairs={{0,16},{4,20},{8,24},{12,28},{16,0},{20,4},{24,8},{28,12},{1,17},{... | collective-permute-start | bytes 98312 | tf_op jit(solution)/shard_map/ppermute | solution.py:21
  57.0 4.6 %collective-permute-start.19 = (bf16[64,256]{1,0:T(8,128)(2,1)S(1)}, bf16[64,256]{1,0:T(8,128)(2,1)S(1)}, u32[]{:S(2)}, u32[]{:S(2)}) collective-permute-start(bf16[64,256]{1,0:T(8,128)(2,1)S(1)} %get-tuple-element.33), channel_id=1, source_target_pairs={{0,8},{4,12},{8,0},{12,4},{16,24},{20,28},{24,16},{28,20},{1,9},{5... | collective-permute-start | bytes 98312 | tf_op jit(solution)/shard_map/ppermute | solution.py:21

commit v6 on v3

--- a/solution.py
+++ b/solution.py
@@ -67,6 +67,17 @@
     out_b[...] = solved.astype(BF16)
 
 
+def pick_kernel(level, cols, pattern, raw, own):
+    shape = own.shape[1:]
+    for group in range(own.shape[0]):
+        total = jnp.zeros(shape, F32)
+        for slot in range(raw.shape[0]):
+            place = jnp.broadcast_to(pattern[1, level, :, slot : slot + 1], shape)
+            here = (place >= cols * group) & (place < cols * (group + 1))
+            total = total + jnp.where(here, raw[slot].astype(F32), 0.0)
+        own[group] = total.astype(BF16)
+
+
 def early_kernel(repeat, cols, steps, near, far, *refs):
     refs[-1][...] = update(near, far, refs[:-1], steps, repeat, cols)
 
@@ -150,12 +161,13 @@
     chip_segs_b = jax.ShapeDtypeStruct((chips, nrhs, bs), BF16)
 
     def gathered_tiles(level, after):
-        groups = jnp.arange(repeat, dtype=jnp.int32)[:, None, None, None]
-        raw, slots = tiles[level, 0], pattern[1, level, 0]
+        source = tiles
         if after is not None:
-            raw, slots, _ = lax.optimization_barrier((raw, slots, after))
-        here = (slots // cols)[None, :, None, None] == groups
-        own = jnp.sum(jnp.where(here, raw[None].astype(F32), 0.0), axis=1).astype(BF16)
+            source, _ = lax.optimization_barrier((tiles, after))
+        own = call(
+            functools.partial(pick_kernel, level, cols),
+            jax.ShapeDtypeStruct((repeat, bs, bs), BF16), [], pattern, source[level, 0],
+        )
         found = [own] + [None] * (cols - 1)
         for step in send_order(cols):
             found[step] = swap(own, "col", cols, step)

time: 61 us -> 62.6 us (1.026)
  waiting for transfers between devices: 26.9 us -> 28.6 us
  other arithmetic: 1.55 us -> 0.11 us
  local copies, waits for them, and re-layouts: 1.93 us -> 2.92 us
    ppermute x22, waiting for transfers between devices: 26.9 us -> 28.6 us  [swap(): return lax.ppermute(value, axis, [(i, i ^ mask) for i in range(size)])]
    squeeze x1 -> x0, other arithmetic: 1.09 us -> none  [gathered_tiles(): raw, slots = (tiles[level, 0], pattern[1, level, 0])]
    squeeze x1 -> x2, local copies, waits for them, and re-layouts: 0.01 us -> 0.98 us  [gathered_tiles(): source[level, 0]]
    pallas_call x9 -> x11, Pallas kernels: 3.66 us -> 4.05 us  [call(): pl.pallas_call(kernel, out_shape=outs, in_specs=[pl.BlockSpec(memory_spac...]
    unnamed x8 -> x12, local copies, waits for them, and re-layouts: 1.9 us -> 1.91 us
  transfers between devices with their start and end apart: 22 -> 22, of which waited for: 12 -> 14; matrix products, arithmetic and copies ran while one was open for 2% -> 2% of each run, Pallas kernels for 2% -> 2%
where the time goes in v6:
time: 62.6 us; the launch traced here: 62.4 us
  waiting for transfers between devices  28.6 us (46%)
  starting transfers between devices  26.5 us (42%)
  Pallas kernels  4.05 us (6%)
  local copies, waits for them, and re-layouts  2.92 us (5%)
    ppermute x22, waiting for transfers between devices, swap(): return lax.ppermute(value, axis, [(i, i ^ mask) for i in range(size)])  28.6 us
    ppermute x22, starting transfers between devices, swap(): return lax.ppermute(value, axis, [(i, i ^ mask) for i in range(size)])  26.5 us
    pallas_call x11, Pallas kernels, call(): pl.pallas_call(kernel, out_shape=outs, in_specs=[pl.BlockSpec(memory_spac...  4.05 us
    unnamed x12, local copies, waits for them, and re-layouts  1.91 us
  transfers between devices with their start and end apart: 22, of which 14 were waited for; matrix products, arithmetic and copies ran while one was open for 2% of the time, Pallas kernels for 2%

profile of v6, /device:TPU:0, one launch (start us, length us, event | category | flops | bytes accessed | tf_op | source)
XLA Modules:
  0.0 62.4 jit_solution(136571133690504821)
XLA Ops:
  0.0 1.0 %copy-done = bf16[3,1,256,256]{3,2,1,0:T(8,128)(2,1)S(1)} copy-done((bf16[3,1,256,256]{3,2,1,0:T(8,128)(2,1)S(1)}, bf16[3,1,256,256]{3,2,1,0:T(8,128)(2,1)}, u32[]{:S(2)}) %copy-start) | copy-done | bytes 393240
  1.0 0.9 %copy-done.2 = bf16[3,1,64,256]{3,2,1,0:T(8,128)(2,1)S(1)} copy-done((bf16[3,1,64,256]{3,2,1,0:T(8,128)(2,1)S(1)}, bf16[3,1,64,256]{3,2,1,0:T(8,128)(2,1)}, u32[]{:S(2)}) %copy-start.2) | copy-done | bytes 98328
  1.9 0.2 shard_map.46
  2.1 5.1 %collective-permute-start.2 = (bf16[64,256]{1,0:T(8,128)(2,1)S(1)}, bf16[64,256]{1,0:T(8,128)(2,1)S(1)}, u32[]{:S(2)}, u32[]{:S(2)}) collective-permute-start(bf16[64,256]{1,0:T(8,128)(2,1)S(1)} %get-tuple-element.16), channel_id=1, source_target_pairs={{0,24},{4,28},{8,16},{12,20},{16,8},{20,12},{24,0},{28,4},{1,25},{... | collective-permute-start | bytes 98312 | tf_op jit(solution)/shard_map/ppermute | solution.py:21
  7.2 0.0 collective-permute-start.1
  7.2 0.6 %collective-permute-start = (bf16[64,256]{1,0:T(8,128)(2,1)S(1)}, bf16[64,256]{1,0:T(8,128)(2,1)S(1)}, u32[]{:S(2)}, u32[]{:S(2)}) collective-permute-start(bf16[64,256]{1,0:T(8,128)(2,1)S(1)} %get-tuple-element.16), channel_id=1, source_target_pairs={{0,8},{4,12},{8,0},{12,4},{16,24},{20,28},{24,16},{28,20},{1,9},{5... | collective-permute-start | bytes 98312 | tf_op jit(solution)/shard_map/ppermute | solution.py:21
  7.9 1.0 %slice_bitcast_fusion.1.raw = bf16[2,256,256]{2,1,0:T(8,128)(2,1)S(1)} fusion(bf16[2,1,2,256,256]{4,3,2,1,0:T(8,128)(2,1)} %param.6), kind=kLoop, calls=%fused_computation.3 | loop fusion | bytes 524288 | tf_op jit(solution)/shard_map/squeeze | solution.py:169
  8.8 0.0 copy-done.4
  8.8 0.2 shard_map.47.refs_0_.refs_4_
  9.0 2.7 %collective-permute-start.4 = (bf16[2,256,256]{2,1,0:T(8,128)(2,1)S(1)}, bf16[2,256,256]{2,1,0:T(8,128)(2,1)S(1)}, u32[]{:S(2)}, u32[]{:S(2)}) collective-permute-start(bf16[2,256,256]{2,1,0:T(8,128)(2,1)S(1)} %shard_map.47.refs_0_.refs_4_), channel_id=1, source_target_pairs={{0,3},{1,2},{2,1},{3,0},{4,7},{5,6},{6,5},{7,4},{8,11},{9,10},{10,... | collective-permute-start | bytes 786440 | tf_op jit(solution)/shard_map/ppermute | solution.py:21
  11.7 0.5 collective-permute-start.6
  12.2 0.0 collective-permute-done.2
  12.2 0.4 collective-permute-start.5
  12.6 0.0 collective-permute-done.1
  12.6 0.0 collective-permute-done
  12.6 0.0 copy-start.1
  12.6 0.0 copy-start.3
  12.7 0.1 collective-permute-start.3
  12.7 1.3 %collective-permute-done.3.far = bf16[4,64,256]{2,1,0:T(8,128)(2,1)S(1)} collective-permute-done((bf16[4,64,256]{2,1,0:T(8,128)(2,1)S(1)}, bf16[4,64,256]{2,1,0:T(8,128)(2,1)S(1)}, u32[]{:S(2)}, u32[]{:S(2)}) %collective-permute-start.3) | collective-permute-done | bytes 131104 | tf_op jit(solution)/shard_map/ppermute | solution.py:21
  14.1 5.2 %collective-permute-done.4.refs_1_.refs_7_.refs_3_ = bf16[2,256,256]{2,1,0:T(8,128)(2,1)S(1)} collective-permute-done((bf16[2,256,256]{2,1,0:T(8,128)(2,1)S(1)}, bf16[2,256,256]{2,1,0:T(8,128)(2,1)S(1)}, u32[]{:S(2)}, u32[]{:S(2)}) %collective-permute-start.4) | collective-permute-done | bytes 262176 | tf_op jit(solution)/shard_map/ppermute | solution.py:21
  19.2 0.3 shard_map.48.part
  19.5 0.0 copy-start.5
  19.5 3.7 %collective-permute-done.6.refs_1_.refs_5_ = bf16[2,256,256]{2,1,0:T(8,128)(2,1)S(1)} collective-permute-done((bf16[2,256,256]{2,1,0:T(8,128)(2,1)S(1)}, bf16[2,256,256]{2,1,0:T(8,128)(2,1)S(1)}, u32[]{:S(2)}, u32[]{:S(2)}) %collective-permute-start.6) | collective-permute-done | bytes 262176 | tf_op jit(solution)/shard_map/ppermute | solution.py:21
  23.2 0.0 collective-permute-done.5.refs_0_.refs_6_.refs_2_
  23.2 0.0 copy-done.3
  23.2 0.5 shard_map.49
  23.7 3.5 %collective-permute-start.9 = (bf16[64,256]{1,0:T(8,128)(2,1)S(1)}, bf16[64,256]{1,0:T(8,128)(2,1)S(1)}, u32[]{:S(2)}, u32[]{:S(2)}) collective-permute-start(bf16[64,256]{1,0:T(8,128)(2,1)S(1)} %get-tuple-element.17), channel_id=1, source_target_pairs={{0,24},{4,28},{8,16},{12,20},{16,8},{20,12},{24,0},{28,4},{1,25},{... | collective-permute-start | bytes 98312 | tf_op jit(solution)/shard_map/ppermute | solution.py:21
  27.2 0.0 collective-permute-start.8
  27.2 0.9 %collective-permute-start.7 = (bf16[64,256]{1,0:T(8,128)(2,1)S(1)}, bf16[64,256]{1,0:T(8,128)(2,1)S(1)}, u32[]{:S(2)}, u32[]{:S(2)}) collective-permute-start(bf16[64,256]{1,0:T(8,128)(2,1)S(1)} %get-tuple-element.17), channel_id=1, source_target_pairs={{0,8},{4,12},{8,0},{12,4},{16,24},{20,28},{24,16},{28,20},{1,9},{5... | collective-permute-start | bytes 98312 | tf_op jit(solution)/shard_map/ppermute | solution.py:21
  28.1 0.0 copy-done.5
  28.2 0.2 shard_map.50.refs_0_
  28.4 2.4 %collective-permute-start.11 = (bf16[2,256,256]{2,1,0:T(8,128)(2,1)S(1)}, bf16[2,256,256]{2,1,0:T(8,128)(2,1)S(1)}, u32[]{:S(2)}, u32[]{:S(2)}) collective-permute-start(bf16[2,256,256]{2,1,0:T(8,128)(2,1)S(1)} %shard_map.50.refs_0_), channel_id=1, source_target_pairs={{0,3},{1,2},{2,1},{3,0},{4,7},{5,6},{6,5},{7,4},{8,11},{9,10},{10,... | collective-permute-start | bytes 786440 | tf_op jit(solution)/shard_map/ppermute | solution.py:21
  30.8 0.6 collective-permute-start.13
  31.4 0.0 collective-permute-done.9
  31.4 0.5 collective-permute-start.12
  31.9 0.1 collective-permute-done.8
  32.0 0.0 collective-permute-done.7
  32.1 0.1 collective-permute-start.10
  32.1 6.4 %collective-permute-done.11.refs_1_.refs_3_ = bf16[2,256,256]{2,1,0:T(8,128)(2,1)S(1)} collective-permute-done((bf16[2,256,256]{2,1,0:T(8,128)(2,1)S(1)}, bf16[2,256,256]{2,1,0:T(8,128)(2,1)S(1)}, u32[]{:S(2)}, u32[]{:S(2)}) %collective-permute-start.11) | collective-permute-done | bytes 262176 | tf_op jit(solution)/shard_map/ppermute | solution.py:21
  38.6 0.0 collective-permute-done.10.far
  38.6 0.3 shard_map.51.part
  38.8 3.4 %collective-permute-done.13.refs_2_ = bf16[2,256,256]{2,1,0:T(8,128)(2,1)S(1)} collective-permute-done((bf16[2,256,256]{2,1,0:T(8,128)(2,1)S(1)}, bf16[2,256,256]{2,1,0:T(8,128)(2,1)S(1)}, u32[]{:S(2)}, u32[]{:S(2)}) %collective-permute-start.13) | collective-permute-done | bytes 262176 | tf_op jit(solution)/shard_map/ppermute | solution.py:21
  42.2 0.1 collective-permute-done.12.refs_1_
  42.3 0.9 %shard_map.52 = (f32[64,256]{1,0:T(8,128)S(1)}, bf16[64,256]{1,0:T(8,128)(2,1)S(1)}, bf16[4,64,256]{2,1,0:T(8,128)(2,1)S(1)}) custom-call(f32[64,256]{1,0:T(8,128)S(1)} %shard_map.51.part, bf16[4,64,256]{2,1,0:T(8,128)(2,1)S(1)} %pad_maximum_fusion.1.near, bf16[4,64,256]{2,1,0:T(8,128)(2,1)S(1)} %collective-permute-done.10.far, ...), custom_call_target="tpu_custom_call" | custom-call | tf_op jit(solution)/shard_map/pallas_call | solution.py:140
  43.2 0.1 collective-permute-start.14
  43.3 0.2 shard_map.53
  43.5 1.1 %collective-permute-done.14 = bf16[4,64,256]{2,1,0:T(8,128)(2,1)S(1)} collective-permute-done((bf16[4,64,256]{2,1,0:T(8,128)(2,1)S(1)}, bf16[4,64,256]{2,1,0:T(8,128)(2,1)S(1)}, u32[]{:S(2)}, u32[]{:S(2)}) %collective-permute-start.14) | collective-permute-done | bytes 131104 | tf_op jit(solution)/shard_map/ppermute | solution.py:21
  44.7 3.5 %collective-permute-start.17 = (bf16[64,256]{1,0:T(8,128)(2,1)S(1)}, bf16[64,256]{1,0:T(8,128)(2,1)S(1)}, u32[]{:S(2)}, u32[]{:S(2)}) collective-permute-start(bf16[64,256]{1,0:T(8,128)(2,1)S(1)} %get-tuple-element.34), channel_id=1, source_target_pairs={{0,24},{4,28},{8,16},{12,20},{16,8},{20,12},{24,0},{28,4},{1,25},{... | collective-permute-start | bytes 98312 | tf_op jit(solution)/shard_map/ppermute | solution.py:21
  48.2 0.0 collective-permute-start.16
  48.2 0.9 %collective-permute-start.15 = (bf16[64,256]{1,0:T(8,128)(2,1)S(1)}, bf16[64,256]{1,0:T(8,128)(2,1)S(1)}, u32[]{:S(2)}, u32[]{:S(2)}) collective-permute-start(bf16[64,256]{1,0:T(8,128)(2,1)S(1)} %get-tuple-element.36), channel_id=1, source_target_pairs={{0,8},{4,12},{8,0},{12,4},{16,24},{20,28},{24,16},{28,20},{1,9},{5... | collective-permute-start | bytes 98312 | tf_op jit(solution)/shard_map/ppermute | solution.py:21
  49.1 1.4 %collective-permute-done.17.refs_3_ = bf16[64,256]{1,0:T(8,128)(2,1)S(1)} collective-permute-done((bf16[64,256]{1,0:T(8,128)(2,1)S(1)}, bf16[64,256]{1,0:T(8,128)(2,1)S(1)}, u32[]{:S(2)}, u32[]{:S(2)}) %collective-permute-start.17) | collective-permute-done | bytes 32800 | tf_op jit(solution)/shard_map/ppermute | solution.py:21
  50.5 2.5 %collective-permute-done.16.refs_2_ = bf16[64,256]{1,0:T(8,128)(2,1)S(1)} collective-permute-done((bf16[64,256]{1,0:T(8,128)(2,1)S(1)}, bf16[64,256]{1,0:T(8,128)(2,1)S(1)}, u32[]{:S(2)}, u32[]{:S(2)}) %collective-permute-start.16) | collective-permute-done | bytes 32800 | tf_op jit(solution)/shard_map/ppermute | solution.py:21
  53.0 0.0 collective-permute-done.15.refs_1_
  53.0 0.3 shard_map.54
  53.4 0.1 collective-permute-start.18
  53.4 0.2 shard_map.55
  53.7 1.1 %collective-permute-done.18 = bf16[4,64,256]{2,1,0:T(8,128)(2,1)S(1)} collective-permute-done((bf16[4,64,256]{2,1,0:T(8,128)(2,1)S(1)}, bf16[4,64,256]{2,1,0:T(8,128)(2,1)S(1)}, u32[]{:S(2)}, u32[]{:S(2)}) %collective-permute-start.18) | collective-permute-done | bytes 131104 | tf_op jit(solution)/shard_map/ppermute | solution.py:21
  54.8 1.5 %collective-permute-start.21 = (bf16[64,256]{1,0:T(8,128)(2,1)S(1)}, bf16[64,256]{1,0:T(8,128)(2,1)S(1)}, u32[]{:S(2)}, u32[]{:S(2)}) collective-permute-start(bf16[64,256]{1,0:T(8,128)(2,1)S(1)} %get-tuple-element.31), channel_id=1, source_target_pairs={{0,24},{4,28},{8,16},{12,20},{16,8},{20,12},{24,0},{28,4},{1,25},{... | collective-permute-start | bytes 98312 | tf_op jit(solution)/shard_map/ppermute | solution.py:21
  56.4 0.6 %collective-permute-start.20 = (bf16[64,256]{1,0:T(8,128)(2,1)S(1)}, bf16[64,256]{1,0:T(8,128)(2,1)S(1)}, u32[]{:S(2)}, u32[]{:S(2)}) collective-permute-start(bf16[64,256]{1,0:T(8,128)(2,1)S(1)} %get-tuple-element.32), channel_id=1, source_target_pairs={{0,16},{4,20},{8,24},{12,28},{16,0},{20,4},{24,8},{28,12},{1,17},{... | collective-permute-start | bytes 98312 | tf_op jit(solution)/shard_map/ppermute | solution.py:21
  57.0 2.3 %collective-permute-start.19 = (bf16[64,256]{1,0:T(8,128)(2,1)S(1)}, bf16[64,256]{1,0:T(8,128)(2,1)S(1)}, u32[]{:S(2)}, u32[]{:S(2)}) collective-permute-start(bf16[64,256]{1,0:T(8,128)(2,1)S(1)} %get-tuple-element.33), channel_id=1, source_target_pairs={{0,8},{4,12},{8,0},{12,4},{16,24},{20,28},{24,16},{28,20},{1,9},{5... | collective-permute-start | bytes 98312 | tf_op jit(solution)/shard_map/ppermute | solution.py:21
  59.3 1.6 %collective-permute-done.21.refs_3_ = bf16[64,256]{1,0:T(8,128)(2,1)S(1)} collective-permute-done((bf16[64,256]{1,0:T(8,128)(2,1)S(1)}, bf16[64,256]{1,0:T(8,128)(2,1)S(1)}, u32[]{:S(2)}, u32[]{:S(2)}) %collective-permute-start.21) | collective-permute-done | bytes 32800 | tf_op jit(solution)/shard_map/ppermute | solution.py:21
  60.9 0.4 collective-permute-done.20.refs_2_
  61.3 0.3 collective-permute-done.19.refs_1_
  61.6 0.8 %shard_map.56 = f32[3,1,64,256]{3,2,1,0:T(8,128)} custom-call(f32[64,256]{1,0:T(8,128)S(1)} %slice_bitcast_fusion.2.refs_0_, bf16[64,256]{1,0:T(8,128)(2,1)S(1)} %collective-permute-done.19.refs_1_, bf16[64,256]{1,0:T(8,128)(2,1)S(1)} %collective-permute-done.20.refs_2_, bf16[64,256]{1,0:T(8,128)(2,1)S(1)} %collective-permute-done.21.refs_3_, ...), custom_call_target="tpu_custom_call" | custom-call | tf_op jit(solution)/shard_map/pallas_call | solution.py:140
  (13 shorter events, 0.2 us)
Async XLA Ops:
  0.0 1.0 %copy-start = (bf16[3,1,256,256]{3,2,1,0:T(8,128)(2,1)S(1)}, bf16[3,1,256,256]{3,2,1,0:T(8,128)(2,1)}, u32[]{:S(2)}) copy-start(bf16[3,1,256,256]{3,2,1,0:T(8,128)(2,1)} %refs_5_.3) | copy-start | bytes 1179652
  1.0 0.9 %copy-start.2 = (bf16[3,1,64,256]{3,2,1,0:T(8,128)(2,1)S(1)}, bf16[3,1,64,256]{3,2,1,0:T(8,128)(2,1)}, u32[]{:S(2)}) copy-start(bf16[3,1,64,256]{3,2,1,0:T(8,128)(2,1)} %refs_4_.1) | copy-start | bytes 294916
  2.0 6.8 %copy-start.4 = (s32[2,2,1,2]{3,2,1,0:T(1,128)S(1)}, s32[2,2,1,2]{3,2,1,0:T(1,128)}, u32[]{:S(2)}) copy-start(s32[2,2,1,2]{3,2,1,0:T(1,128)} %pattern.3) | copy-start | bytes 100
  2.1 10.2 %collective-permute-start.2 = (bf16[64,256]{1,0:T(8,128)(2,1)S(1)}, bf16[64,256]{1,0:T(8,128)(2,1)S(1)}, u32[]{:S(2)}, u32[]{:S(2)}) collective-permute-start(bf16[64,256]{1,0:T(8,128)(2,1)S(1)} %get-tuple-element.16), channel_id=1, source_target_pairs={{0,24},{4,28},{8,16},{12,20},{16,8},{20,12},{24,0},{28,4},{1,25},{... | collective-permute-start | bytes 98312 | tf_op jit(solution)/shard_map/ppermute | solution.py:21
  7.2 5.4 %collective-permute-start.1 = (bf16[64,256]{1,0:T(8,128)(2,1)S(1)}, bf16[64,256]{1,0:T(8,128)(2,1)S(1)}, u32[]{:S(2)}, u32[]{:S(2)}) collective-permute-start(bf16[64,256]{1,0:T(8,128)(2,1)S(1)} %get-tuple-element.16), channel_id=1, source_target_pairs={{0,16},{4,20},{8,24},{12,28},{16,0},{20,4},{24,8},{28,12},{1,17},{... | collective-permute-start | bytes 98312 | tf_op jit(solution)/shard_map/ppermute | solution.py:21
  7.2 5.4 %collective-permute-start = (bf16[64,256]{1,0:T(8,128)(2,1)S(1)}, bf16[64,256]{1,0:T(8,128)(2,1)S(1)}, u32[]{:S(2)}, u32[]{:S(2)}) collective-permute-start(bf16[64,256]{1,0:T(8,128)(2,1)S(1)} %get-tuple-element.16), channel_id=1, source_target_pairs={{0,8},{4,12},{8,0},{12,4},{16,24},{20,28},{24,16},{28,20},{1,9},{5... | collective-permute-start | bytes 98312 | tf_op jit(solution)/shard_map/ppermute | solution.py:21
  9.0 10.2 %collective-permute-start.4 = (bf16[2,256,256]{2,1,0:T(8,128)(2,1)S(1)}, bf16[2,256,256]{2,1,0:T(8,128)(2,1)S(1)}, u32[]{:S(2)}, u32[]{:S(2)}) collective-permute-start(bf16[2,256,256]{2,1,0:T(8,128)(2,1)S(1)} %shard_map.47.refs_0_.refs_4_), channel_id=1, source_target_pairs={{0,3},{1,2},{2,1},{3,0},{4,7},{5,6},{6,5},{7,4},{8,11},{9,10},{10,... | collective-permute-start | bytes 786440 | tf_op jit(solution)/shard_map/ppermute | solution.py:21
  11.7 11.5 %collective-permute-start.6 = (bf16[2,256,256]{2,1,0:T(8,128)(2,1)S(1)}, bf16[2,256,256]{2,1,0:T(8,128)(2,1)S(1)}, u32[]{:S(2)}, u32[]{:S(2)}) collective-permute-start(bf16[2,256,256]{2,1,0:T(8,128)(2,1)S(1)} %shard_map.47.refs_0_.refs_4_), channel_id=1, source_target_pairs={{0,1},{1,0},{2,3},{3,2},{4,5},{5,4},{6,7},{7,6},{8,9},{9,8},{10,11... | collective-permute-start | bytes 786440 | tf_op jit(solution)/shard_map/ppermute | solution.py:21
  12.2 11.0 %collective-permute-start.5 = (bf16[2,256,256]{2,1,0:T(8,128)(2,1)S(1)}, bf16[2,256,256]{2,1,0:T(8,128)(2,1)S(1)}, u32[]{:S(2)}, u32[]{:S(2)}) collective-permute-start(bf16[2,256,256]{2,1,0:T(8,128)(2,1)S(1)} %shard_map.47.refs_0_.refs_4_), channel_id=1, source_target_pairs={{0,2},{1,3},{2,0},{3,1},{4,6},{5,7},{6,4},{7,5},{8,10},{9,11},{10,... | collective-permute-start | bytes 786440 | tf_op jit(solution)/shard_map/ppermute | solution.py:21
  12.6 10.6 %copy-start.1 = (bf16[3,1,256,256]{3,2,1,0:T(8,128)(2,1)S(1)}, bf16[3,1,256,256]{3,2,1,0:T(8,128)(2,1)}, u32[]{:S(2)}) copy-start(bf16[3,1,256,256]{3,2,1,0:T(8,128)(2,1)} %refs_5_.3) | copy-start | bytes 1179652
  12.6 10.6 %copy-start.3 = (bf16[3,1,64,256]{3,2,1,0:T(8,128)(2,1)S(1)}, bf16[3,1,64,256]{3,2,1,0:T(8,128)(2,1)}, u32[]{:S(2)}) copy-start(bf16[3,1,64,256]{3,2,1,0:T(8,128)(2,1)} %refs_4_.1) | copy-start | bytes 294916
  12.7 1.4 %collective-permute-start.3 = (bf16[4,64,256]{2,1,0:T(8,128)(2,1)S(1)}, bf16[4,64,256]{2,1,0:T(8,128)(2,1)S(1)}, u32[]{:S(2)}, u32[]{:S(2)}) collective-permute-start(bf16[4,64,256]{2,1,0:T(8,128)(2,1)S(1)} %pad_maximum_fusion.near), channel_id=1, source_target_pairs={{0,4},{4,0},{8,12},{12,8},{16,20},{20,16},{24,28},{28,24},{1,5},{5... | collective-permute-start | bytes 393224 | tf_op jit(solution)/shard_map/ppermute | solution.py:21
  19.5 8.6 %copy-start.5 = (bf16[2,1,2,256,256]{4,3,2,1,0:T(8,128)(2,1)S(1)}, bf16[2,1,2,256,256]{4,3,2,1,0:T(8,128)(2,1)}, u32[]{:S(2)}) copy-start(bf16[2,1,2,256,256]{4,3,2,1,0:T(8,128)(2,1)} %param.6) | copy-start | bytes 1572868
  23.7 7.7 %collective-permute-start.9 = (bf16[64,256]{1,0:T(8,128)(2,1)S(1)}, bf16[64,256]{1,0:T(8,128)(2,1)S(1)}, u32[]{:S(2)}, u32[]{:S(2)}) collective-permute-start(bf16[64,256]{1,0:T(8,128)(2,1)S(1)} %get-tuple-element.17), channel_id=1, source_target_pairs={{0,24},{4,28},{8,16},{12,20},{16,8},{20,12},{24,0},{28,4},{1,25},{... | collective-permute-start | bytes 98312 | tf_op jit(solution)/shard_map/ppermute | solution.py:21
  27.2 4.8 %collective-permute-start.8 = (bf16[64,256]{1,0:T(8,128)(2,1)S(1)}, bf16[64,256]{1,0:T(8,128)(2,1)S(1)}, u32[]{:S(2)}, u32[]{:S(2)}) collective-permute-start(bf16[64,256]{1,0:T(8,128)(2,1)S(1)} %get-tuple-element.17), channel_id=1, source_target_pairs={{0,16},{4,20},{8,24},{12,28},{16,0},{20,4},{24,8},{28,12},{1,17},{... | collective-permute-start | bytes 98312 | tf_op jit(solution)/shard_map/ppermute | solution.py:21
  27.2 4.8 %collective-permute-start.7 = (bf16[64,256]{1,0:T(8,128)(2,1)S(1)}, bf16[64,256]{1,0:T(8,128)(2,1)S(1)}, u32[]{:S(2)}, u32[]{:S(2)}) collective-permute-start(bf16[64,256]{1,0:T(8,128)(2,1)S(1)} %get-tuple-element.17), channel_id=1, source_target_pairs={{0,8},{4,12},{8,0},{12,4},{16,24},{20,28},{24,16},{28,20},{1,9},{5... | collective-permute-start | bytes 98312 | tf_op jit(solution)/shard_map/ppermute | solution.py:21
  28.4 10.2 %collective-permute-start.11 = (bf16[2,256,256]{2,1,0:T(8,128)(2,1)S(1)}, bf16[2,256,256]{2,1,0:T(8,128)(2,1)S(1)}, u32[]{:S(2)}, u32[]{:S(2)}) collective-permute-start(bf16[2,256,256]{2,1,0:T(8,128)(2,1)S(1)} %shard_map.50.refs_0_), channel_id=1, source_target_pairs={{0,3},{1,2},{2,1},{3,0},{4,7},{5,6},{6,5},{7,4},{8,11},{9,10},{10,... | collective-permute-start | bytes 786440 | tf_op jit(solution)/shard_map/ppermute | solution.py:21
  30.8 11.5 %collective-permute-start.13 = (bf16[2,256,256]{2,1,0:T(8,128)(2,1)S(1)}, bf16[2,256,256]{2,1,0:T(8,128)(2,1)S(1)}, u32[]{:S(2)}, u32[]{:S(2)}) collective-permute-start(bf16[2,256,256]{2,1,0:T(8,128)(2,1)S(1)} %shard_map.50.refs_0_), channel_id=1, source_target_pairs={{0,2},{1,3},{2,0},{3,1},{4,6},{5,7},{6,4},{7,5},{8,10},{9,11},{10,... | collective-permute-start | bytes 786440 | tf_op jit(solution)/shard_map/ppermute | solution.py:21
  31.4 10.9 %collective-permute-start.12 = (bf16[2,256,256]{2,1,0:T(8,128)(2,1)S(1)}, bf16[2,256,256]{2,1,0:T(8,128)(2,1)S(1)}, u32[]{:S(2)}, u32[]{:S(2)}) collective-permute-start(bf16[2,256,256]{2,1,0:T(8,128)(2,1)S(1)} %shard_map.50.refs_0_), channel_id=1, source_target_pairs={{0,1},{1,0},{2,3},{3,2},{4,5},{5,4},{6,7},{7,6},{8,9},{9,8},{10,11... | collective-permute-start | bytes 786440 | tf_op jit(solution)/shard_map/ppermute | solution.py:21
  32.1 6.5 %collective-permute-start.10 = (bf16[4,64,256]{2,1,0:T(8,128)(2,1)S(1)}, bf16[4,64,256]{2,1,0:T(8,128)(2,1)S(1)}, u32[]{:S(2)}, u32[]{:S(2)}) collective-permute-start(bf16[4,64,256]{2,1,0:T(8,128)(2,1)S(1)} %pad_maximum_fusion.1.near), channel_id=1, source_target_pairs={{0,4},{4,0},{8,12},{12,8},{16,20},{20,16},{24,28},{28,24},{1,5},{5... | collective-permute-start | bytes 393224 | tf_op jit(solution)/shard_map/ppermute | solution.py:21
  43.2 1.4 %collective-permute-start.14 = (bf16[4,64,256]{2,1,0:T(8,128)(2,1)S(1)}, bf16[4,64,256]{2,1,0:T(8,128)(2,1)S(1)}, u32[]{:S(2)}, u32[]{:S(2)}) collective-permute-start(bf16[4,64,256]{2,1,0:T(8,128)(2,1)S(1)} %get-tuple-element.20), channel_id=1, source_target_pairs={{0,4},{4,0},{8,12},{12,8},{16,20},{20,16},{24,28},{28,24},{1,5},{5... | collective-permute-start | bytes 393224 | tf_op jit(solution)/shard_map/ppermute | solution.py:21
  44.7 5.8 %collective-permute-start.17 = (bf16[64,256]{1,0:T(8,128)(2,1)S(1)}, bf16[64,256]{1,0:T(8,128)(2,1)S(1)}, u32[]{:S(2)}, u32[]{:S(2)}) collective-permute-start(bf16[64,256]{1,0:T(8,128)(2,1)S(1)} %get-tuple-element.34), channel_id=1, source_target_pairs={{0,24},{4,28},{8,16},{12,20},{16,8},{20,12},{24,0},{28,4},{1,25},{... | collective-permute-start | bytes 98312 | tf_op jit(solution)/shard_map/ppermute | solution.py:21
  48.2 4.8 %collective-permute-start.16 = (bf16[64,256]{1,0:T(8,128)(2,1)S(1)}, bf16[64,256]{1,0:T(8,128)(2,1)S(1)}, u32[]{:S(2)}, u32[]{:S(2)}) collective-permute-start(bf16[64,256]{1,0:T(8,128)(2,1)S(1)} %get-tuple-element.35), channel_id=1, source_target_pairs={{0,16},{4,20},{8,24},{12,28},{16,0},{20,4},{24,8},{28,12},{1,17},{... | collective-permute-start | bytes 98312 | tf_op jit(solution)/shard_map/ppermute | solution.py:21
  48.2 4.8 %collective-permute-start.15 = (bf16[64,256]{1,0:T(8,128)(2,1)S(1)}, bf16[64,256]{1,0:T(8,128)(2,1)S(1)}, u32[]{:S(2)}, u32[]{:S(2)}) collective-permute-start(bf16[64,256]{1,0:T(8,128)(2,1)S(1)} %get-tuple-element.36), channel_id=1, source_target_pairs={{0,8},{4,12},{8,0},{12,4},{16,24},{20,28},{24,16},{28,20},{1,9},{5... | collective-permute-start | bytes 98312 | tf_op jit(solution)/shard_map/ppermute | solution.py:21
  53.4 1.4 %collective-permute-start.18 = (bf16[4,64,256]{2,1,0:T(8,128)(2,1)S(1)}, bf16[4,64,256]{2,1,0:T(8,128)(2,1)S(1)}, u32[]{:S(2)}, u32[]{:S(2)}) collective-permute-start(bf16[4,64,256]{2,1,0:T(8,128)(2,1)S(1)} %get-tuple-element.23), channel_id=1, source_target_pairs={{0,4},{4,0},{8,12},{12,8},{16,20},{20,16},{24,28},{28,24},{1,5},{5... | collective-permute-start | bytes 393224 | tf_op jit(solution)/shard_map/ppermute | solution.py:21
  54.8 6.1 %collective-permute-start.21 = (bf16[64,256]{1,0:T(8,128)(2,1)S(1)}, bf16[64,256]{1,0:T(8,128)(2,1)S(1)}, u32[]{:S(2)}, u32[]{:S(2)}) collective-permute-start(bf16[64,256]{1,0:T(8,128)(2,1)S(1)} %get-tuple-element.31), channel_id=1, source_target_pairs={{0,24},{4,28},{8,16},{12,20},{16,8},{20,12},{24,0},{28,4},{1,25},{... | collective-permute-start | bytes 98312 | tf_op jit(solution)/shard_map/ppermute | solution.py:21
  56.4 4.9 %collective-permute-start.20 = (bf16[64,256]{1,0:T(8,128)(2,1)S(1)}, bf16[64,256]{1,0:T(8,128)(2,1)S(1)}, u32[]{:S(2)}, u32[]{:S(2)}) collective-permute-start(bf16[64,256]{1,0:T(8,128)(2,1)S(1)} %get-tuple-element.32), channel_id=1, source_target_pairs={{0,16},{4,20},{8,24},{12,28},{16,0},{20,4},{24,8},{28,12},{1,17},{... | collective-permute-start | bytes 98312 | tf_op jit(solution)/shard_map/ppermute | solution.py:21
  57.0 4.6 %collective-permute-start.19 = (bf16[64,256]{1,0:T(8,128)(2,1)S(1)}, bf16[64,256]{1,0:T(8,128)(2,1)S(1)}, u32[]{:S(2)}, u32[]{:S(2)}) collective-permute-start(bf16[64,256]{1,0:T(8,128)(2,1)S(1)} %get-tuple-element.33), channel_id=1, source_target_pairs={{0,8},{4,12},{8,0},{12,4},{16,24},{20,28},{24,16},{28,20},{1,9},{5... | collective-permute-start | bytes 98312 | tf_op jit(solution)/shard_map/ppermute | solution.py:21
